TPU v7x, 128 devices: a whole 4x4x4 slice. The times are simulated.
128 devices in a mesh: dp: 8 (over z, y_lo), expert: 16 (over y_hi, x, core).
Axes of the slice: x: 4, y: 4 (y_hi: 2, y_lo: 2; y = y_hi * 2 + y_lo), z: 4, core: 2. Of those that a mesh axis runs over, the one named last changes fastest.
Arguments:
- tokens: bfloat16 [16384, 2048], P(('dp', 'expert')), may hold values from -120 to 120
- norm_gain: float32 [2048], replicated, may hold values from 0.1 to 1.9
- expert_ids: int32 [16384, 6], P(('dp', 'expert')), may hold values from 0 to 63, all different within a row; in each aligned block of 128 rows (0 to 127, 128 to 255, ...) at most 14 rows name the same one
- gate_weights: float32 [16384, 6], P(('dp', 'expert')), may hold values from 0.05 to 1
- gate_proj: bfloat16 [128, 2048, 704], P(('dp', 'expert')), may hold values from -0.125 to 0.125
- up_proj: bfloat16 [128, 2048, 704], P(('dp', 'expert')), may hold values from -0.125 to 0.125
- down_proj: bfloat16 [128, 704, 2048], P(('dp', 'expert')), may hold values from -0.15625 to 0.15625
- student_one: bfloat16 [2048, 4096], P(None, 'expert'), may hold values from -0.125 to 0.125
- student_two: bfloat16 [2048, 8192], P(None, 'expert'), may hold values from -0.125 to 0.125
- cot_one: bfloat16 [16384, 4096], P('dp', 'expert'), may hold values from -6 to 6
- cot_two: bfloat16 [16384, 8192], P('dp', 'expert'), may hold values from -6 to 6
Outputs:
- layer_out: bfloat16 [16384, 2048], P(('dp', 'expert'))
- feat_one: bfloat16 [16384, 4096], P('dp', 'expert')
- feat_two: bfloat16 [16384, 8192], P('dp', 'expert')
- grad_one: float32 [2048, 4096], P('dp', 'expert')
- grad_two: float32 [2048, 8192], P('dp', 'expert')
Inputs may be any that keep to these rules, and one draw needn't show every extreme that they name: `expert_ids`: in each aligned block of 128 rows (the rows of one device) no expert is named by more than 14 entries; in every draw some expert is named by exactly 14 entries of some block.
All inputs are finite; a program needn't handle non-finite values.
Results may differ from a plain program's by a relative error of at most 0.0082.
Values may be sent and summed in bfloat16 or wider, within the bound.
No kernel may reach another device: no remote copies, remote signals or barrier semaphores. Data moves between devices by JAX's collectives and lax.ppermute only.
A program may use at most 128 MiB of HBM per device.

v0:
```python
import math

import jax
import jax.numpy as jnp
from jax import lax
from jax.sharding import PartitionSpec as P


def local(
    tokens,
    norm_gain,
    expert_ids,
    gate_weights,
    gate_proj,
    up_proj,
    down_proj,
    student_one,
    student_two,
    cot_one,
    cot_two,
):
    tok_dev, model_width = tokens.shape
    top_count = expert_ids.shape[1]
    halves = lax.axis_size("dp") * lax.axis_size("expert")
    experts = halves // 2
    capacity = 2 * ((tok_dev * top_count * 7 + 12 * experts - 1) // (12 * experts))
    widened = tokens.astype(jnp.float32)
    mean_sq = jnp.mean(widened * widened, axis=-1, keepdims=True)
    normed = (widened * lax.rsqrt(mean_sq + 1e-06) * norm_gain).astype(jnp.bfloat16)
    flat_ids = expert_ids.reshape(-1)
    one_hot = (flat_ids[:, None] == jnp.arange(experts, dtype=jnp.int32)[None, :]).astype(jnp.int32)
    earlier = jnp.cumsum(one_hot, axis=0) - one_hot
    slots = jnp.sum(earlier * one_hot, axis=-1)
    positions = flat_ids * capacity + slots
    rows_rep = jnp.repeat(normed, top_count, axis=0)
    dispatch = (
        jnp.zeros((experts * capacity, model_width), jnp.bfloat16).at[positions].set(rows_rep)
    )
    doubled = jnp.repeat(dispatch.reshape(experts, capacity, model_width), 2, axis=0)
    received = lax.all_to_all(doubled, ("dp", "expert"), split_axis=0, concat_axis=0, tiled=True)
    count = received.shape[1]
    flat_rows = received.reshape(halves * count, model_width)
    gate_val = jnp.dot(flat_rows, gate_proj[0], preferred_element_type=jnp.float32)
    up_val = jnp.dot(flat_rows, up_proj[0], preferred_element_type=jnp.float32)
    hidden = (jax.nn.silu(gate_val) * up_val).astype(jnp.bfloat16)
    partial_out = jnp.dot(hidden, down_proj[0], preferred_element_type=jnp.float32).astype(
        jnp.bfloat16
    )
    outputs = lax.all_to_all(
        partial_out.reshape(halves, count, model_width),
        ("dp", "expert"),
        split_axis=0,
        concat_axis=0,
        tiled=True,
    )
    halves_out = outputs.reshape(experts, 2, capacity, model_width).astype(jnp.float32)
    pair_sum = (halves_out[:, 0] + halves_out[:, 1]).reshape(experts * capacity, model_width)
    expert_out = lax.optimization_barrier(pair_sum.astype(jnp.bfloat16))
    picked = expert_out.astype(jnp.float32)[positions] * gate_weights.reshape(-1)[:, None]
    layer_out = jnp.sum(picked.reshape(tok_dev, top_count, model_width), axis=1).astype(
        jnp.bfloat16
    )
    gathered = lax.all_gather(layer_out, "expert", axis=0, tiled=True)
    feat_one = jnp.dot(gathered, student_one, preferred_element_type=jnp.float32).astype(
        jnp.bfloat16
    )
    feat_two = jnp.dot(gathered, student_two, preferred_element_type=jnp.float32).astype(
        jnp.bfloat16
    )
    cotangents = jnp.concatenate([cot_one, cot_two], axis=1)
    grad_scale = 1.0 / math.sqrt(gathered.shape[0] * lax.axis_size("dp"))
    grads = (
        lax.psum_scatter(
            lax.dot_general(
                gathered, cotangents, (((0,), (0,)), ((), ())), preferred_element_type=jnp.float32
            ),
            "dp",
            scatter_dimension=0,
            tiled=True,
        )
        * grad_scale
    )
    split_at = student_one.shape[1]
    return (layer_out, feat_one, feat_two, grads[:, :split_at], grads[:, split_at:])


def solution(mesh):
    return jax.shard_map(
        local,
        mesh=mesh,
        in_specs=(
            P(("dp", "expert"), None),
            P(),
            P(("dp", "expert"), None),
            P(("dp", "expert"), None),
            P(("dp", "expert"), None, None),
            P(("dp", "expert"), None, None),
            P(("dp", "expert"), None, None),
            P(None, "expert"),
            P(None, "expert"),
            P("dp", "expert"),
            P("dp", "expert"),
        ),
        out_specs=(
            P(("dp", "expert"), None),
            P("dp", "expert"),
            P("dp", "expert"),
            P("dp", "expert"),
            P("dp", "expert"),
        ),
        check_vma=False,
    )
```

profile of v0, /device:TPU:1, one launch (start us, length us, event | category | flops | bytes accessed | tf_op | source)
XLA Modules:
  0.0 590.1 jit_solution(1634338609135616471)
XLA Ops:
  14.0 2.6 broadcast_in_dim.7
  16.6 6.3 %reshape.115 = bf16[768,2048]{1,0:T(8,128)(2,1)} reshape(bf16[128,6,2048]{2,1,0:T(8,128)(2,1)} %broadcast_in_dim.7) | data formatting | bytes 6291456 | tf_op jit(solution)/shard_map/reshape | solution.py:35
  23.1 10.1 %scatter_custom_fusion = bf16[896,2048]{1,0:T(8,128)(2,1)} fusion(s32[768]{0:T(1024)S(1)} %fusion.22, bf16[768,2048]{1,0:T(8,128)(2,1)} %reshape.115, bf16[]{:T(256)} %constant.9.clone.1), kind=kCustom, calls=%fused_computation.20 | custom fusion | bytes 3670528 | tf_op jit(solution)/shard_map/scatter | solution.py:37
  33.2 5.9 reshape.98
  39.1 6.8 %broadcast_in_dim.16 = bf16[64,2,14,2048]{3,2,1,0:T(8,128)(2,1)} broadcast(bf16[64,14,2048]{2,1,0:T(8,128)(2,1)} %reshape.98), dimensions={0,2,3} | broadcast | bytes 11010048 | tf_op jit(solution)/shard_map/broadcast_in_dim | solution.py:39
  45.8 109.2 %all_to_all.10 = bf16[128,14,2048]{2,1,0:T(8,128)(2,1)} all-to-all(bf16[128,14,2048]{2,1,0:T(8,128)(2,1)} %bitcast.53), channel_id=1, replica_groups=mesh['dp'=8,'expert'=16] {'dp','expert'}, dimensions={0} | all-to-all | bytes 14680064 | tf_op jit(solution)/shard_map/all_to_all | solution.py:40
  155.0 10.9 %reshape.100 = bf16[1792,2048]{1,0:T(8,128)(2,1)} reshape(bf16[128,14,2048]{2,1,0:T(8,128)(2,1)} %all_to_all.10) | data formatting | bytes 14680064 | tf_op jit(solution)/shard_map/reshape | solution.py:42
  165.8 10.6 %fusion.10 = f32[1792,704]{0,1:T(8,128)} fusion(bf16[1792,2048]{1,0:T(8,128)(2,1)} %reshape.100, bf16[1,2048,704]{1,2,0:T(8,128)(2,1)} %param.15), kind=kOutput, calls=%fused_computation.16 | convolution fusion | flops 5167382528 | bytes 15269888 | tf_op jit(solution)/shard_map/dot_general | solution.py:43
  176.5 17.9 %convolution_convert_fusion = bf16[1792,2048]{1,0:T(8,128)(2,1)} fusion(bf16[1,704,2048]{2,1,0:T(8,128)(2,1)S(1)} %copy-done, f32[1792,704]{0,1:T(8,128)} %fusion.10, bf16[1792,2048]{1,0:T(8,128)(2,1)} %reshape.100, bf16[1,2048,704]{1,2,0:T(8,128)(2,1)} %param.16), kind=kOutput, calls=%fused_computation.7 | convolution fusion | flops 10346004480 | bytes 25493504 | tf_op jit(solution)/shard_map/dot_general | solution.py:46
  194.3 11.1 %reshape.101 = bf16[128,14,2048]{2,1,0:T(8,128)(2,1)} reshape(bf16[1792,2048]{1,0:T(8,128)(2,1)} %convolution_convert_fusion) | data formatting | bytes 14680064 | tf_op jit(solution)/shard_map/reshape | solution.py:50
  205.4 6.0 %all-to-all-start.1 = ((bf16[128,14,2048]{2,1,0:T(8,128)(2,1)}), bf16[128,14,2048]{2,1,0:T(8,128)(2,1)}, u32[]{:S(2)}, u32[]{:S(2)}) async-start(bf16[128,14,2048]{2,1,0:T(8,128)(2,1)} %reshape.101), calls=%async_computation.1 | async-start | bytes 16777216 | tf_op jit(solution)/shard_map/all_to_all | solution.py:49
  211.9 98.8 %all-to-all-done.1 = bf16[128,14,2048]{2,1,0:T(8,128)(2,1)} async-done(((bf16[128,14,2048]{2,1,0:T(8,128)(2,1)}), bf16[128,14,2048]{2,1,0:T(8,128)(2,1)}, u32[]{:S(2)}, u32[]{:S(2)}) %all-to-all-start.1) | async-done | bytes 7340064 | tf_op jit(solution)/shard_map/all_to_all | solution.py:49
  310.6 11.2 %convert.1 = f32[64,2,14,2048]{3,2,1,0:T(8,128)} convert(bf16[64,2,14,2048]{3,2,1,0:T(8,128)(2,1)} %bitcast.6) | non-fusion elementwise | flops 3670016 | bytes 22020096 | tf_op jit(solution)/shard_map/convert_element_type | solution.py:56
  321.9 8.5 %fusion.1 = bf16[64,1,14,2048]{3,2,0,1:T(8,128)(2,1)} fusion(f32[64,2,14,2048]{3,2,1,0:T(8,128)} %convert.1), kind=kLoop, calls=%fused_computation.4 | loop fusion | flops 3670016 | bytes 18350080 | tf_op jit(solution)/shard_map/convert_element_type | solution.py:58
  330.4 6.0 %convert_element_type.52 = bf16[896,2048]{1,0:T(8,128)(2,1)} reshape(bf16[64,1,14,2048]{3,2,0,1:T(8,128)(2,1)} %fusion.1) | data formatting | bytes 7340032 | tf_op jit(solution)/shard_map/convert_element_type | solution.py:58
  336.4 5.9 %convert_element_type.53 = f32[896,2048]{1,0:T(8,128)} convert(bf16[896,2048]{1,0:T(8,128)(2,1)} %convert_element_type.52) | non-fusion elementwise | flops 1835008 | bytes 11010048 | tf_op jit(solution)/shard_map/convert_element_type | solution.py:59
  342.4 10.3 %gather_fusion = f32[768,2048]{1,0:T(8,128)} fusion(f32[896,2048]{1,0:T(8,128)} %convert_element_type.53, s32[1024]{0:T(1024)S(1)} %pad_clamp_fusion), kind=kCustom, calls=%fused_computation | custom fusion | bytes 12585984 | tf_op jit(solution)/shard_map/gather | solution.py:59
  352.7 7.8 %gather.6 = f32[128,6,2048]{2,1,0:T(8,128)} reshape(f32[768,2048]{1,0:T(8,128)} %gather_fusion) | data formatting | bytes 12582912 | tf_op jit(solution)/shard_map/gather | solution.py:59
  360.5 7.5 %multiply_reduce_fusion = bf16[128,2048]{1,0:T(8,128)(2,1)} fusion(f32[128,6,2048]{2,1,0:T(8,128)} %gather.6, f32[128,6]{1,0:T(8,128)S(1)} %copy.25), kind=kLoop, calls=%fused_computation.6 | loop fusion | flops 2883584 | bytes 6818816 | tf_op jit(solution)/shard_map/reduce_sum | solution.py:60
  368.4 73.3 %all-gather.2.cloned.1.call-done = bf16[2048,2048]{1,0:T(8,128)(2,1)} async-done(((bf16[128,2048]{1,0:T(8,128)(2,1)}), bf16[2048,2048]{1,0:T(8,128)(2,1)}) %all-gather.2.cloned.1.call-update) | async-done | bytes 8388624 | tf_op jit(solution)/shard_map/all_gather | solution.py:63
  441.7 11.3 %fusion.2 = f32[2048,768]{1,0:T(8,128)} fusion(bf16[2048,2048]{1,0:T(8,128)(2,1)} %all-gather.2.cloned.1.call-done, bf16[2048,512]{1,0:T(8,128)(2,1)S(1)} %copy-done.3, bf16[2048,256]{1,0:T(8,128)(2,1)} %param.20), kind=kOutput, calls=%fused_computation.9 | convolution fusion | flops 6448742400 | bytes 17825792 | tf_op jit(solution)/shard_map/dot_general | solution.py:74
  454.2 6.8 %convolution_convert_fusion.2 = bf16[2048,256]{1,0:T(8,128)(2,1)} fusion(bf16[2048,2048]{1,0:T(8,128)(2,1)} %all-gather.2.cloned.1.call-done, bf16[2048,256]{1,0:T(8,128)(2,1)S(1)} %copy-done.5), kind=kOutput, calls=%fused_computation.18 | convolution fusion | flops 2148007936 | bytes 10485760 | tf_op jit(solution)/shard_map/dot_general | solution.py:64
  461.0 9.2 %convolution_convert_fusion.1 = bf16[2048,512]{1,0:T(8,128)(2,1)} fusion(bf16[2048,2048]{1,0:T(8,128)(2,1)} %all-gather.2.cloned.1.call-done, bf16[2048,512]{1,0:T(8,128)(2,1)S(1)} %copy-done.4), kind=kOutput, calls=%fused_computation.13 | convolution fusion | flops 4296015872 | bytes 12582912 | tf_op jit(solution)/shard_map/dot_general | solution.py:67
  470.2 110.3 %reduce-scatter.2.cloned.1.call-done = f32[256,768]{1,0:T(8,128)} async-done(((f32[2048,768]{1,0:T(8,128)}), f32[256,768]{1,0:T(8,128)}) %reduce-scatter.2.cloned.1.call-update) | async-done | bytes 786448 | tf_op jit(solution)/shard_map/reduce_scatter | solution.py:73
  (36 shorter events, 11.6 us)
Async XLA Ops:
  7.2 169.3 %copy-start = (bf16[1,704,2048]{2,1,0:T(8,128)(2,1)S(1)}, bf16[1,704,2048]{2,1,0:T(8,128)(2,1)}, u32[]{:S(2)}) copy-start(bf16[1,704,2048]{2,1,0:T(8,128)(2,1)} %param.17) | copy-start | bytes 8650756
  205.4 6.3 %copy-start.2 = (f32[128,6]{0,1:T(8,128)S(1)}, f32[128,6]{0,1:T(8,128)}, u32[]{:S(2)}) copy-start(f32[128,6]{0,1:T(8,128)} %param.14) | copy-start | bytes 9220
  205.4 105.2 %all-to-all-start.1 = ((bf16[128,14,2048]{2,1,0:T(8,128)(2,1)}), bf16[128,14,2048]{2,1,0:T(8,128)(2,1)}, u32[]{:S(2)}, u32[]{:S(2)}) async-start(bf16[128,14,2048]{2,1,0:T(8,128)(2,1)} %reshape.101), calls=%async_computation.1 | async-start | bytes 16777216 | tf_op jit(solution)/shard_map/all_to_all | solution.py:49
  211.5 230.2 %all-gather.2.cloned.1.call-start = ((), (), s32[]{:S(2)}) async-start(), calls=%async_computation.3 | async-start | bytes 8912896 | tf_op jit(solution)/shard_map/all_gather | solution.py:63
  360.5 81.1 %copy-start.3 = (bf16[2048,512]{1,0:T(8,128)(2,1)S(1)}, bf16[2048,512]{1,0:T(8,128)(2,1)}, u32[]{:S(2)}) copy-start(bf16[2048,512]{1,0:T(8,128)(2,1)} %param.21) | copy-start | bytes 6291460
  368.1 212.4 %reduce-scatter.2.cloned.1.call-start = ((), (), s32[]{:S(2)}) async-start(), calls=%async_computation.4 | async-start | bytes 7077888 | tf_op jit(solution)/shard_map/reduce_scatter | solution.py:73
  452.9 1.2 copy-start.5
  454.2 6.9 %copy-start.4 = (bf16[2048,512]{1,0:T(8,128)(2,1)S(1)}, bf16[2048,512]{1,0:T(8,128)(2,1)}, u32[]{:S(2)}) copy-start(bf16[2048,512]{1,0:T(8,128)(2,1)} %param.19) | copy-start | bytes 6291460
  461.0 122.2 %copy-start.1 = (bf16[1,704,2048]{2,1,0:T(8,128)(2,1)S(1)}, bf16[1,704,2048]{2,1,0:T(8,128)(2,1)}, u32[]{:S(2)}) copy-start(bf16[1,704,2048]{2,1,0:T(8,128)(2,1)} %param.17) | copy-start | bytes 8650756
Sparse Core Ops, SparseCore 0:
  368.2 73.4 all-gather.1
  453.1 127.3 reduce-scatter.1
where the time goes:
time: 592 us; the launch traced here: 590 us
  waiting for transfers between devices  282 us (48%)
  blocking collectives  109 us (18%)
  local copies, waits for them, and re-layouts  82.5 us (14%)
  matrix products  55.8 us (9%)
  other arithmetic  39.6 us (7%)
  between operations  14.1 us (2%)
  starting transfers between devices  6.59 us (1%)
    reduce_scatter x1, waiting for transfers between devices, local(): lax.psum_scatter(lax.dot_general(gathered, cotangents, (((0,), (0,)), (()...  110 us
    all_to_all x1, blocking collectives, local(): lax.all_to_all(doubled, ('dp', 'expert'), split_axis=0, concat_axis=0, ti...  109 us
    all_to_all x1, waiting for transfers between devices, local(): lax.all_to_all(partial_out.reshape(halves, count, model_width), ('dp', 'e...  98.8 us
    all_gather x1, waiting for transfers between devices, local(): gathered = lax.all_gather(layer_out, 'expert', axis=0, tiled=True)  73.3 us
    gather x2, local copies, waits for them, and re-layouts, local(): expert_out.astype(jnp.float32)[positions]  18.2 us
    dot_general x1, matrix products, local(): jnp.dot(hidden, down_proj[0], preferred_element_type=jnp.float32)  17.9 us
  transfers between devices with their start and end apart: 3, of which 3 were waited for; matrix products, arithmetic and copies ran while one was open for 3% of the time, Pallas kernels for 0%

commit v1 on v0

v1 whole, which is shorter than its diff:
```python
import functools
import math

import jax
import jax.numpy as jnp
from jax import lax
from jax.experimental import pallas as pl
from jax.experimental.pallas import tpu as pltpu
from jax.sharding import PartitionSpec as P

LANES = 128


def dispatch_body(ids_ref, tok_ref, gain_ref, out_ref, pos_ref, rows_ref, pos_smem, sem, *, experts, cap):
    top, toks = ids_ref.shape
    width = tok_ref.shape[1]
    sub = width // LANES
    expert_iota = lax.broadcasted_iota(jnp.int32, (experts, toks), 0)
    named = [(ids_ref[k : k + 1, :] == expert_iota).astype(jnp.float32) for k in range(top)]
    total = named[0]
    for k in range(1, top):
        total = total + named[k]
    row = lax.broadcasted_iota(jnp.int32, (toks, toks), 0)
    col = lax.broadcasted_iota(jnp.int32, (toks, toks), 1)
    before = (row < col).astype(jnp.bfloat16)
    earlier = jnp.dot(total.astype(jnp.bfloat16), before, preferred_element_type=jnp.float32)
    for k in range(top):
        slot = jnp.sum(earlier * named[k], axis=0, keepdims=True)
        pos_ref[k : k + 1, :] = ids_ref[k : k + 1, :] * cap + slot.astype(jnp.int32)
    copy = pltpu.make_async_copy(pos_ref, pos_smem, sem)
    copy.start()
    out_ref[...] = jnp.zeros_like(out_ref)
    wide = tok_ref[...].astype(jnp.float32)
    mean_sq = jnp.mean(wide * wide, axis=-1, keepdims=True)
    normed = wide * lax.rsqrt(mean_sq + 1e-06) * gain_ref[...]
    for j in range(sub):
        rows_ref[pl.ds(j, toks, stride=sub), :] = normed[:, j * LANES : (j + 1) * LANES]
    copy.wait()

    def place(t, carry):
        one = rows_ref[pl.ds(pl.multiple_of(t * sub, sub), sub), :].astype(jnp.bfloat16)
        for k in range(top):
            out_ref[pos_smem[k, t]] = one
        return carry

    lax.fori_loop(0, toks, place, 0, unroll=4)


def dispatch(ids, tokens, gain, experts, cap):
    top, toks = ids.shape
    width = tokens.shape[1]
    sub = width // LANES
    return pl.pallas_call(
        functools.partial(dispatch_body, experts=experts, cap=cap),
        name="dispatch",
        out_shape=(
            jax.ShapeDtypeStruct((experts * cap, sub, LANES), jnp.bfloat16),
            jax.ShapeDtypeStruct((top, toks), jnp.int32),
        ),
        scratch_shapes=[
            pltpu.VMEM((toks * sub, LANES), jnp.float32),
            pltpu.SMEM((top, toks), jnp.int32),
            pltpu.SemaphoreType.DMA,
        ],
    )(ids, tokens, gain)


def combine_body(pos_ref, gates_ref, rows_ref, out_ref, acc_ref):
    top, toks = pos_ref.shape
    sub = rows_ref.shape[1]

    def gather(t, carry):
        acc = rows_ref[pos_ref[0, t]].astype(jnp.float32) * gates_ref[0, t]
        for k in range(1, top):
            acc = acc + rows_ref[pos_ref[k, t]].astype(jnp.float32) * gates_ref[k, t]
        acc_ref[pl.ds(pl.multiple_of(t * sub, sub), sub), :] = acc
        return carry

    lax.fori_loop(0, toks, gather, 0, unroll=4)
    for j in range(sub):
        out_ref[:, j * LANES : (j + 1) * LANES] = acc_ref[pl.ds(j, toks, stride=sub), :].astype(jnp.bfloat16)


def combine(pos, gates, rows):
    top, toks = pos.shape
    sub = rows.shape[1]
    return pl.pallas_call(
        combine_body,
        name="combine",
        grid_spec=pltpu.PrefetchScalarGridSpec(
            num_scalar_prefetch=2,
            grid=(1,),
            in_specs=[pl.BlockSpec(rows.shape, lambda i, p, g: (0, 0, 0), pipeline_mode=pl.Buffered(1))],
            out_specs=pl.BlockSpec((toks, sub * LANES), lambda i, p, g: (0, 0), pipeline_mode=pl.Buffered(1)),
            scratch_shapes=[pltpu.VMEM((toks * sub, LANES), jnp.float32)],
        ),
        out_shape=jax.ShapeDtypeStruct((toks, sub * LANES), jnp.bfloat16),
    )(pos, gates, rows)


def half_expert(rows, gate, up, down):
    gate_val = lax.dot_general(rows, gate, (((1,), (0,)), ((), ())), preferred_element_type=jnp.float32)
    up_val = lax.dot_general(rows, up, (((1,), (0,)), ((), ())), preferred_element_type=jnp.float32)
    hidden = (jax.nn.silu(gate_val) * up_val).astype(jnp.bfloat16)
    return jnp.dot(hidden, down, preferred_element_type=jnp.float32).astype(jnp.bfloat16)


def local(
    tokens,
    norm_gain,
    expert_ids,
    gate_weights,
    gate_proj,
    up_proj,
    down_proj,
    student_one,
    student_two,
    cot_one,
    cot_two,
):
    tok_dev, model_width = tokens.shape
    top_count = expert_ids.shape[1]
    devices = lax.axis_size("dp") * lax.axis_size("expert")
    experts = devices // 2
    capacity = 2 * ((tok_dev * top_count * 7 + 12 * experts - 1) // (12 * experts))
    sub = model_width // LANES
    partner = [(i, i ^ 1) for i in range(lax.axis_size("expert"))]
    other_gate = lax.ppermute(jnp.swapaxes(gate_proj[0], 0, 1), "expert", partner)
    other_up = lax.ppermute(jnp.swapaxes(up_proj[0], 0, 1), "expert", partner)
    other_down = lax.ppermute(down_proj[0], "expert", partner)

    placed, positions = dispatch(expert_ids.T, tokens, norm_gain.reshape(1, -1), experts, capacity)
    received = lax.all_to_all(
        placed.reshape(devices, capacity // 2, sub, LANES),
        ("dp", "expert"),
        split_axis=0,
        concat_axis=0,
        tiled=True,
    )
    flat_rows = received.reshape(devices * capacity // 2, model_width)
    first = half_expert(flat_rows, gate_proj[0], up_proj[0], down_proj[0])
    second = half_expert(flat_rows, other_gate.T, other_up.T, other_down)
    expert_out = (first.astype(jnp.float32) + second.astype(jnp.float32)).astype(jnp.bfloat16)
    returned = lax.all_to_all(
        expert_out.reshape(devices, capacity // 2, sub, LANES),
        ("dp", "expert"),
        split_axis=0,
        concat_axis=0,
        tiled=True,
    )
    layer_out = combine(positions, gate_weights.T, returned.reshape(experts * capacity, sub, LANES))
    gathered = lax.all_gather(layer_out, "expert", axis=0, tiled=True)
    feat_one = jnp.dot(gathered, student_one, preferred_element_type=jnp.float32).astype(jnp.bfloat16)
    feat_two = jnp.dot(gathered, student_two, preferred_element_type=jnp.float32).astype(jnp.bfloat16)
    cotangents = jnp.concatenate([cot_one, cot_two], axis=1)
    grad_scale = 1.0 / math.sqrt(gathered.shape[0] * lax.axis_size("dp"))
    terms = lax.dot_general(
        gathered, cotangents, (((0,), (0,)), ((), ())), preferred_element_type=jnp.float32
    )
    batches = lax.axis_size("dp")
    pieces = (terms * grad_scale).astype(jnp.bfloat16).reshape(batches, model_width // batches, -1)
    pieces = lax.all_to_all(pieces, "dp", split_axis=0, concat_axis=0, tiled=True)
    grads = jnp.sum(pieces.astype(jnp.float32), axis=0)
    split_at = student_one.shape[1]
    return (layer_out, feat_one, feat_two, grads[:, :split_at], grads[:, split_at:])


def solution(mesh):
    return jax.shard_map(
        local,
        mesh=mesh,
        in_specs=(
            P(("dp", "expert"), None),
            P(),
            P(("dp", "expert"), None),
            P(("dp", "expert"), None),
            P(("dp", "expert"), None, None),
            P(("dp", "expert"), None, None),
            P(("dp", "expert"), None, None),
            P(None, "expert"),
            P(None, "expert"),
            P("dp", "expert"),
            P("dp", "expert"),
        ),
        out_specs=(
            P(("dp", "expert"), None),
            P("dp", "expert"),
            P("dp", "expert"),
            P("dp", "expert"),
            P("dp", "expert"),
        ),
        check_vma=False,
    )
```

time: 592 us -> 308 us (0.52)
  waiting for transfers between devices: 282 us -> 136 us
  local copies, waits for them, and re-layouts: 82.5 us -> 4.83 us
  blocking collectives: 109 us -> 51.9 us
  other arithmetic: 39.6 us -> 2.4 us
  matrix products: 55.8 us -> 68.3 us
  starting transfers between devices: 6.59 us -> 18.5 us
  Pallas kernels: 0 us -> 11.5 us
    reduce_scatter x1 -> x0, waiting for transfers between devices: 110 us -> none  [local(): lax.psum_scatter(lax.dot_general(gathered, cotangents, (((0,), (0,)), (()...]
    all_to_all x1, blocking collectives: 109 us -> 51.9 us  [local(): lax.all_to_all(expert_out.reshape(devices, capacity // 2, sub, LANES), ('...]
    reshape x4 -> x0, local copies, waits for them, and re-layouts: 34.2 us -> none  [the longest x1 11.1 us: local(): partial_out.reshape(halves, count, model_width)]
    all_to_all x1 -> x2, waiting for transfers between devices: 98.8 us -> 66.9 us  [the longest x1 45 us: local(): lax.all_to_all(placed.reshape(devices, capacity // 2, sub, LANES), ('dp',...]
    convert_element_type x5 -> x0, other arithmetic: 27 us -> none  [the longest x1 11.2 us: local(): outputs.reshape(experts, 2, capacity, model_width).astype(jnp.float32)]
    gather x2 -> x0, local copies, waits for them, and re-layouts: 18.2 us -> none  [local(): expert_out.astype(jnp.float32)[positions]]
    dot_general x2 -> x4, matrix products: 28.5 us -> 41.4 us  [the longest x2 26.3 us: half_expert(): jnp.dot(hidden, down, preferred_element_type=jnp.float32)]
    pallas_call x0 -> x2, Pallas kernels: none -> 11.5 us  [the longest x1 5.85 us: dispatch(): pl.pallas_call(functools.partial(dispatch_body, experts=experts, cap=cap)...]
  transfers between devices with their start and end apart: 3 -> 6, of which waited for: 3 -> 3; matrix products, arithmetic and copies ran while one was open for 3% -> 14% of each run, Pallas kernels for 0% -> 0%
where the time goes in v1:
time: 308 us
  waiting for transfers between devices  136 us (44%)
  matrix products  68.3 us (22%)
  blocking collectives  51.9 us (17%)
  starting transfers between devices  18.5 us (6%)
  between operations  14.1 us (5%)
  Pallas kernels  11.5 us (4%)
  local copies, waits for them, and re-layouts  4.83 us (2%)
    all_gather x1, waiting for transfers between devices, local(): gathered = lax.all_gather(layer_out, 'expert', axis=0, tiled=True)  69.2 us
    all_to_all x1, blocking collectives, local(): lax.all_to_all(expert_out.reshape(devices, capacity // 2, sub, LANES), ('...  51.9 us
    all_to_all x1, waiting for transfers between devices, local(): lax.all_to_all(placed.reshape(devices, capacity // 2, sub, LANES), ('dp',...  45 us
    dot_general x2, matrix products, half_expert(): jnp.dot(hidden, down, preferred_element_type=jnp.float32)  26.3 us
    all_to_all x1, waiting for transfers between devices, local(): lax.all_to_all(pieces, 'dp', split_axis=0, concat_axis=0, tiled=True)  21.9 us
    all_to_all x1, starting transfers between devices, local(): lax.all_to_all(placed.reshape(devices, capacity // 2, sub, LANES), ('dp',...  11.9 us
    dot_general x1, matrix products, local(): lax.dot_general(gathered, cotangents, (((0,), (0,)), ((), ())), preferred...  11.1 us
    dot_general x1, matrix products, local(): jnp.dot(gathered, student_two, preferred_element_type=jnp.float32)  9.07 us
  transfers between devices with their start and end apart: 6, of which 3 were waited for; matrix products, arithmetic and copies ran while one was open for 14% of the time, Pallas kernels for 0%

profile of v1, /device:TPU:1, one launch (start us, length us, event | category | flops | bytes accessed | tf_op | source)
XLA Modules:
  0.0 307.6 jit_solution(1808737650828924984)
XLA Ops:
  7.2 5.8 %dispatch.1 = (bf16[896,16,128]{2,1,0:T(8,128)(2,1)}, s32[6,128]{1,0:T(8,128)}) custom-call(s32[6,128]{1,0:T(8,128)} %bitcast.59, bf16[128,2048]{1,0:T(8,128)(2,1)} %tok_ref.1, f32[1,2048]{1,0:T(1,128)} %bitcast.58), custom_call_target="tpu_custom_call" | custom-call | tf_op jit(solution)/shard_map/dispatch/pallas_call | solution.py:53
  13.0 11.9 %all-to-all-start = ((bf16[128,7,16,128]{3,2,1,0:T(8,128)(2,1)}), bf16[128,7,16,128]{3,2,1,0:T(8,128)(2,1)}, u32[]{:S(2)}, u32[]{:S(2)}) async-start(bf16[128,7,16,128]{3,2,1,0:T(8,128)(2,1)} %bitcast.56), calls=%async_computation | async-start | bytes 7340032 | tf_op jit(solution)/shard_map/all_to_all | solution.py:133
  24.9 0.0 all-gather.2.cloned.1.call-start
  25.0 1.2 collective-permute-start
  26.2 0.1 collective-permute-start.2
  26.3 0.4 collective-permute-start.1
  26.7 45.0 %all-to-all-done = bf16[128,7,16,128]{3,2,1,0:T(8,128)(2,1)} async-done(((bf16[128,7,16,128]{3,2,1,0:T(8,128)(2,1)}), bf16[128,7,16,128]{3,2,1,0:T(8,128)(2,1)}, u32[]{:S(2)}, u32[]{:S(2)}) %all-to-all-start) | async-done | bytes 3670048 | tf_op jit(solution)/shard_map/all_to_all | solution.py:133
  71.7 7.6 %fusion.5 = f32[896,704]{0,1:T(8,128)} fusion(bf16[1,2048,704]{1,2,0:T(8,128)(2,1)} %param.16, bf16[112,8,16,128]{3,2,1,0:T(8,128)(2,1)} %bitcast.14), kind=kOutput, calls=%fused_computation.8 | convolution fusion | flops 2583691264 | bytes 9076736 | tf_op jit(solution)/shard_map/dot_general | solution.py:103
  79.2 7.6 %fusion.3 = f32[896,704]{0,1:T(8,128)} fusion(bf16[704,2048]{1,0:T(8,128)(2,1)} %collective-permute-done, bf16[112,8,16,128]{3,2,1,0:T(8,128)(2,1)} %bitcast.14), kind=kOutput, calls=%fused_computation.6 | convolution fusion | flops 2583691264 | bytes 9076736 | tf_op jit(solution)/shard_map/dot_general | solution.py:102
  86.8 12.5 %fusion.26 = bf16[896,2048]{1,0:T(8,128)(2,1)} fusion(f32[896,704]{0,1:T(8,128)} %fusion.5, bf16[1,2048,704]{1,2,0:T(8,128)(2,1)} %param.15, bf16[112,8,16,128]{3,2,1,0:T(8,128)(2,1)} %bitcast.14, bf16[1,704,2048]{2,1,0:T(8,128)(2,1)} %param.17), kind=kOutput, calls=%fused_computation.25 | convolution fusion | flops 5171167232 | bytes 15630336 | tf_op jit(solution)/shard_map/dot_general | solution.py:105
  99.2 13.8 %fusion = bf16[112,8,16,128]{3,1,2,0:T(8,128)(2,1)} fusion(bf16[896,2048]{1,0:T(8,128)(2,1)} %fusion.26, bf16[704,2048]{1,0:T(8,128)(2,1)} %collective-permute-done.2, f32[896,704]{0,1:T(8,128)} %fusion.3, bf16[704,2048]{1,0:T(8,128)(2,1)} %collective-permute-done.1, bf16[112,8,16,128]{3,2,1,0:T(8,128)(2,1)} %bitcast.14), kind=kOutput, calls=%fused_computation.3 | convolution fusion | flops 5180342272 | bytes 19300352 | tf_op jit(solution)/shard_map/dot_general | solution.py:105
  113.1 3.2 %copy.17 = bf16[112,8,16,128]{3,2,1,0:T(8,128)(2,1)S(1)} copy(bf16[112,8,16,128]{3,1,2,0:T(8,128)(2,1)} %fusion) | data formatting | bytes 7340032
  116.3 51.9 %all_to_all.15 = bf16[128,7,16,128]{3,2,1,0:T(8,128)(2,1)} all-to-all(bf16[128,7,16,128]{3,2,1,0:T(8,128)(2,1)S(1)} %bitcast.54), channel_id=1, replica_groups=mesh['dp'=8,'expert'=16] {'dp','expert'}, dimensions={0} | all-to-all | bytes 7340032 | tf_op jit(solution)/shard_map/all_to_all | solution.py:144
  168.2 5.6 %combine.1 = bf16[128,2048]{1,0:T(8,128)(2,1)} custom-call(s32[6,128]{1,0:T(8,128)} %get-tuple-element.7.pos_ref, f32[6,128]{1,0:T(8,128)} %bitcast.60, bf16[896,16,128]{2,1,0:T(8,128)(2,1)} %bitcast.55), custom_call_target="tpu_custom_call" | custom-call | tf_op jit(solution)/shard_map/combine/pallas_call | solution.py:87
  173.8 0.0 all-gather.2.cloned.1.call-update
  173.9 69.2 %all-gather.2.cloned.1.call-done = bf16[2048,2048]{1,0:T(8,128)(2,1)} async-done(((bf16[128,2048]{1,0:T(8,128)(2,1)}), bf16[2048,2048]{1,0:T(8,128)(2,1)}) %all-gather.2.cloned.1.call-update) | async-done | bytes 8388624 | tf_op jit(solution)/shard_map/all_gather | solution.py:152
  243.1 11.1 %multiply_convert_fusion = bf16[2048,768]{1,0:T(8,128)(2,1)} fusion(bf16[2048,2048]{1,0:T(8,128)(2,1)} %all-gather.2.cloned.1.call-done, bf16[2048,512]{1,0:T(8,128)(2,1)} %param.21, bf16[2048,256]{1,0:T(8,128)(2,1)S(1)} %copy-done.1), kind=kOutput, calls=%fused_computation.2 | convolution fusion | flops 6451888128 | bytes 14680064 | tf_op jit(solution)/shard_map/dot_general | solution.py:157
  254.2 4.9 %all-to-all-start.2 = ((bf16[8,256,768]{2,1,0:T(8,128)(2,1)}), bf16[8,256,768]{2,1,0:T(8,128)(2,1)}, u32[]{:S(2)}, u32[]{:S(2)}) async-start(bf16[8,256,768]{2,1,0:T(8,128)(2,1)} %bitcast.57), calls=%async_computation.2 | async-start | bytes 6291456 | tf_op jit(solution)/shard_map/all_to_all | solution.py:162
  259.0 6.7 %convolution_convert_fusion.1 = bf16[2048,256]{1,0:T(8,128)(2,1)} fusion(bf16[2048,2048]{1,0:T(8,128)(2,1)} %all-gather.2.cloned.1.call-done, bf16[2048,256]{1,0:T(8,128)(2,1)S(1)} %copy-done.2), kind=kOutput, calls=%fused_computation.18 | convolution fusion | flops 2148007936 | bytes 10485760 | tf_op jit(solution)/shard_map/dot_general | solution.py:153
  265.7 9.1 %convolution_convert_fusion = bf16[2048,512]{1,0:T(8,128)(2,1)} fusion(bf16[2048,2048]{1,0:T(8,128)(2,1)} %all-gather.2.cloned.1.call-done, bf16[2048,512]{1,0:T(8,128)(2,1)S(1)} %copy-done), kind=kOutput, calls=%fused_computation.15 | convolution fusion | flops 4296015872 | bytes 12582912 | tf_op jit(solution)/shard_map/dot_general | solution.py:154
  274.8 21.9 %all-to-all-done.2 = bf16[8,256,768]{2,1,0:T(8,128)(2,1)} async-done(((bf16[8,256,768]{2,1,0:T(8,128)(2,1)}), bf16[8,256,768]{2,1,0:T(8,128)(2,1)}, u32[]{:S(2)}, u32[]{:S(2)}) %all-to-all-start.2) | async-done | bytes 3145760 | tf_op jit(solution)/shard_map/all_to_all | solution.py:162
  296.8 2.4 convert_reduce_fusion
  299.2 0.7 slice.8
  299.9 0.9 slice.9
  (9 shorter events, 0.0 us)
Async XLA Ops:
  7.2 258.6 %copy-start = (bf16[2048,512]{1,0:T(8,128)(2,1)S(1)}, bf16[2048,512]{1,0:T(8,128)(2,1)}, u32[]{:S(2)}) copy-start(bf16[2048,512]{1,0:T(8,128)(2,1)} %param.19) | copy-start | bytes 6291460
  13.0 58.6 %all-to-all-start = ((bf16[128,7,16,128]{3,2,1,0:T(8,128)(2,1)}), bf16[128,7,16,128]{3,2,1,0:T(8,128)(2,1)}, u32[]{:S(2)}, u32[]{:S(2)}) async-start(bf16[128,7,16,128]{3,2,1,0:T(8,128)(2,1)} %bitcast.56), calls=%async_computation | async-start | bytes 7340032 | tf_op jit(solution)/shard_map/all_to_all | solution.py:133
  24.9 218.1 %all-gather.2.cloned.1.call-start = ((), (), s32[]{:S(2)}) async-start(), calls=%async_computation.3 | async-start | bytes 8912896 | tf_op jit(solution)/shard_map/all_gather | solution.py:152
  25.0 54.2 %collective-permute-start = (bf16[704,2048]{1,0:T(8,128)(2,1)}, bf16[704,2048]{1,0:T(8,128)(2,1)}, u32[]{:S(2)}, u32[]{:S(2)}) collective-permute-start(bf16[704,2048]{1,0:T(8,128)(2,1)} %bitcast.61), channel_id=1, source_target_pairs={{0,1},{1,0},{2,3},{3,2},{4,5},{5,4},{6,7},{7,6},{8,9},{9,8},{10,11... | collective-permute-start | bytes 8650760 | tf_op jit(solution)/shard_map/ppermute | solution.py:128
  26.2 73.0 %collective-permute-start.2 = (bf16[704,2048]{1,0:T(8,128)(2,1)}, bf16[704,2048]{1,0:T(8,128)(2,1)}, u32[]{:S(2)}, u32[]{:S(2)}) collective-permute-start(bf16[704,2048]{1,0:T(8,128)(2,1)} %bitcast.62), channel_id=1, source_target_pairs={{0,1},{1,0},{2,3},{3,2},{4,5},{5,4},{6,7},{7,6},{8,9},{9,8},{10,11... | collective-permute-start | bytes 8650760 | tf_op jit(solution)/shard_map/ppermute | solution.py:130
  26.3 73.0 %collective-permute-start.1 = (bf16[704,2048]{1,0:T(8,128)(2,1)}, bf16[704,2048]{1,0:T(8,128)(2,1)}, u32[]{:S(2)}, u32[]{:S(2)}) collective-permute-start(bf16[704,2048]{1,0:T(8,128)(2,1)} %bitcast.63), channel_id=1, source_target_pairs={{0,1},{1,0},{2,3},{3,2},{4,5},{5,4},{6,7},{7,6},{8,9},{9,8},{10,11... | collective-permute-start | bytes 8650760 | tf_op jit(solution)/shard_map/ppermute | solution.py:129
  168.2 74.9 %copy-start.1 = (bf16[2048,256]{1,0:T(8,128)(2,1)S(1)}, bf16[2048,256]{1,0:T(8,128)(2,1)}, u32[]{:S(2)}) copy-start(bf16[2048,256]{1,0:T(8,128)(2,1)} %param.20) | copy-start | bytes 3145732
  254.2 4.9 %copy-start.2 = (bf16[2048,256]{1,0:T(8,128)(2,1)S(1)}, bf16[2048,256]{1,0:T(8,128)(2,1)}, u32[]{:S(2)}) copy-start(bf16[2048,256]{1,0:T(8,128)(2,1)} %param.18) | copy-start | bytes 3145732
  254.2 42.6 %all-to-all-start.2 = ((bf16[8,256,768]{2,1,0:T(8,128)(2,1)}), bf16[8,256,768]{2,1,0:T(8,128)(2,1)}, u32[]{:S(2)}, u32[]{:S(2)}) async-start(bf16[8,256,768]{2,1,0:T(8,128)(2,1)} %bitcast.57), calls=%async_computation.2 | async-start | bytes 6291456 | tf_op jit(solution)/shard_map/all_to_all | solution.py:162
Sparse Core Ops, SparseCore 0:
  174.0 69.0 all-gather.1

commit v2 on v1

--- a/solution.py
+++ b/solution.py
@@ -7,6 +7,7 @@
 from jax.experimental import pallas as pl
 from jax.experimental.pallas import tpu as pltpu
 from jax.sharding import PartitionSpec as P
+
 
 LANES = 128
 
@@ -65,7 +66,7 @@
     )(ids, tokens, gain)
 
 
-def combine_body(pos_ref, gates_ref, rows_ref, out_ref, acc_ref):
+def combine_body(pos_ref, gates_ref, rows_ref, out_ref, even_ref, odd_ref, acc_ref):
     top, toks = pos_ref.shape
     sub = rows_ref.shape[1]
 
@@ -78,12 +79,16 @@
 
     lax.fori_loop(0, toks, gather, 0, unroll=4)
     for j in range(sub):
-        out_ref[:, j * LANES : (j + 1) * LANES] = acc_ref[pl.ds(j, toks, stride=sub), :].astype(jnp.bfloat16)
+        block = acc_ref[pl.ds(j, toks, stride=sub), :].astype(jnp.bfloat16)
+        out_ref[:, j * LANES : (j + 1) * LANES] = block
+        part_ref = (even_ref, odd_ref)[j % 2]
+        part_ref[:, j // 2 * LANES : (j // 2 + 1) * LANES] = block
 
 
 def combine(pos, gates, rows):
-    top, toks = pos.shape
+    _, toks = pos.shape
     sub = rows.shape[1]
+    widths = (sub * LANES, sub // 2 * LANES, sub // 2 * LANES)
     return pl.pallas_call(
         combine_body,
         name="combine",
@@ -91,18 +96,317 @@
             num_scalar_prefetch=2,
             grid=(1,),
             in_specs=[pl.BlockSpec(rows.shape, lambda i, p, g: (0, 0, 0), pipeline_mode=pl.Buffered(1))],
-            out_specs=pl.BlockSpec((toks, sub * LANES), lambda i, p, g: (0, 0), pipeline_mode=pl.Buffered(1)),
+            out_specs=tuple(pl.BlockSpec((toks, w), lambda i, p, g: (0, 0)) for w in widths),
             scratch_shapes=[pltpu.VMEM((toks * sub, LANES), jnp.float32)],
         ),
-        out_shape=jax.ShapeDtypeStruct((toks, sub * LANES), jnp.bfloat16),
+        out_shape=tuple(jax.ShapeDtypeStruct((toks, w), jnp.bfloat16) for w in widths),
     )(pos, gates, rows)
 
 
-def half_expert(rows, gate, up, down):
-    gate_val = lax.dot_general(rows, gate, (((1,), (0,)), ((), ())), preferred_element_type=jnp.float32)
-    up_val = lax.dot_general(rows, up, (((1,), (0,)), ((), ())), preferred_element_type=jnp.float32)
-    hidden = (jax.nn.silu(gate_val) * up_val).astype(jnp.bfloat16)
-    return jnp.dot(hidden, down, preferred_element_type=jnp.float32).astype(jnp.bfloat16)
+def expert_body(rows_hbm, gate0, up0, down0, gate1, up1, down1, out_hbm,
+                rows_ref, x_ref, acc_ref, gate_ref, up_ref, down_ref, hid_ref, in_sem, w_sem, out_sem, *, step, tile, cols):
+    count, sub, _ = rows_hbm.shape
+    hidden, width = down0.shape
+    chunks = count // step
+    ins = [
+        pltpu.make_async_copy(rows_hbm.at[pl.ds(i * step, step)], rows_ref.at[pl.ds(i * step, step)], in_sem.at[i])
+        for i in range(chunks)
+    ]
+    gates = [pltpu.make_async_copy(w, gate_ref.at[h], w_sem.at[h, 0]) for h, w in enumerate((gate0, gate1))]
+    ups = [pltpu.make_async_copy(w, up_ref.at[h], w_sem.at[h, 1]) for h, w in enumerate((up0, up1))]
+    downs = [pltpu.make_async_copy(w, down_ref.at[h], w_sem.at[h, 2]) for h, w in enumerate((down0, down1))]
+    for c in ins[:2]:
+        c.start()
+    gates[0].start()
+    for c in ins[2:]:
+        c.start()
+    for c in (ups[0], gates[1], ups[1], downs[0], downs[1]):
+        c.start()
+    for i in range(chunks):
+        ins[i].wait()
+        acc_ref[pl.ds(0, step * sub), :] = rows_ref[pl.ds(i * step, step)].astype(jnp.float32).reshape(step * sub, LANES)
+        for j in range(sub):
+            x_ref[pl.ds(i * step, step), j * LANES : (j + 1) * LANES] = acc_ref[
+                pl.ds(j, step, stride=sub), :
+            ].astype(jnp.bfloat16)
+    contract = (((1,), (1,)), ((), ()))
+    for h in range(2):
+        gates[h].wait()
+        ups[h].wait()
+        for lo in range(0, hidden, tile):
+            n = min(tile, hidden - lo)
+            gate_val = lax.dot_general(x_ref[...], gate_ref[h, pl.ds(lo, n), :], contract, preferred_element_type=jnp.float32)
+            up_val = lax.dot_general(x_ref[...], up_ref[h, pl.ds(lo, n), :], contract, preferred_element_type=jnp.float32)
+            hid_ref[h, :, lo : lo + n] = (gate_val / (1.0 + jnp.exp(-gate_val)) * up_val).astype(jnp.bfloat16)
+    for c in downs:
+        c.wait()
+
+    def down_step(d, carry):
+        at = pl.ds(pl.multiple_of(d * cols, cols), cols)
+        first = jnp.dot(hid_ref[0], down_ref[0, :, at], preferred_element_type=jnp.float32).astype(jnp.bfloat16)
+        second = jnp.dot(hid_ref[1], down_ref[1, :, at], preferred_element_type=jnp.float32).astype(jnp.bfloat16)
+        both = first.astype(jnp.float32) + second.astype(jnp.float32)
+        for j in range(cols // LANES):
+            acc_ref[pl.ds(d * (cols // LANES) + j, count, stride=sub), :] = both[:, j * LANES : (j + 1) * LANES]
+        return carry
+
+    lax.fori_loop(0, width // cols, down_step, 0)
+    outs = [
+        pltpu.make_async_copy(rows_ref.at[pl.ds(i * step, step)], out_hbm.at[pl.ds(i * step, step)], out_sem.at[i])
+        for i in range(chunks)
+    ]
+    for i in range(chunks):
+        rows_ref[pl.ds(i * step, step)] = (
+            acc_ref[pl.ds(i * step * sub, step * sub), :].reshape(step, sub, LANES).astype(jnp.bfloat16)
+        )
+        outs[i].start()
+    for c in outs:
+        c.wait()
+
+
+def expert(rows, gate0, up0, down0, gate1, up1, down1, step=128, tile=256, cols=256):
+    count, sub, _ = rows.shape
+    hidden, width = down0.shape
+    chunks = count // step
+    anywhere = pl.BlockSpec(memory_space=pl.ANY)
+    return pl.pallas_call(
+        functools.partial(expert_body, step=step, tile=tile, cols=cols),
+        name="expert",
+        in_specs=[anywhere] * 7,
+        out_specs=anywhere,
+        out_shape=jax.ShapeDtypeStruct(rows.shape, jnp.bfloat16),
+        scratch_shapes=[
+            pltpu.VMEM(rows.shape, jnp.bfloat16),
+            pltpu.VMEM((count, width), jnp.bfloat16),
+            pltpu.VMEM((count * sub, LANES), jnp.float32),
+            pltpu.VMEM((2, hidden, width), jnp.bfloat16),
+            pltpu.VMEM((2, hidden, width), jnp.bfloat16),
+            pltpu.VMEM((2, hidden, width), jnp.bfloat16),
+            pltpu.VMEM((2, count, hidden), jnp.bfloat16),
+            pltpu.SemaphoreType.DMA((chunks,)),
+            pltpu.SemaphoreType.DMA((2, 3)),
+            pltpu.SemaphoreType.DMA((chunks,)),
+        ],
+        compiler_params=pltpu.CompilerParams(vmem_limit_bytes=60 * 1024 * 1024),
+    )(rows, gate0, up0, down0, gate1, up1, down1)
+
+
+VMEM_LIMIT = 60 * 1024 * 1024
+
+
+def terms_body(at_ref, *refs, pieces, scale):
+    parts = refs[:pieces]
+    cot_hbm, out_hbm, all_rows, rows_ref, cot_ref, cut_ref, sem, side_sem, out_sem = refs[pieces:]
+    count = rows_ref.shape[0]
+    block = count // (2 * pieces - 4)
+    loads = []
+    for i, piece in enumerate(parts):
+        for k in range(piece.shape[0] // block):
+            to = pl.ds(pl.multiple_of(at_ref[2 * i + k], block), block)
+            loads.append(pltpu.make_async_copy(piece.at[pl.ds(k * block, block)], rows_ref.at[to], sem.at[2 * i + k]))
+    cot_load = pltpu.make_async_copy(cot_hbm, cot_ref, side_sem.at[0])
+    cot_load.start()
+    for c in loads:
+        c.start()
+    for c in loads:
+        c.wait()
+    keep = pltpu.make_async_copy(rows_ref, all_rows, side_sem.at[1])
+    keep.start()
+    cot_load.wait()
+    owners = cut_ref.shape[0]
+
+    def step(d, carry):
+        at = pl.ds(pl.multiple_of(d * 2 * LANES, 2 * LANES), 2 * LANES)
+        terms = jnp.dot(cot_ref[...], rows_ref[:, at], preferred_element_type=jnp.float32) * scale
+        cut_ref[2 * d] = terms[:, :LANES].astype(jnp.bfloat16)
+        cut_ref[2 * d + 1] = terms[:, LANES:].astype(jnp.bfloat16)
+        pltpu.make_async_copy(cut_ref.at[pl.ds(2 * d, 2)], out_hbm.at[pl.ds(2 * d, 2)], out_sem.at[d]).start()
+        return carry
+
+    lax.fori_loop(0, owners // 2, step, 0)
+    for d in range(owners // 2):
+        pltpu.make_async_copy(cut_ref.at[pl.ds(2 * d, 2)], out_hbm.at[pl.ds(2 * d, 2)], out_sem.at[d]).wait()
+    keep.wait()
+
+
+def features_body(rows0, rows1, one_hbm, two_hbm, feat_one, feat_two, rows_ref, one_ref, two_ref, out_one, out_two, sem, row_sem, out_sem):
+    count = rows0.shape[0]
+    step = 512
+    loads = []
+    for half in range(2):
+        loads.append(pltpu.make_async_copy(one_hbm.at[:, half], one_ref.at[half], sem.at[half, 0]))
+        loads.append(pltpu.make_async_copy(two_hbm.at[:, half], two_ref.at[half], sem.at[half, 1]))
+    for c in loads:
+        c.start()
+
+    def row_loads(i):
+        at = pl.ds(i * step if isinstance(i, int) else pl.multiple_of(i * step, step), step)
+        return [
+            pltpu.make_async_copy(rows.at[at], rows_ref.at[half, at], row_sem.at[half, i])
+            for half, rows in enumerate((rows0, rows1))
+        ]
+
+    def stores(i):
+        at = pl.ds(i * step if isinstance(i, int) else pl.multiple_of(i * step, step), step)
+        return [
+            pltpu.make_async_copy(out_one.at[at], feat_one.at[at], out_sem.at[0, i]),
+            pltpu.make_async_copy(out_two.at[at], feat_two.at[at], out_sem.at[1, i]),
+        ]
+
+    for i in range(count // step):
+        for c in row_loads(i):
+            c.start()
+    for c in loads:
+        c.wait()
+
+    def body(i, carry):
+        for c in row_loads(i):
+            c.wait()
+        at = pl.ds(pl.multiple_of(i * step, step), step)
+        for w_ref, out_ref in ((one_ref, out_one), (two_ref, out_two)):
+            for lo in range(0, w_ref.shape[-1], 256):
+                total = [
+                    jnp.dot(
+                        rows_ref[half, at, :],
+                        w_ref[half, :, :, lo : lo + 256].reshape(-1, 256),
+                        preferred_element_type=jnp.float32,
+                    )
+                    for half in range(2)
+                ]
+                out_ref[at, lo : lo + 256] = (total[0] + total[1]).astype(jnp.bfloat16)
+        for c in stores(i):
+            c.start()
+        return carry
+
+    lax.fori_loop(0, count // step, body, 0)
+    for i in range(count // step):
+        for c in stores(i):
+            c.wait()
+
+
+def total_of(pieces_ref):
+    total = pieces_ref[0].astype(jnp.float32)
+    for i in range(1, pieces_ref.shape[0]):
+        total = total + pieces_ref[i].astype(jnp.float32)
+    return total.T
+
+
+def sum_first_body(pieces_ref, out_ref):
+    out_ref[...] = total_of(pieces_ref)
+
+
+def sum_last_body(first_ref, pieces_ref, one_ref, two_ref):
+    split = one_ref.shape[1]
+    half = first_ref.shape[0]
+    one_ref[:half] = first_ref[:, :split]
+    two_ref[:half] = first_ref[:, split:]
+    total = total_of(pieces_ref)
+    one_ref[half:] = total[:, :split]
+    two_ref[half:] = total[:, split:]
+
+
+def project(parts, student_one, student_two, cots, move, place):
+    rows, half_width = parts[0].shape
+    y_hi, x, core = place
+    ring, owners = 4, 8
+    count = 4 * ring * rows
+    split = student_one.shape[1]
+    cols = split + student_two.shape[1]
+    bf16, f32 = jnp.bfloat16, jnp.float32
+    dma = pltpu.SemaphoreType.DMA
+    anywhere = pl.BlockSpec(memory_space=pl.ANY)
+
+    def row_of(y, at, c):
+        return (y * ring + at % ring) * (2 * rows) + c * rows
+
+    spots = []
+    for c in (core, 1 - core):
+        for at in (x, x + ring - 1, x + 1):
+            spots += [row_of(y_hi, at, c), row_of(1 - y_hi, at, c)]
+        spots += [row_of(y_hi, x + 2, c), 0, row_of(1 - y_hi, x + 2, c), 0]
+    spots = jnp.stack(spots).astype(jnp.int32)
+
+    def gather(part, other):
+        both = jnp.concatenate([part, other], axis=0)
+        right = move(both, 0, 1, 0)
+        left = move(both, 0, -1, 0)
+        far_right = move(right[:rows], 0, 1, 0)
+        far_left = move(left[rows:], 0, -1, 0)
+        own = [both, right, left, far_right, far_left]
+        swapped = []
+        for piece in own:
+            swapped.append(move(piece, 0, 0, 1))
+        return own + swapped
+
+    def terms(pieces):
+        return pl.pallas_call(
+            functools.partial(terms_body, pieces=len(pieces), scale=1.0 / math.sqrt(count * owners)),
+            name="terms",
+            grid_spec=pltpu.PrefetchScalarGridSpec(
+                num_scalar_prefetch=1,
+                grid=(1,),
+                in_specs=[anywhere] * (len(pieces) + 1),
+                out_specs=(anywhere, anywhere),
+                scratch_shapes=[
+                    pltpu.VMEM((count, half_width), bf16),
+                    pltpu.VMEM((cols, count), bf16),
+                    pltpu.VMEM((owners, cols, LANES), bf16),
+                    dma((2 * len(pieces),)),
+                    dma((2,)),
+                    dma((owners // 2,)),
+                ],
+            ),
+            out_shape=(
+                jax.ShapeDtypeStruct((owners, cols, LANES), bf16),
+                jax.ShapeDtypeStruct((count, half_width), bf16),
+            ),
+            compiler_params=pltpu.CompilerParams(vmem_limit_bytes=VMEM_LIMIT),
+            cost_estimate=pl.CostEstimate(
+                flops=2 * count * half_width * cols, transcendentals=0, bytes_accessed=12 << 20
+            ),
+        )(spots, *pieces, cots)
+
+    other0 = move(parts[0], 2, 0, 0)
+    other1 = move(parts[1], 2, 0, 0)
+    cut0, rows0 = terms(gather(parts[0], other0))
+    cut0 = lax.all_to_all(cut0, "dp", split_axis=0, concat_axis=0, tiled=True)
+    cut1, rows1 = terms(gather(parts[1], other1))
+    cut1 = lax.all_to_all(cut1, "dp", split_axis=0, concat_axis=0, tiled=True)
+    shape = (owners, 2, LANES)
+    feat_one, feat_two = pl.pallas_call(
+        features_body,
+        name="features",
+        in_specs=[anywhere] * 4,
+        out_specs=(anywhere, anywhere),
+        out_shape=(
+            jax.ShapeDtypeStruct((count, split), bf16),
+            jax.ShapeDtypeStruct((count, cols - split), bf16),
+        ),
+        scratch_shapes=[
+            pltpu.VMEM((2, count, half_width), bf16),
+            pltpu.VMEM((2, owners, LANES, split), bf16),
+            pltpu.VMEM((2, owners, LANES, cols - split), bf16),
+            pltpu.VMEM((count, split), bf16),
+            pltpu.VMEM((count, cols - split), bf16),
+            dma((2, 2)),
+            dma((2, count // 512)),
+            dma((2, count // 512)),
+        ],
+        compiler_params=pltpu.CompilerParams(vmem_limit_bytes=VMEM_LIMIT),
+        cost_estimate=pl.CostEstimate(flops=4 * count * half_width * cols, transcendentals=0, bytes_accessed=14 << 20),
+    )(rows0, rows1, student_one.reshape(*shape, split), student_two.reshape(*shape, cols - split))
+    total0 = pl.pallas_call(
+        sum_first_body, name="sum_first", out_shape=jax.ShapeDtypeStruct((LANES, cols), f32)
+    )(cut0)
+    grad_one, grad_two = pl.pallas_call(
+        sum_last_body,
+        name="sum_last",
+        out_shape=(
+            jax.ShapeDtypeStruct((2 * LANES, split), f32),
+            jax.ShapeDtypeStruct((2 * LANES, cols - split), f32),
+        ),
+    )(total0, cut1)
+    return feat_one, feat_two, grad_one, grad_two
 
 
 def local(
@@ -124,10 +428,21 @@
     experts = devices // 2
     capacity = 2 * ((tok_dev * top_count * 7 + 12 * experts - 1) // (12 * experts))
     sub = model_width // LANES
-    partner = [(i, i ^ 1) for i in range(lax.axis_size("expert"))]
-    other_gate = lax.ppermute(jnp.swapaxes(gate_proj[0], 0, 1), "expert", partner)
-    other_up = lax.ppermute(jnp.swapaxes(up_proj[0], 0, 1), "expert", partner)
-    other_down = lax.ppermute(down_proj[0], "expert", partner)
+    axes = ("dp", "expert")
+    index = lax.axis_index(axes)
+
+    def move(array, y, x, core):
+        def target(d):
+            z, y_lo, y_hi, at_x, at_core = d // 32, d // 16 % 2, d // 8 % 2, d // 2 % 4, d % 2
+            to_y = (y_hi * 2 + y_lo + y) % 4
+            return z * 32 + to_y % 2 * 16 + to_y // 2 * 8 + (at_x + x) % 4 * 2 + (at_core + core) % 2
+
+        return lax.ppermute(array, axes, [(d, target(d)) for d in range(devices)])
+
+    cots = jnp.concatenate([cot_one, cot_two], axis=1).T
+    other_gate = move(jnp.swapaxes(gate_proj[0], 0, 1), 0, 0, 1)
+    other_up = move(jnp.swapaxes(up_proj[0], 0, 1), 0, 0, 1)
+    other_down, cots = lax.optimization_barrier((move(down_proj[0], 0, 0, 1), cots))
 
     placed, positions = dispatch(expert_ids.T, tokens, norm_gain.reshape(1, -1), experts, capacity)
     received = lax.all_to_all(
@@ -137,10 +452,15 @@
         concat_axis=0,
         tiled=True,
     )
-    flat_rows = received.reshape(devices * capacity // 2, model_width)
-    first = half_expert(flat_rows, gate_proj[0], up_proj[0], down_proj[0])
-    second = half_expert(flat_rows, other_gate.T, other_up.T, other_down)
-    expert_out = (first.astype(jnp.float32) + second.astype(jnp.float32)).astype(jnp.bfloat16)
+    expert_out = expert(
+        received.reshape(devices * capacity // 2, sub, LANES),
+        jnp.swapaxes(gate_proj[0], 0, 1),
+        jnp.swapaxes(up_proj[0], 0, 1),
+        down_proj[0],
+        other_gate,
+        other_up,
+        other_down,
+    )
     returned = lax.all_to_all(
         expert_out.reshape(devices, capacity // 2, sub, LANES),
         ("dp", "expert"),
@@ -148,21 +468,11 @@
         concat_axis=0,
         tiled=True,
     )
-    layer_out = combine(positions, gate_weights.T, returned.reshape(experts * capacity, sub, LANES))
-    gathered = lax.all_gather(layer_out, "expert", axis=0, tiled=True)
-    feat_one = jnp.dot(gathered, student_one, preferred_element_type=jnp.float32).astype(jnp.bfloat16)
-    feat_two = jnp.dot(gathered, student_two, preferred_element_type=jnp.float32).astype(jnp.bfloat16)
-    cotangents = jnp.concatenate([cot_one, cot_two], axis=1)
-    grad_scale = 1.0 / math.sqrt(gathered.shape[0] * lax.axis_size("dp"))
-    terms = lax.dot_general(
-        gathered, cotangents, (((0,), (0,)), ((), ())), preferred_element_type=jnp.float32
+    layer_out, *parts = combine(positions, gate_weights.T, returned.reshape(experts * capacity, sub, LANES))
+    feat_one, feat_two, grad_one, grad_two = project(
+        parts, student_one, student_two, cots, move, (index // 8 % 2, index // 2 % 4, index % 2)
     )
-    batches = lax.axis_size("dp")
-    pieces = (terms * grad_scale).astype(jnp.bfloat16).reshape(batches, model_width // batches, -1)
-    pieces = lax.all_to_all(pieces, "dp", split_axis=0, concat_axis=0, tiled=True)
-    grads = jnp.sum(pieces.astype(jnp.float32), axis=0)
-    split_at = student_one.shape[1]
-    return (layer_out, feat_one, feat_two, grads[:, :split_at], grads[:, split_at:])
+    return (layer_out, feat_one, feat_two, grad_one, grad_two)
 
 
 def solution(mesh):

time: 308 us -> 269 us (0.87)
  matrix products: 68.3 us -> 0 us
  Pallas kernels: 11.5 us -> 75.1 us
  waiting for transfers between devices: 136 us -> 78.3 us
  starting transfers between devices: 18.5 us -> 49.2 us
  between operations: 14.1 us -> 0.95 us
  local copies, waits for them, and re-layouts: 4.83 us -> 9.78 us
    all_gather x1 -> x0, waiting for transfers between devices: 69.2 us -> none  [local(): gathered = lax.all_gather(layer_out, 'expert', axis=0, tiled=True)]
    dot_general x7 -> x0, matrix products: 68.3 us -> none  [the longest x2 26.3 us: half_expert(): jnp.dot(hidden, down, preferred_element_type=jnp.float32)]
    pallas_call x0 -> x6, Pallas kernels: none -> 63.8 us  [the longest x1 29.1 us: expert(): pl.pallas_call(functools.partial(expert_body, step=step, tile=tile, cols=...]
    ppermute x3 -> x23, waiting for transfers between devices: 0.01 us -> 40.1 us  [move(): return lax.ppermute(array, axes, [(d, target(d)) for d in range(devices)])]
    ppermute x3 -> x23, starting transfers between devices: 1.72 us -> 28.5 us  [move(): return lax.ppermute(array, axes, [(d, target(d)) for d in range(devices)])]
    all_to_all x1 -> x2, waiting for transfers between devices: 21.9 us -> 6.2 us  [the longest x1 6.2 us: project(): cut1 = lax.all_to_all(cut1, 'dp', split_axis=0, concat_axis=0, tiled=True)]
    all_to_all x1, waiting for transfers between devices: 45 us -> 32 us  [local(): lax.all_to_all(placed.reshape(devices, capacity // 2, sub, LANES), ('dp',...]
    unnamed x7 -> x40, local copies, waits for them, and re-layouts: 3.26 us -> 8.97 us
  transfers between devices with their start and end apart: 6 -> 26, of which waited for: 3 -> 12; matrix products, arithmetic and copies ran while one was open for 14% -> 3% of each run, Pallas kernels for 0% -> 12%
where the time goes in v2:
time: 269 us; the launch traced here: 268 us
  waiting for transfers between devices  78.3 us (29%)
  Pallas kernels  75.1 us (28%)
  blocking collectives  52.9 us (20%)
  starting transfers between devices  49.2 us (18%)
  local copies, waits for them, and re-layouts  9.78 us (4%)
    all_to_all x1, blocking collectives, local(): lax.all_to_all(expert_out.reshape(devices, capacity // 2, sub, LANES), ('...  52.9 us
    ppermute x23, waiting for transfers between devices, move(): return lax.ppermute(array, axes, [(d, target(d)) for d in range(devices)])  40.1 us
    all_to_all x1, waiting for transfers between devices, local(): lax.all_to_all(placed.reshape(devices, capacity // 2, sub, LANES), ('dp',...  32 us
    pallas_call x1, Pallas kernels, expert(): pl.pallas_call(functools.partial(expert_body, step=step, tile=tile, cols=...  29.1 us
    ppermute x23, starting transfers between devices, move(): return lax.ppermute(array, axes, [(d, target(d)) for d in range(devices)])  28.5 us
    pallas_call x2, Pallas kernels, terms(): pl.pallas_call(functools.partial(terms_body, pieces=len(pieces), scale=1....  17.5 us
    pallas_call x1, Pallas kernels, project(): pl.pallas_call(features_body, name='features', in_specs=[anywhere] * 4, o...  12.2 us
    all_to_all x1, starting transfers between devices, local(): lax.all_to_all(placed.reshape(devices, capacity // 2, sub, LANES), ('dp',...  11.9 us
  transfers between devices with their start and end apart: 26, of which 12 were waited for; matrix products, arithmetic and copies ran while one was open for 3% of the time, Pallas kernels for 12%

profile of v2, /device:TPU:1, one launch (start us, length us, event | category | flops | bytes accessed | tf_op | source)
XLA Modules:
  0.0 268.0 jit_solution(16777381947775277428)
XLA Ops:
  0.6 5.7 %dispatch.1 = (bf16[896,16,128]{2,1,0:T(8,128)(2,1)}, s32[6,128]{1,0:T(8,128)}) custom-call(s32[6,128]{1,0:T(8,128)} %bitcast.38, bf16[128,2048]{1,0:T(8,128)(2,1)} %tok_ref.1, f32[1,2048]{1,0:T(1,128)} %bitcast.37), custom_call_target="tpu_custom_call" | custom-call | tf_op jit(solution)/shard_map/dispatch/pallas_call | solution.py:54
  6.3 11.9 %all-to-all-start = ((bf16[128,7,16,128]{3,2,1,0:T(8,128)(2,1)}), bf16[128,7,16,128]{3,2,1,0:T(8,128)(2,1)}, u32[]{:S(2)}, u32[]{:S(2)}) async-start(bf16[128,7,16,128]{3,2,1,0:T(8,128)(2,1)} %bitcast.36), calls=%async_computation | async-start | bytes 7340032 | tf_op jit(solution)/shard_map/all_to_all | solution.py:448
  20.6 3.1 %copy.17 = bf16[2048,512]{0,1:T(8,128)(2,1)S(1)} copy(bf16[2048,512]{1,0:T(8,128)(2,1)} %param.21) | data formatting | bytes 4194304 | tf_op args[10]
  25.6 3.3 %collective-permute-done.gate1 = bf16[704,2048]{1,0:T(8,128)(2,1)} collective-permute-done((bf16[704,2048]{1,0:T(8,128)(2,1)}, bf16[704,2048]{1,0:T(8,128)(2,1)}, u32[]{:S(2)}, u32[]{:S(2)}) %collective-permute-start) | collective-permute-done | bytes 2883616 | tf_op jit(solution)/shard_map/ppermute | solution.py:440
  28.8 4.1 %collective-permute-done.1.up1 = bf16[704,2048]{1,0:T(8,128)(2,1)} collective-permute-done((bf16[704,2048]{1,0:T(8,128)(2,1)}, bf16[704,2048]{1,0:T(8,128)(2,1)}, u32[]{:S(2)}, u32[]{:S(2)}) %collective-permute-start.1) | collective-permute-done | bytes 2883616 | tf_op jit(solution)/shard_map/ppermute | solution.py:440
  33.0 32.0 %all-to-all-done = bf16[128,7,16,128]{3,2,1,0:T(8,128)(2,1)} async-done(((bf16[128,7,16,128]{3,2,1,0:T(8,128)(2,1)}), bf16[128,7,16,128]{3,2,1,0:T(8,128)(2,1)}, u32[]{:S(2)}, u32[]{:S(2)}) %all-to-all-start) | async-done | bytes 3670048 | tf_op jit(solution)/shard_map/all_to_all | solution.py:448
  65.0 29.1 %expert.1 = bf16[896,16,128]{2,1,0:T(8,128)(2,1)} custom-call(bf16[896,16,128]{2,1,0:T(8,128)(2,1)} %bitcast.4.rows_hbm, bf16[704,2048]{1,0:T(8,128)(2,1)} %bitcast.6.gate0, bf16[704,2048]{1,0:T(8,128)(2,1)} %bitcast.8.up0, bf16[704,2048]{1,0:T(8,128)(2,1)} %bitcast.9.down0, bf16[704,2048]{1,0:T(8,128)(2,1)} %collective-permute-done.gate1, ...), custom_call_target="tpu_custom_call" | custom-call | tf_op jit(solution)/shard_map/expert/pallas_call | solution.py:172
  94.0 52.9 %all_to_all.20 = bf16[128,7,16,128]{3,2,1,0:T(8,128)(2,1)} all-to-all(bf16[128,7,16,128]{3,2,1,0:T(8,128)(2,1)} %bitcast.35), channel_id=1, replica_groups=mesh['dp'=8,'expert'=16] {'dp','expert'}, dimensions={0} | all-to-all | bytes 7340032 | tf_op jit(solution)/shard_map/all_to_all | solution.py:464
  146.9 5.6 %combine.1 = (bf16[128,2048]{1,0:T(8,128)(2,1)}, bf16[128,1024]{1,0:T(8,128)(2,1)}, bf16[128,1024]{1,0:T(8,128)(2,1)}) custom-call(s32[6,128]{1,0:T(8,128)} %get-tuple-element.20.pos_ref, f32[6,128]{1,0:T(8,128)} %bitcast.39, bf16[896,16,128]{2,1,0:T(8,128)(2,1)} %bitcast.34), custom_call_target="tpu_custom_call" | custom-call | tf_op jit(solution)/shard_map/combine/pallas_call | solution.py:92
  154.3 6.6 %collective-permute-done.3 = bf16[128,1024]{1,0:T(8,128)(2,1)S(1)} collective-permute-done((bf16[128,1024]{1,0:T(8,128)(2,1)}, bf16[128,1024]{1,0:T(8,128)(2,1)S(1)}, u32[]{:S(2)}, u32[]{:S(2)}) %collective-permute-start.3) | collective-permute-done | bytes 262176 | tf_op jit(solution)/shard_map/ppermute | solution.py:440
  165.1 7.8 %collective-permute-done.5.refs_2_ = bf16[256,1024]{1,0:T(8,128)(2,1)S(1)} collective-permute-done((bf16[256,1024]{1,0:T(8,128)(2,1)S(1)}, bf16[256,1024]{1,0:T(8,128)(2,1)S(1)}, u32[]{:S(2)}, u32[]{:S(2)}) %collective-permute-start.5) | collective-permute-done | bytes 524320 | tf_op jit(solution)/shard_map/ppermute | solution.py:440
  173.0 3.5 %collective-permute-start.7 = (bf16[128,1024]{1,0:T(8,128)(2,1)S(1)}, bf16[128,1024]{1,0:T(8,128)(2,1)S(1)}, u32[]{:S(2)}, u32[]{:S(2)}) collective-permute-start(bf16[128,1024]{1,0:T(8,128)(2,1)S(1)} %slice.17), channel_id=1, source_target_pairs={{0,6},{1,7},{2,0},{3,1},{4,2},{5,3},{6,4},{7,5},{8,14},{9,15},{10,... | collective-permute-start | bytes 786440 | tf_op jit(solution)/shard_map/ppermute | solution.py:440
  180.1 2.9 %collective-permute-start.12 = (bf16[128,1024]{1,0:T(8,128)(2,1)S(1)}, bf16[128,1024]{1,0:T(8,128)(2,1)}, u32[]{:S(2)}, u32[]{:S(2)}) collective-permute-start(bf16[128,1024]{1,0:T(8,128)(2,1)S(1)} %collective-permute-done.7.refs_4_), channel_id=1, source_target_pairs={{0,1},{1,0},{2,3},{3,2},{4,5},{5,4},{6,7},{7,6},{8,9},{9,8},{10,11... | collective-permute-start | bytes 786440 | tf_op jit(solution)/shard_map/ppermute | solution.py:440
  183.4 3.2 %collective-permute-start.11 = (bf16[128,1024]{1,0:T(8,128)(2,1)}, bf16[128,1024]{1,0:T(8,128)(2,1)}, u32[]{:S(2)}, u32[]{:S(2)}) collective-permute-start(bf16[128,1024]{1,0:T(8,128)(2,1)} %collective-permute-done.6.refs_3_), channel_id=1, source_target_pairs={{0,1},{1,0},{2,3},{3,2},{4,5},{5,4},{6,7},{7,6},{8,9},{9,8},{10,11... | collective-permute-start | bytes 786440 | tf_op jit(solution)/shard_map/ppermute | solution.py:440
  189.1 8.7 %terms.2 = (bf16[8,768,128]{2,1,0:T(8,128)(2,1)}, bf16[2048,1024]{1,0:T(8,128)(2,1)}) custom-call(s32[20]{0:T(128)} %stack.67.at_ref, bf16[256,1024]{1,0:T(8,128)(2,1)} %copy-done.9, bf16[256,1024]{1,0:T(8,128)(2,1)} %copy-done.5, bf16[256,1024]{1,0:T(8,128)(2,1)} %copy-done.4, bf16[128,1024]{1,0:T(8,128)(2,1)} %collective-permute-done.6.refs_3_, ...), custom_call_target="tpu_custom_call" | custom-call | flops 3221225472 | bytes 12582912 | tf_op jit(solution)/shard_map/terms/pallas_call | solution.py:342
  197.9 3.6 %all-to-all-start.2 = ((bf16[8,768,128]{2,1,0:T(8,128)(2,1)}), bf16[8,768,128]{2,1,0:T(8,128)(2,1)S(1)}, u32[]{:S(2)}, u32[]{:S(2)}) async-start(bf16[8,768,128]{2,1,0:T(8,128)(2,1)} %get-tuple-element.31), calls=%async_computation.2 | async-start | bytes 3145728 | tf_op jit(solution)/shard_map/all_to_all | solution.py:372
  204.2 10.3 %collective-permute-done.15.refs_2_ = bf16[256,1024]{1,0:T(8,128)(2,1)S(1)} collective-permute-done((bf16[256,1024]{1,0:T(8,128)(2,1)S(1)}, bf16[256,1024]{1,0:T(8,128)(2,1)S(1)}, u32[]{:S(2)}, u32[]{:S(2)}) %collective-permute-start.15) | collective-permute-done | bytes 524320 | tf_op jit(solution)/shard_map/ppermute | solution.py:440
  218.2 2.9 %collective-permute-done.17.refs_4_ = bf16[128,1024]{1,0:T(8,128)(2,1)S(1)} collective-permute-done((bf16[128,1024]{1,0:T(8,128)(2,1)S(1)}, bf16[128,1024]{1,0:T(8,128)(2,1)S(1)}, u32[]{:S(2)}, u32[]{:S(2)}) %collective-permute-start.17) | collective-permute-done | bytes 262176 | tf_op jit(solution)/shard_map/ppermute | solution.py:440
  223.3 3.4 %collective-permute-done.16.refs_3_ = bf16[128,1024]{1,0:T(8,128)(2,1)S(1)} collective-permute-done((bf16[128,1024]{1,0:T(8,128)(2,1)S(1)}, bf16[128,1024]{1,0:T(8,128)(2,1)S(1)}, u32[]{:S(2)}, u32[]{:S(2)}) %collective-permute-start.16) | collective-permute-done | bytes 262176 | tf_op jit(solution)/shard_map/ppermute | solution.py:440
  229.5 8.8 %terms.3 = (bf16[8,768,128]{2,1,0:T(8,128)(2,1)}, bf16[2048,1024]{1,0:T(8,128)(2,1)}) custom-call(s32[20]{0:T(128)} %stack.67.at_ref, bf16[256,1024]{1,0:T(8,128)(2,1)} %copy-done.8, bf16[256,1024]{1,0:T(8,128)(2,1)} %copy-done.7, bf16[256,1024]{1,0:T(8,128)(2,1)} %copy-done.6, bf16[128,1024]{1,0:T(8,128)(2,1)} %copy-done.15, bf16[128,1024]{1,0:T(8,128)(2,1)} %copy-done.14, ...), custom_call_target="tpu_custom_call" | custom-call | flops 3221225472 | bytes 12582912 | tf_op jit(solution)/shard_map/terms/pallas_call | solution.py:342
  238.3 5.1 %all-to-all-start.3 = ((bf16[8,768,128]{2,1,0:T(8,128)(2,1)}), bf16[8,768,128]{2,1,0:T(8,128)(2,1)S(1)}, u32[]{:S(2)}, u32[]{:S(2)}) async-start(bf16[8,768,128]{2,1,0:T(8,128)(2,1)} %get-tuple-element.32), calls=%async_computation.3 | async-start | bytes 3145728 | tf_op jit(solution)/shard_map/all_to_all | solution.py:374
  243.4 12.2 %features.1 = (bf16[2048,256]{1,0:T(8,128)(2,1)}, bf16[2048,512]{1,0:T(8,128)(2,1)}) custom-call(bf16[2048,1024]{1,0:T(8,128)(2,1)} %get-tuple-element.26.rows0, bf16[2048,1024]{1,0:T(8,128)(2,1)} %get-tuple-element.28.rows1, bf16[8,2,128,256]{3,2,1,0:T(8,128)(2,1)} %bitcast.41, bf16[8,2,128,512]{3,2,1,0:T(8,128)(2,1)} %bitcast.40), custom_call_target="tpu_custom_call" | custom-call | flops 6442450944 | bytes 14680064 | tf_op jit(solution)/shard_map/features/pallas_call | solution.py:376
  258.0 6.2 %all-to-all-done.3.pieces_ref = bf16[8,768,128]{2,1,0:T(8,128)(2,1)S(1)} async-done(((bf16[8,768,128]{2,1,0:T(8,128)(2,1)}), bf16[8,768,128]{2,1,0:T(8,128)(2,1)S(1)}, u32[]{:S(2)}, u32[]{:S(2)}) %all-to-all-start.3) | async-done | bytes 1572896 | tf_op jit(solution)/shard_map/all_to_all | solution.py:374
  265.4 2.6 sum_last.1
  (85 shorter events, 31.5 us)
Async XLA Ops:
  6.3 58.6 %all-to-all-start = ((bf16[128,7,16,128]{3,2,1,0:T(8,128)(2,1)}), bf16[128,7,16,128]{3,2,1,0:T(8,128)(2,1)}, u32[]{:S(2)}, u32[]{:S(2)}) async-start(bf16[128,7,16,128]{3,2,1,0:T(8,128)(2,1)} %bitcast.36), calls=%async_computation | async-start | bytes 7340032 | tf_op jit(solution)/shard_map/all_to_all | solution.py:448
  18.2 7.3 %collective-permute-start.2 = (bf16[704,2048]{1,0:T(8,128)(2,1)}, bf16[704,2048]{1,0:T(8,128)(2,1)}, u32[]{:S(2)}, u32[]{:S(2)}) collective-permute-start(bf16[704,2048]{1,0:T(8,128)(2,1)} %bitcast.9.down0), channel_id=1, source_target_pairs={{0,1},{1,0},{2,3},{3,2},{4,5},{5,4},{6,7},{7,6},{8,9},{9,8},{10,11... | collective-permute-start | bytes 8650760 | tf_op jit(solution)/shard_map/ppermute | solution.py:440
  19.5 9.4 %collective-permute-start = (bf16[704,2048]{1,0:T(8,128)(2,1)}, bf16[704,2048]{1,0:T(8,128)(2,1)}, u32[]{:S(2)}, u32[]{:S(2)}) collective-permute-start(bf16[704,2048]{1,0:T(8,128)(2,1)} %bitcast.6.gate0), channel_id=1, source_target_pairs={{0,1},{1,0},{2,3},{3,2},{4,5},{5,4},{6,7},{7,6},{8,9},{9,8},{10,11... | collective-permute-start | bytes 8650760 | tf_op jit(solution)/shard_map/ppermute | solution.py:440
  19.6 13.4 %collective-permute-start.1 = (bf16[704,2048]{1,0:T(8,128)(2,1)}, bf16[704,2048]{1,0:T(8,128)(2,1)}, u32[]{:S(2)}, u32[]{:S(2)}) collective-permute-start(bf16[704,2048]{1,0:T(8,128)(2,1)} %bitcast.8.up0), channel_id=1, source_target_pairs={{0,1},{1,0},{2,3},{3,2},{4,5},{5,4},{6,7},{7,6},{8,9},{9,8},{10,11... | collective-permute-start | bytes 8650760 | tf_op jit(solution)/shard_map/ppermute | solution.py:440
  152.5 8.3 %collective-permute-start.3 = (bf16[128,1024]{1,0:T(8,128)(2,1)}, bf16[128,1024]{1,0:T(8,128)(2,1)S(1)}, u32[]{:S(2)}, u32[]{:S(2)}) collective-permute-start(bf16[128,1024]{1,0:T(8,128)(2,1)} %get-tuple-element.24), channel_id=1, source_target_pairs={{0,8},{1,9},{2,10},{3,11},{4,12},{5,13},{6,14},{7,15},{8,0},{9,1},... | collective-permute-start | bytes 786440 | tf_op jit(solution)/shard_map/ppermute | solution.py:440
  160.9 12.1 %collective-permute-start.5 = (bf16[256,1024]{1,0:T(8,128)(2,1)S(1)}, bf16[256,1024]{1,0:T(8,128)(2,1)S(1)}, u32[]{:S(2)}, u32[]{:S(2)}) collective-permute-start(bf16[256,1024]{1,0:T(8,128)(2,1)S(1)} %constant_dynamic-update-slice_fusion.refs_0_), channel_id=1, source_target_pairs={{0,6},{1,7},{2,0},{3,1},{4,2},{5,3},{6,4},{7,5},{8,14},{9,15},{10,... | collective-permute-start | bytes 1572872 | tf_op jit(solution)/shard_map/ppermute | solution.py:440
  162.9 13.6 %collective-permute-start.4 = (bf16[256,1024]{1,0:T(8,128)(2,1)S(1)}, bf16[256,1024]{1,0:T(8,128)(2,1)S(1)}, u32[]{:S(2)}, u32[]{:S(2)}) collective-permute-start(bf16[256,1024]{1,0:T(8,128)(2,1)S(1)} %constant_dynamic-update-slice_fusion.refs_0_), channel_id=1, source_target_pairs={{0,2},{1,3},{2,4},{3,5},{4,6},{5,7},{6,0},{7,1},{8,10},{9,11},{10,... | collective-permute-start | bytes 1572872 | tf_op jit(solution)/shard_map/ppermute | solution.py:440
  162.9 25.4 %collective-permute-start.8 = (bf16[256,1024]{1,0:T(8,128)(2,1)S(1)}, bf16[256,1024]{1,0:T(8,128)(2,1)S(1)}, u32[]{:S(2)}, u32[]{:S(2)}) collective-permute-start(bf16[256,1024]{1,0:T(8,128)(2,1)S(1)} %constant_dynamic-update-slice_fusion.refs_0_), channel_id=1, source_target_pairs={{0,1},{1,0},{2,3},{3,2},{4,5},{5,4},{6,7},{7,6},{8,9},{9,8},{10,11... | collective-permute-start | bytes 1572872 | tf_op jit(solution)/shard_map/ppermute | solution.py:440
  173.0 7.1 %collective-permute-start.7 = (bf16[128,1024]{1,0:T(8,128)(2,1)S(1)}, bf16[128,1024]{1,0:T(8,128)(2,1)S(1)}, u32[]{:S(2)}, u32[]{:S(2)}) collective-permute-start(bf16[128,1024]{1,0:T(8,128)(2,1)S(1)} %slice.17), channel_id=1, source_target_pairs={{0,6},{1,7},{2,0},{3,1},{4,2},{5,3},{6,4},{7,5},{8,14},{9,15},{10,... | collective-permute-start | bytes 786440 | tf_op jit(solution)/shard_map/ppermute | solution.py:440
  176.5 6.9 %collective-permute-start.6 = (bf16[128,1024]{1,0:T(8,128)(2,1)S(1)}, bf16[128,1024]{1,0:T(8,128)(2,1)}, u32[]{:S(2)}, u32[]{:S(2)}) collective-permute-start(bf16[128,1024]{1,0:T(8,128)(2,1)S(1)} %slice.16), channel_id=1, source_target_pairs={{0,2},{1,3},{2,4},{3,5},{4,6},{5,7},{6,0},{7,1},{8,10},{9,11},{10,... | collective-permute-start | bytes 786440 | tf_op jit(solution)/shard_map/ppermute | solution.py:440
  176.6 12.0 %collective-permute-start.10 = (bf16[256,1024]{1,0:T(8,128)(2,1)S(1)}, bf16[256,1024]{1,0:T(8,128)(2,1)}, u32[]{:S(2)}, u32[]{:S(2)}) collective-permute-start(bf16[256,1024]{1,0:T(8,128)(2,1)S(1)} %collective-permute-done.5.refs_2_), channel_id=1, source_target_pairs={{0,1},{1,0},{2,3},{3,2},{4,5},{5,4},{6,7},{7,6},{8,9},{9,8},{10,11... | collective-permute-start | bytes 1572872 | tf_op jit(solution)/shard_map/ppermute | solution.py:440
  179.0 9.6 %collective-permute-start.9 = (bf16[256,1024]{1,0:T(8,128)(2,1)S(1)}, bf16[256,1024]{1,0:T(8,128)(2,1)}, u32[]{:S(2)}, u32[]{:S(2)}) collective-permute-start(bf16[256,1024]{1,0:T(8,128)(2,1)S(1)} %collective-permute-done.4.refs_1_), channel_id=1, source_target_pairs={{0,1},{1,0},{2,3},{3,2},{4,5},{5,4},{6,7},{7,6},{8,9},{9,8},{10,11... | collective-permute-start | bytes 1572872 | tf_op jit(solution)/shard_map/ppermute | solution.py:440
  180.1 8.5 %collective-permute-start.12 = (bf16[128,1024]{1,0:T(8,128)(2,1)S(1)}, bf16[128,1024]{1,0:T(8,128)(2,1)}, u32[]{:S(2)}, u32[]{:S(2)}) collective-permute-start(bf16[128,1024]{1,0:T(8,128)(2,1)S(1)} %collective-permute-done.7.refs_4_), channel_id=1, source_target_pairs={{0,1},{1,0},{2,3},{3,2},{4,5},{5,4},{6,7},{7,6},{8,9},{9,8},{10,11... | collective-permute-start | bytes 786440 | tf_op jit(solution)/shard_map/ppermute | solution.py:440
  188.3 13.2 %collective-permute-start.13 = (bf16[128,1024]{1,0:T(8,128)(2,1)S(1)}, bf16[128,1024]{1,0:T(8,128)(2,1)S(1)}, u32[]{:S(2)}, u32[]{:S(2)}) collective-permute-start(bf16[128,1024]{1,0:T(8,128)(2,1)S(1)} %copy-done.3), channel_id=1, source_target_pairs={{0,8},{1,9},{2,10},{3,11},{4,12},{5,13},{6,14},{7,15},{8,0},{9,1},... | collective-permute-start | bytes 786440 | tf_op jit(solution)/shard_map/ppermute | solution.py:440
  197.9 40.4 %all-to-all-start.2 = ((bf16[8,768,128]{2,1,0:T(8,128)(2,1)}), bf16[8,768,128]{2,1,0:T(8,128)(2,1)S(1)}, u32[]{:S(2)}, u32[]{:S(2)}) async-start(bf16[8,768,128]{2,1,0:T(8,128)(2,1)} %get-tuple-element.31), calls=%async_computation.2 | async-start | bytes 3145728 | tf_op jit(solution)/shard_map/all_to_all | solution.py:372
  201.5 13.0 %collective-permute-start.15 = (bf16[256,1024]{1,0:T(8,128)(2,1)S(1)}, bf16[256,1024]{1,0:T(8,128)(2,1)S(1)}, u32[]{:S(2)}, u32[]{:S(2)}) collective-permute-start(bf16[256,1024]{1,0:T(8,128)(2,1)S(1)} %constant_dynamic-update-slice_fusion.2.refs_0_), channel_id=1, source_target_pairs={{0,6},{1,7},{2,0},{3,1},{4,2},{5,3},{6,4},{7,5},{8,14},{9,15},{10,... | collective-permute-start | bytes 1572872 | tf_op jit(solution)/shard_map/ppermute | solution.py:440
  201.6 15.9 %collective-permute-start.14 = (bf16[256,1024]{1,0:T(8,128)(2,1)S(1)}, bf16[256,1024]{1,0:T(8,128)(2,1)S(1)}, u32[]{:S(2)}, u32[]{:S(2)}) collective-permute-start(bf16[256,1024]{1,0:T(8,128)(2,1)S(1)} %constant_dynamic-update-slice_fusion.2.refs_0_), channel_id=1, source_target_pairs={{0,2},{1,3},{2,4},{3,5},{4,6},{5,7},{6,0},{7,1},{8,10},{9,11},{10,... | collective-permute-start | bytes 1572872 | tf_op jit(solution)/shard_map/ppermute | solution.py:440
  203.1 24.5 %collective-permute-start.18 = (bf16[256,1024]{1,0:T(8,128)(2,1)S(1)}, bf16[256,1024]{1,0:T(8,128)(2,1)S(1)}, u32[]{:S(2)}, u32[]{:S(2)}) collective-permute-start(bf16[256,1024]{1,0:T(8,128)(2,1)S(1)} %constant_dynamic-update-slice_fusion.2.refs_0_), channel_id=1, source_target_pairs={{0,1},{1,0},{2,3},{3,2},{4,5},{5,4},{6,7},{7,6},{8,9},{9,8},{10,11... | collective-permute-start | bytes 1572872 | tf_op jit(solution)/shard_map/ppermute | solution.py:440
  214.5 6.5 %collective-permute-start.17 = (bf16[128,1024]{1,0:T(8,128)(2,1)S(1)}, bf16[128,1024]{1,0:T(8,128)(2,1)S(1)}, u32[]{:S(2)}, u32[]{:S(2)}) collective-permute-start(bf16[128,1024]{1,0:T(8,128)(2,1)S(1)} %slice.19), channel_id=1, source_target_pairs={{0,6},{1,7},{2,0},{3,1},{4,2},{5,3},{6,4},{7,5},{8,14},{9,15},{10,... | collective-permute-start | bytes 786440 | tf_op jit(solution)/shard_map/ppermute | solution.py:440
  215.5 12.1 %collective-permute-start.20 = (bf16[256,1024]{1,0:T(8,128)(2,1)S(1)}, bf16[256,1024]{1,0:T(8,128)(2,1)S(1)}, u32[]{:S(2)}, u32[]{:S(2)}) collective-permute-start(bf16[256,1024]{1,0:T(8,128)(2,1)S(1)} %collective-permute-done.15.refs_2_), channel_id=1, source_target_pairs={{0,1},{1,0},{2,3},{3,2},{4,5},{5,4},{6,7},{7,6},{8,9},{9,8},{10,11... | collective-permute-start | bytes 1572872 | tf_op jit(solution)/shard_map/ppermute | solution.py:440
  217.6 9.1 %collective-permute-start.16 = (bf16[128,1024]{1,0:T(8,128)(2,1)S(1)}, bf16[128,1024]{1,0:T(8,128)(2,1)S(1)}, u32[]{:S(2)}, u32[]{:S(2)}) collective-permute-start(bf16[128,1024]{1,0:T(8,128)(2,1)S(1)} %slice.18), channel_id=1, source_target_pairs={{0,2},{1,3},{2,4},{3,5},{4,6},{5,7},{6,0},{7,1},{8,10},{9,11},{10,... | collective-permute-start | bytes 786440 | tf_op jit(solution)/shard_map/ppermute | solution.py:440
  217.9 11.6 %collective-permute-start.19 = (bf16[256,1024]{1,0:T(8,128)(2,1)S(1)}, bf16[256,1024]{1,0:T(8,128)(2,1)}, u32[]{:S(2)}, u32[]{:S(2)}) collective-permute-start(bf16[256,1024]{1,0:T(8,128)(2,1)S(1)} %collective-permute-done.14.refs_1_), channel_id=1, source_target_pairs={{0,1},{1,0},{2,3},{3,2},{4,5},{5,4},{6,7},{7,6},{8,9},{9,8},{10,11... | collective-permute-start | bytes 1572872 | tf_op jit(solution)/shard_map/ppermute | solution.py:440
  221.1 6.5 %collective-permute-start.22 = (bf16[128,1024]{1,0:T(8,128)(2,1)S(1)}, bf16[128,1024]{1,0:T(8,128)(2,1)S(1)}, u32[]{:S(2)}, u32[]{:S(2)}) collective-permute-start(bf16[128,1024]{1,0:T(8,128)(2,1)S(1)} %collective-permute-done.17.refs_4_), channel_id=1, source_target_pairs={{0,1},{1,0},{2,3},{3,2},{4,5},{5,4},{6,7},{7,6},{8,9},{9,8},{10,11... | collective-permute-start | bytes 786440 | tf_op jit(solution)/shard_map/ppermute | solution.py:440
  238.3 25.9 %all-to-all-start.3 = ((bf16[8,768,128]{2,1,0:T(8,128)(2,1)}), bf16[8,768,128]{2,1,0:T(8,128)(2,1)S(1)}, u32[]{:S(2)}, u32[]{:S(2)}) async-start(bf16[8,768,128]{2,1,0:T(8,128)(2,1)} %get-tuple-element.32), calls=%async_computation.3 | async-start | bytes 3145728 | tf_op jit(solution)/shard_map/all_to_all | solution.py:374
  (20 other events, 209.5 us)

commit v3 on v2

--- a/solution.py
+++ b/solution.py
@@ -12,7 +12,10 @@
 LANES = 128
 
 
-def dispatch_body(ids_ref, tok_ref, gain_ref, out_ref, pos_ref, rows_ref, pos_smem, sem, *, experts, cap):
+def dispatch_body(
+    ids_ref, tok_ref, gain_ref, out0, out1, pos_ref, placed_ref, rows_ref, pos_smem, sem, out_sem, *, experts, cap
+):
+    half = cap // 2
     top, toks = ids_ref.shape
     width = tok_ref.shape[1]
     sub = width // LANES
@@ -27,10 +30,12 @@
     earlier = jnp.dot(total.astype(jnp.bfloat16), before, preferred_element_type=jnp.float32)
     for k in range(top):
         slot = jnp.sum(earlier * named[k], axis=0, keepdims=True)
-        pos_ref[k : k + 1, :] = ids_ref[k : k + 1, :] * cap + slot.astype(jnp.int32)
+        slot = slot.astype(jnp.int32)
+        late = (slot >= half).astype(jnp.int32)
+        pos_ref[k : k + 1, :] = ids_ref[k : k + 1, :] * half + slot + late * ((experts - 1) * half)
     copy = pltpu.make_async_copy(pos_ref, pos_smem, sem)
     copy.start()
-    out_ref[...] = jnp.zeros_like(out_ref)
+    placed_ref[...] = jnp.zeros_like(placed_ref)
     wide = tok_ref[...].astype(jnp.float32)
     mean_sq = jnp.mean(wide * wide, axis=-1, keepdims=True)
     normed = wide * lax.rsqrt(mean_sq + 1e-06) * gain_ref[...]
@@ -41,10 +46,19 @@
     def place(t, carry):
         one = rows_ref[pl.ds(pl.multiple_of(t * sub, sub), sub), :].astype(jnp.bfloat16)
         for k in range(top):
-            out_ref[pos_smem[k, t]] = one
+            placed_ref[pos_smem[k, t]] = one
         return carry
 
     lax.fori_loop(0, toks, place, 0, unroll=4)
+    chunk = experts * half
+    outs = [
+        pltpu.make_async_copy(placed_ref.at[pl.ds(i * chunk, chunk)], out, out_sem.at[i])
+        for i, out in enumerate((out0, out1))
+    ]
+    for c in outs:
+        c.start()
+    for c in outs:
+        c.wait()
 
 
 def dispatch(ids, tokens, gain, experts, cap):
@@ -55,18 +69,35 @@
         functools.partial(dispatch_body, experts=experts, cap=cap),
         name="dispatch",
         out_shape=(
-            jax.ShapeDtypeStruct((experts * cap, sub, LANES), jnp.bfloat16),
+            jax.ShapeDtypeStruct((experts * (cap // 2), sub, LANES), jnp.bfloat16),
+            jax.ShapeDtypeStruct((experts * (cap // 2), sub, LANES), jnp.bfloat16),
             jax.ShapeDtypeStruct((top, toks), jnp.int32),
         ),
+        out_specs=(
+            pl.BlockSpec(memory_space=pl.ANY),
+            pl.BlockSpec(memory_space=pl.ANY),
+            pl.BlockSpec(memory_space=pltpu.VMEM),
+        ),
         scratch_shapes=[
+            pltpu.VMEM((experts * cap, sub, LANES), jnp.bfloat16),
             pltpu.VMEM((toks * sub, LANES), jnp.float32),
             pltpu.SMEM((top, toks), jnp.int32),
             pltpu.SemaphoreType.DMA,
+            pltpu.SemaphoreType.DMA((2,)),
         ],
     )(ids, tokens, gain)
 
 
-def combine_body(pos_ref, gates_ref, rows_ref, out_ref, even_ref, odd_ref, acc_ref):
+def combine_body(pos_ref, gates_ref, rows0_hbm, rows1_hbm, out_ref, even_ref, odd_ref, acc_ref, rows_ref, sem):
+    half = rows0_hbm.shape[0]
+    loads = [
+        pltpu.make_async_copy(rows, rows_ref.at[pl.ds(i * half, half)], sem.at[i])
+        for i, rows in enumerate((rows0_hbm, rows1_hbm))
+    ]
+    for c in loads:
+        c.start()
+    for c in loads:
+        c.wait()
     top, toks = pos_ref.shape
     sub = rows_ref.shape[1]
 
@@ -87,7 +118,7 @@
 
 def combine(pos, gates, rows):
     _, toks = pos.shape
-    sub = rows.shape[1]
+    half, sub, _ = rows[0].shape
     widths = (sub * LANES, sub // 2 * LANES, sub // 2 * LANES)
     return pl.pallas_call(
         combine_body,
@@ -95,12 +126,16 @@
         grid_spec=pltpu.PrefetchScalarGridSpec(
             num_scalar_prefetch=2,
             grid=(1,),
-            in_specs=[pl.BlockSpec(rows.shape, lambda i, p, g: (0, 0, 0), pipeline_mode=pl.Buffered(1))],
+            in_specs=[pl.BlockSpec(memory_space=pl.ANY)] * 2,
             out_specs=tuple(pl.BlockSpec((toks, w), lambda i, p, g: (0, 0)) for w in widths),
-            scratch_shapes=[pltpu.VMEM((toks * sub, LANES), jnp.float32)],
+            scratch_shapes=[
+                pltpu.VMEM((toks * sub, LANES), jnp.float32),
+                pltpu.VMEM((2 * half, sub, LANES), jnp.bfloat16),
+                pltpu.SemaphoreType.DMA((2,)),
+            ],
         ),
         out_shape=tuple(jax.ShapeDtypeStruct((toks, w), jnp.bfloat16) for w in widths),
-    )(pos, gates, rows)
+    )(pos, gates, *rows)
 
 
 def expert_body(rows_hbm, gate0, up0, down0, gate1, up1, down1, out_hbm,
@@ -164,7 +199,7 @@
         c.wait()
 
 
-def expert(rows, gate0, up0, down0, gate1, up1, down1, step=128, tile=256, cols=256):
+def expert(rows, gate0, up0, down0, gate1, up1, down1, step=64, tile=256, cols=256):
     count, sub, _ = rows.shape
     hidden, width = down0.shape
     chunks = count // step
@@ -424,11 +459,11 @@
 ):
     tok_dev, model_width = tokens.shape
     top_count = expert_ids.shape[1]
-    devices = lax.axis_size("dp") * lax.axis_size("expert")
+    axes = ("dp", "pair", "core")
+    devices = lax.axis_size(axes)
     experts = devices // 2
     capacity = 2 * ((tok_dev * top_count * 7 + 12 * experts - 1) // (12 * experts))
     sub = model_width // LANES
-    axes = ("dp", "expert")
     index = lax.axis_index(axes)
 
     def move(array, y, x, core):
@@ -444,16 +479,13 @@
     other_up = move(jnp.swapaxes(up_proj[0], 0, 1), 0, 0, 1)
     other_down, cots = lax.optimization_barrier((move(down_proj[0], 0, 0, 1), cots))
 
-    placed, positions = dispatch(expert_ids.T, tokens, norm_gain.reshape(1, -1), experts, capacity)
-    received = lax.all_to_all(
-        placed.reshape(devices, capacity // 2, sub, LANES),
-        ("dp", "expert"),
-        split_axis=0,
-        concat_axis=0,
-        tiled=True,
-    )
-    expert_out = expert(
-        received.reshape(devices * capacity // 2, sub, LANES),
+    *placed, positions = dispatch(expert_ids.T, tokens, norm_gain.reshape(1, -1), experts, capacity)
+    chunks = [c.reshape(experts, capacity // 2, sub, LANES) for c in placed]
+
+    def exchange(rows):
+        return lax.all_to_all(rows, ("dp", "pair"), split_axis=0, concat_axis=0, tiled=True)
+
+    weights = (
         jnp.swapaxes(gate_proj[0], 0, 1),
         jnp.swapaxes(up_proj[0], 0, 1),
         down_proj[0],
@@ -461,14 +493,15 @@
         other_up,
         other_down,
     )
-    returned = lax.all_to_all(
-        expert_out.reshape(devices, capacity // 2, sub, LANES),
-        ("dp", "expert"),
-        split_axis=0,
-        concat_axis=0,
-        tiled=True,
-    )
-    layer_out, *parts = combine(positions, gate_weights.T, returned.reshape(experts * capacity, sub, LANES))
+
+    def run(rows):
+        out = expert(rows.reshape(experts * (capacity // 2), sub, LANES), *weights)
+        return out.reshape(experts, capacity // 2, sub, LANES)
+
+    sent = [exchange(chunks[c]) for c in range(2)]
+    done = [run(sent[c]) for c in range(2)]
+    back = [exchange(done[c]).reshape(-1, sub, LANES) for c in range(2)]
+    layer_out, *parts = combine(positions, gate_weights.T, back)
     feat_one, feat_two, grad_one, grad_two = project(
         parts, student_one, student_two, cots, move, (index // 8 % 2, index // 2 % 4, index % 2)
     )
@@ -476,28 +509,31 @@
 
 
 def solution(mesh):
+    batches, group = mesh.devices.shape
+    split = jax.sharding.Mesh(mesh.devices.reshape(batches, group // 2, 2), ("dp", "pair", "core"))
+    group, whole = ("pair", "core"), ("dp", "pair", "core")
     return jax.shard_map(
         local,
-        mesh=mesh,
+        mesh=split,
         in_specs=(
-            P(("dp", "expert"), None),
+            P(whole, None),
             P(),
-            P(("dp", "expert"), None),
-            P(("dp", "expert"), None),
-            P(("dp", "expert"), None, None),
-            P(("dp", "expert"), None, None),
-            P(("dp", "expert"), None, None),
-            P(None, "expert"),
-            P(None, "expert"),
-            P("dp", "expert"),
-            P("dp", "expert"),
+            P(whole, None),
+            P(whole, None),
+            P(whole, None, None),
+            P(whole, None, None),
+            P(whole, None, None),
+            P(None, group),
+            P(None, group),
+            P("dp", group),
+            P("dp", group),
         ),
         out_specs=(
-            P(("dp", "expert"), None),
-            P("dp", "expert"),
-            P("dp", "expert"),
-            P("dp", "expert"),
-            P("dp", "expert"),
+            P(whole, None),
+            P("dp", group),
+            P("dp", group),
+            P("dp", group),
+            P("dp", group),
         ),
         check_vma=False,
     )

time: 269 us -> 271 us (level)
  starting transfers between devices: 49.2 us -> 71.6 us
  blocking collectives: 52.9 us -> 32 us
  waiting for transfers between devices: 78.3 us -> 66.3 us
  Pallas kernels: 75.1 us -> 83.6 us
    all_to_all x1, blocking collectives: 52.9 us -> 32 us  [exchange(): lax.all_to_all(rows, ('dp', 'pair'), split_axis=0, concat_axis=0, tiled=T...]
    all_to_all x1 -> x3, starting transfers between devices: 11.9 us -> 28.7 us  [exchange(): lax.all_to_all(rows, ('dp', 'pair'), split_axis=0, concat_axis=0, tiled=T...]
    ppermute x23, waiting for transfers between devices: 40.1 us -> 29.5 us  [move(): return lax.ppermute(array, axes, [(d, target(d)) for d in range(devices)])]
    pallas_call x1 -> x2, Pallas kernels: 29.1 us -> 36.7 us  [expert(): pl.pallas_call(functools.partial(expert_body, step=step, tile=tile, cols=...]
    ppermute x23, starting transfers between devices: 28.5 us -> 32.3 us  [move(): return lax.ppermute(array, axes, [(d, target(d)) for d in range(devices)])]
    unnamed x40 -> x42, local copies, waits for them, and re-layouts: 8.97 us -> 10.8 us
    all_to_all x1 -> x3, waiting for transfers between devices: 32 us -> 30.3 us  [exchange(): lax.all_to_all(rows, ('dp', 'pair'), split_axis=0, concat_axis=0, tiled=T...]
  transfers between devices with their start and end apart: 26 -> 28, of which waited for: 12 -> 10; matrix products, arithmetic and copies ran while one was open for 3% -> 4% of each run, Pallas kernels for 12% -> 25%
where the time goes in v3:
time: 271 us; the launch traced here: 270 us
  Pallas kernels  83.6 us (31%)
  starting transfers between devices  71.6 us (26%)
  waiting for transfers between devices  66.3 us (24%)
  blocking collectives  32 us (12%)
  local copies, waits for them, and re-layouts  11.5 us (4%)
  other arithmetic  3.89 us (1%)
    pallas_call x2, Pallas kernels, expert(): pl.pallas_call(functools.partial(expert_body, step=step, tile=tile, cols=...  36.7 us
    ppermute x23, starting transfers between devices, move(): return lax.ppermute(array, axes, [(d, target(d)) for d in range(devices)])  32.3 us
    all_to_all x1, blocking collectives, exchange(): lax.all_to_all(rows, ('dp', 'pair'), split_axis=0, concat_axis=0, tiled=T...  32 us
    all_to_all x3, waiting for transfers between devices, exchange(): lax.all_to_all(rows, ('dp', 'pair'), split_axis=0, concat_axis=0, tiled=T...  30.3 us
    ppermute x23, waiting for transfers between devices, move(): return lax.ppermute(array, axes, [(d, target(d)) for d in range(devices)])  29.5 us
    all_to_all x3, starting transfers between devices, exchange(): lax.all_to_all(rows, ('dp', 'pair'), split_axis=0, concat_axis=0, tiled=T...  28.7 us
    pallas_call x2, Pallas kernels, terms(): pl.pallas_call(functools.partial(terms_body, pieces=len(pieces), scale=1....  17.5 us
    pallas_call x1, Pallas kernels, project(): pl.pallas_call(features_body, name='features', in_specs=[anywhere] * 4, o...  12.2 us
  transfers between devices with their start and end apart: 28, of which 10 were waited for; matrix products, arithmetic and copies ran while one was open for 4% of the time, Pallas kernels for 25%

profile of v3, /device:TPU:1, one launch (start us, length us, event | category | flops | bytes accessed | tf_op | source)
XLA Modules:
  0.0 269.9 jit_solution(9942286341178932397)
XLA Ops:
  0.6 6.5 %dispatch.1 = (bf16[448,16,128]{2,1,0:T(8,128)(2,1)}, bf16[448,16,128]{2,1,0:T(8,128)(2,1)}, s32[6,128]{1,0:T(8,128)}) custom-call(s32[6,128]{1,0:T(8,128)} %bitcast.54, bf16[128,2048]{1,0:T(8,128)(2,1)} %tok_ref.1, f32[1,2048]{1,0:T(1,128)} %bitcast.53), custom_call_target="tpu_custom_call" | custom-call | tf_op jit(solution)/shard_map/dispatch/pallas_call | solution.py:68
  7.2 12.2 %all-to-all-start = ((bf16[64,7,16,128]{3,2,1,0:T(8,128)(2,1)}), bf16[64,7,16,128]{3,2,1,0:T(8,128)(2,1)}, u32[]{:S(2)}, u32[]{:S(2)}) async-start(bf16[64,7,16,128]{3,2,1,0:T(8,128)(2,1)} %bitcast.52), calls=%async_computation | async-start | bytes 3670016 | tf_op jit(solution)/shard_map/all_to_all | solution.py:486
  20.9 23.7 %all-to-all-done = bf16[64,7,16,128]{3,2,1,0:T(8,128)(2,1)} async-done(((bf16[64,7,16,128]{3,2,1,0:T(8,128)(2,1)}), bf16[64,7,16,128]{3,2,1,0:T(8,128)(2,1)}, u32[]{:S(2)}, u32[]{:S(2)}) %all-to-all-start) | async-done | bytes 1835040 | tf_op jit(solution)/shard_map/all_to_all | solution.py:486
  44.6 6.8 %all-to-all-start.2 = ((bf16[64,7,16,128]{3,2,1,0:T(8,128)(2,1)}), bf16[64,7,16,128]{3,2,1,0:T(8,128)(2,1)}, u32[]{:S(2)}, u32[]{:S(2)}) async-start(bf16[64,7,16,128]{3,2,1,0:T(8,128)(2,1)} %bitcast.51), calls=%async_computation.2 | async-start | bytes 3670016 | tf_op jit(solution)/shard_map/all_to_all | solution.py:486
  53.7 3.9 %copy.17 = bf16[2048,512]{0,1:T(8,128)(2,1)} copy(bf16[2048,512]{1,0:T(8,128)(2,1)} %param.21) | data formatting | bytes 4194304 | tf_op args[10]
  57.6 3.9 %maximum_bitcast_fusion.refs_10_ = bf16[768,2048]{1,0:T(8,128)(2,1)} fusion(bf16[2048,512]{0,1:T(8,128)(2,1)} %copy.17, bf16[2048,256]{0,1:T(8,128)(2,1)} %copy.16), kind=kLoop, calls=%fused_computation | loop fusion | flops 6291456 | bytes 6291456 | tf_op jit(solution)/shard_map/transpose | solution.py:477
  61.5 18.3 %expert.2 = bf16[448,16,128]{2,1,0:T(8,128)(2,1)} custom-call(bf16[448,16,128]{2,1,0:T(8,128)(2,1)} %bitcast.4.rows_hbm, bf16[704,2048]{1,0:T(8,128)(2,1)} %bitcast.38, bf16[704,2048]{1,0:T(8,128)(2,1)} %bitcast.42, bf16[704,2048]{1,0:T(8,128)(2,1)} %bitcast.45, bf16[704,2048]{1,0:T(8,128)(2,1)} %collective-permute-done.gate1, ...), custom_call_target="tpu_custom_call" | custom-call | tf_op jit(solution)/shard_map/expert/pallas_call | solution.py:207
  79.8 9.7 %all-to-all-start.1 = ((bf16[64,7,16,128]{3,2,1,0:T(8,128)(2,1)}), bf16[64,7,16,128]{3,2,1,0:T(8,128)(2,1)S(1)}, u32[]{:S(2)}, u32[]{:S(2)}) async-start(bf16[64,7,16,128]{3,2,1,0:T(8,128)(2,1)} %bitcast.47), calls=%async_computation.1 | async-start | bytes 3670016 | tf_op jit(solution)/shard_map/all_to_all | solution.py:486
  89.5 18.4 %expert.3 = bf16[448,16,128]{2,1,0:T(8,128)(2,1)} custom-call(bf16[448,16,128]{2,1,0:T(8,128)(2,1)} %bitcast.16.rows_hbm, bf16[704,2048]{1,0:T(8,128)(2,1)} %bitcast.39, bf16[704,2048]{1,0:T(8,128)(2,1)} %bitcast.43, bf16[704,2048]{1,0:T(8,128)(2,1)} %bitcast.46, bf16[704,2048]{1,0:T(8,128)(2,1)} %collective-permute-done.gate1, ...), custom_call_target="tpu_custom_call" | custom-call | tf_op jit(solution)/shard_map/expert/pallas_call | solution.py:207
  107.9 6.7 %all-to-all-done.1 = bf16[64,7,16,128]{3,2,1,0:T(8,128)(2,1)S(1)} async-done(((bf16[64,7,16,128]{3,2,1,0:T(8,128)(2,1)}), bf16[64,7,16,128]{3,2,1,0:T(8,128)(2,1)S(1)}, u32[]{:S(2)}, u32[]{:S(2)}) %all-to-all-start.1) | async-done | bytes 1835040 | tf_op jit(solution)/shard_map/all_to_all | solution.py:486
  114.6 32.0 %all_to_all.30 = bf16[64,7,16,128]{3,2,1,0:T(8,128)(2,1)} all-to-all(bf16[64,7,16,128]{3,2,1,0:T(8,128)(2,1)} %bitcast.48), channel_id=1, replica_groups=mesh['dp'=8,'pair'=8,'core'=2] {'dp','pair'}, dimensions={0} | all-to-all | bytes 3670016 | tf_op jit(solution)/shard_map/all_to_all | solution.py:486
  146.6 5.7 %combine.1 = (bf16[128,2048]{1,0:T(8,128)(2,1)}, bf16[128,1024]{1,0:T(8,128)(2,1)}, bf16[128,1024]{1,0:T(8,128)(2,1)}) custom-call(s32[6,128]{1,0:T(8,128)} %get-tuple-element.21.pos_ref, f32[6,128]{1,0:T(8,128)} %bitcast.55, bf16[448,16,128]{2,1,0:T(8,128)(2,1)} %bitcast.49, bf16[448,16,128]{2,1,0:T(8,128)(2,1)} %bitcast.50), custom_call_target="tpu_custom_call" | custom-call | tf_op jit(solution)/shard_map/combine/pallas_call | solution.py:123
  154.7 4.6 %collective-permute-done.3 = bf16[128,1024]{1,0:T(8,128)(2,1)S(1)} collective-permute-done((bf16[128,1024]{1,0:T(8,128)(2,1)}, bf16[128,1024]{1,0:T(8,128)(2,1)S(1)}, u32[]{:S(2)}, u32[]{:S(2)}) %collective-permute-start.3) | collective-permute-done | bytes 262176 | tf_op jit(solution)/shard_map/ppermute | solution.py:475
  160.9 4.5 %collective-permute-start.8 = (bf16[256,1024]{1,0:T(8,128)(2,1)S(1)}, bf16[256,1024]{1,0:T(8,128)(2,1)S(1)}, u32[]{:S(2)}, u32[]{:S(2)}) collective-permute-start(bf16[256,1024]{1,0:T(8,128)(2,1)S(1)} %constant_dynamic-update-slice_fusion.refs_0_), channel_id=1, source_target_pairs={{0,1},{1,0},{2,3},{3,2},{4,5},{5,4},{6,7},{7,6},{8,9},{9,8},{10,11... | collective-permute-start | bytes 1572872 | tf_op jit(solution)/shard_map/ppermute | solution.py:475
  171.2 5.3 %collective-permute-start.10 = (bf16[256,1024]{1,0:T(8,128)(2,1)S(1)}, bf16[256,1024]{1,0:T(8,128)(2,1)}, u32[]{:S(2)}, u32[]{:S(2)}) collective-permute-start(bf16[256,1024]{1,0:T(8,128)(2,1)S(1)} %collective-permute-done.5.refs_2_), channel_id=1, source_target_pairs={{0,1},{1,0},{2,3},{3,2},{4,5},{5,4},{6,7},{7,6},{8,9},{9,8},{10,11... | collective-permute-start | bytes 1572872 | tf_op jit(solution)/shard_map/ppermute | solution.py:475
  176.7 4.1 %collective-permute-start.12 = (bf16[128,1024]{1,0:T(8,128)(2,1)S(1)}, bf16[128,1024]{1,0:T(8,128)(2,1)}, u32[]{:S(2)}, u32[]{:S(2)}) collective-permute-start(bf16[128,1024]{1,0:T(8,128)(2,1)S(1)} %collective-permute-done.7.refs_4_), channel_id=1, source_target_pairs={{0,1},{1,0},{2,3},{3,2},{4,5},{5,4},{6,7},{7,6},{8,9},{9,8},{10,11... | collective-permute-start | bytes 786440 | tf_op jit(solution)/shard_map/ppermute | solution.py:475
  180.8 4.6 %collective-permute-done.6.refs_3_ = bf16[128,1024]{1,0:T(8,128)(2,1)} collective-permute-done((bf16[128,1024]{1,0:T(8,128)(2,1)S(1)}, bf16[128,1024]{1,0:T(8,128)(2,1)}, u32[]{:S(2)}, u32[]{:S(2)}) %collective-permute-start.6) | collective-permute-done | bytes 262176 | tf_op jit(solution)/shard_map/ppermute | solution.py:475
  188.3 8.7 %terms.2 = (bf16[8,768,128]{2,1,0:T(8,128)(2,1)}, bf16[2048,1024]{1,0:T(8,128)(2,1)}) custom-call(s32[20]{0:T(128)} %stack.67.at_ref, bf16[256,1024]{1,0:T(8,128)(2,1)} %copy-done.10, bf16[256,1024]{1,0:T(8,128)(2,1)} %copy-done.6, bf16[256,1024]{1,0:T(8,128)(2,1)} %copy-done.5, bf16[128,1024]{1,0:T(8,128)(2,1)} %collective-permute-done.6.refs_3_, ...), custom_call_target="tpu_custom_call" | custom-call | flops 3221225472 | bytes 12582912 | tf_op jit(solution)/shard_map/terms/pallas_call | solution.py:377
  197.0 5.5 %all-to-all-start.4 = ((bf16[8,768,128]{2,1,0:T(8,128)(2,1)}), bf16[8,768,128]{2,1,0:T(8,128)(2,1)S(1)}, u32[]{:S(2)}, u32[]{:S(2)}) async-start(bf16[8,768,128]{2,1,0:T(8,128)(2,1)} %get-tuple-element.33), calls=%async_computation.4 | async-start | bytes 3145728 | tf_op jit(solution)/shard_map/all_to_all | solution.py:407
  205.2 10.3 %collective-permute-done.15.refs_2_ = bf16[256,1024]{1,0:T(8,128)(2,1)S(1)} collective-permute-done((bf16[256,1024]{1,0:T(8,128)(2,1)S(1)}, bf16[256,1024]{1,0:T(8,128)(2,1)S(1)}, u32[]{:S(2)}, u32[]{:S(2)}) %collective-permute-start.15) | collective-permute-done | bytes 524320 | tf_op jit(solution)/shard_map/ppermute | solution.py:475
  231.1 8.8 %terms.3 = (bf16[8,768,128]{2,1,0:T(8,128)(2,1)}, bf16[2048,1024]{1,0:T(8,128)(2,1)}) custom-call(s32[20]{0:T(128)} %stack.67.at_ref, bf16[256,1024]{1,0:T(8,128)(2,1)} %copy-done.9, bf16[256,1024]{1,0:T(8,128)(2,1)} %copy-done.8, bf16[256,1024]{1,0:T(8,128)(2,1)} %copy-done.7, bf16[128,1024]{1,0:T(8,128)(2,1)} %copy-done.17, bf16[128,1024]{1,0:T(8,128)(2,1)} %copy-done.16, ...), custom_call_target="tpu_custom_call" | custom-call | flops 3221225472 | bytes 12582912 | tf_op jit(solution)/shard_map/terms/pallas_call | solution.py:377
  239.9 5.1 %all-to-all-start.5 = ((bf16[8,768,128]{2,1,0:T(8,128)(2,1)}), bf16[8,768,128]{2,1,0:T(8,128)(2,1)S(1)}, u32[]{:S(2)}, u32[]{:S(2)}) async-start(bf16[8,768,128]{2,1,0:T(8,128)(2,1)} %get-tuple-element.34), calls=%async_computation.5 | async-start | bytes 3145728 | tf_op jit(solution)/shard_map/all_to_all | solution.py:409
  245.0 12.2 %features.1 = (bf16[2048,256]{1,0:T(8,128)(2,1)}, bf16[2048,512]{1,0:T(8,128)(2,1)}) custom-call(bf16[2048,1024]{1,0:T(8,128)(2,1)} %get-tuple-element.28.rows0, bf16[2048,1024]{1,0:T(8,128)(2,1)} %get-tuple-element.30.rows1, bf16[8,2,128,256]{3,2,1,0:T(8,128)(2,1)} %bitcast.57, bf16[8,2,128,512]{3,2,1,0:T(8,128)(2,1)} %bitcast.56), custom_call_target="tpu_custom_call" | custom-call | flops 6442450944 | bytes 14680064 | tf_op jit(solution)/shard_map/features/pallas_call | solution.py:411
  259.6 6.5 %all-to-all-done.5.pieces_ref = bf16[8,768,128]{2,1,0:T(8,128)(2,1)S(1)} async-done(((bf16[8,768,128]{2,1,0:T(8,128)(2,1)}), bf16[8,768,128]{2,1,0:T(8,128)(2,1)S(1)}, u32[]{:S(2)}, u32[]{:S(2)}) %all-to-all-start.5) | async-done | bytes 1572896 | tf_op jit(solution)/shard_map/all_to_all | solution.py:409
  (92 shorter events, 40.9 us)
Async XLA Ops:
  7.2 37.4 %all-to-all-start = ((bf16[64,7,16,128]{3,2,1,0:T(8,128)(2,1)}), bf16[64,7,16,128]{3,2,1,0:T(8,128)(2,1)}, u32[]{:S(2)}, u32[]{:S(2)}) async-start(bf16[64,7,16,128]{3,2,1,0:T(8,128)(2,1)} %bitcast.52), calls=%async_computation | async-start | bytes 3670016 | tf_op jit(solution)/shard_map/all_to_all | solution.py:486
  19.4 42.1 %collective-permute-start.2 = (bf16[704,2048]{1,0:T(8,128)(2,1)}, bf16[704,2048]{1,0:T(8,128)(2,1)}, u32[]{:S(2)}, u32[]{:S(2)}) collective-permute-start(bf16[704,2048]{1,0:T(8,128)(2,1)} %bitcast.44), channel_id=1, source_target_pairs={{0,1},{1,0},{2,3},{3,2},{4,5},{5,4},{6,7},{7,6},{8,9},{9,8},{10,11... | collective-permute-start | bytes 8650760 | tf_op jit(solution)/shard_map/ppermute | solution.py:475
  20.4 41.1 %collective-permute-start = (bf16[704,2048]{1,0:T(8,128)(2,1)S(1)}, bf16[704,2048]{1,0:T(8,128)(2,1)}, u32[]{:S(2)}, u32[]{:S(2)}) collective-permute-start(bf16[704,2048]{1,0:T(8,128)(2,1)S(1)} %bitcast.40), channel_id=1, source_target_pairs={{0,1},{1,0},{2,3},{3,2},{4,5},{5,4},{6,7},{7,6},{8,9},{9,8},{10,11... | collective-permute-start | bytes 8650760 | tf_op jit(solution)/shard_map/ppermute | solution.py:475
  20.5 41.0 %collective-permute-start.1 = (bf16[704,2048]{1,0:T(8,128)(2,1)}, bf16[704,2048]{1,0:T(8,128)(2,1)}, u32[]{:S(2)}, u32[]{:S(2)}) collective-permute-start(bf16[704,2048]{1,0:T(8,128)(2,1)} %bitcast.41), channel_id=1, source_target_pairs={{0,1},{1,0},{2,3},{3,2},{4,5},{5,4},{6,7},{7,6},{8,9},{9,8},{10,11... | collective-permute-start | bytes 8650760 | tf_op jit(solution)/shard_map/ppermute | solution.py:475
  44.6 35.2 %all-to-all-start.2 = ((bf16[64,7,16,128]{3,2,1,0:T(8,128)(2,1)}), bf16[64,7,16,128]{3,2,1,0:T(8,128)(2,1)}, u32[]{:S(2)}, u32[]{:S(2)}) async-start(bf16[64,7,16,128]{3,2,1,0:T(8,128)(2,1)} %bitcast.51), calls=%async_computation.2 | async-start | bytes 3670016 | tf_op jit(solution)/shard_map/all_to_all | solution.py:486
  79.8 34.8 %all-to-all-start.1 = ((bf16[64,7,16,128]{3,2,1,0:T(8,128)(2,1)}), bf16[64,7,16,128]{3,2,1,0:T(8,128)(2,1)S(1)}, u32[]{:S(2)}, u32[]{:S(2)}) async-start(bf16[64,7,16,128]{3,2,1,0:T(8,128)(2,1)} %bitcast.47), calls=%async_computation.1 | async-start | bytes 3670016 | tf_op jit(solution)/shard_map/all_to_all | solution.py:486
  159.3 9.6 %collective-permute-start.5 = (bf16[256,1024]{1,0:T(8,128)(2,1)S(1)}, bf16[256,1024]{1,0:T(8,128)(2,1)S(1)}, u32[]{:S(2)}, u32[]{:S(2)}) collective-permute-start(bf16[256,1024]{1,0:T(8,128)(2,1)S(1)} %constant_dynamic-update-slice_fusion.refs_0_), channel_id=1, source_target_pairs={{0,6},{1,7},{2,0},{3,1},{4,2},{5,3},{6,4},{7,5},{8,14},{9,15},{10,... | collective-permute-start | bytes 1572872 | tf_op jit(solution)/shard_map/ppermute | solution.py:475
  160.3 16.2 %collective-permute-start.4 = (bf16[256,1024]{1,0:T(8,128)(2,1)S(1)}, bf16[256,1024]{1,0:T(8,128)(2,1)S(1)}, u32[]{:S(2)}, u32[]{:S(2)}) collective-permute-start(bf16[256,1024]{1,0:T(8,128)(2,1)S(1)} %constant_dynamic-update-slice_fusion.refs_0_), channel_id=1, source_target_pairs={{0,2},{1,3},{2,4},{3,5},{4,6},{5,7},{6,0},{7,1},{8,10},{9,11},{10,... | collective-permute-start | bytes 1572872 | tf_op jit(solution)/shard_map/ppermute | solution.py:475
  160.9 26.6 %collective-permute-start.8 = (bf16[256,1024]{1,0:T(8,128)(2,1)S(1)}, bf16[256,1024]{1,0:T(8,128)(2,1)S(1)}, u32[]{:S(2)}, u32[]{:S(2)}) collective-permute-start(bf16[256,1024]{1,0:T(8,128)(2,1)S(1)} %constant_dynamic-update-slice_fusion.refs_0_), channel_id=1, source_target_pairs={{0,1},{1,0},{2,3},{3,2},{4,5},{5,4},{6,7},{7,6},{8,9},{9,8},{10,11... | collective-permute-start | bytes 1572872 | tf_op jit(solution)/shard_map/ppermute | solution.py:475
  168.9 7.8 %collective-permute-start.7 = (bf16[128,1024]{1,0:T(8,128)(2,1)S(1)}, bf16[128,1024]{1,0:T(8,128)(2,1)S(1)}, u32[]{:S(2)}, u32[]{:S(2)}) collective-permute-start(bf16[128,1024]{1,0:T(8,128)(2,1)S(1)} %slice.17), channel_id=1, source_target_pairs={{0,6},{1,7},{2,0},{3,1},{4,2},{5,3},{6,4},{7,5},{8,14},{9,15},{10,... | collective-permute-start | bytes 786440 | tf_op jit(solution)/shard_map/ppermute | solution.py:475
  171.2 16.8 %collective-permute-start.10 = (bf16[256,1024]{1,0:T(8,128)(2,1)S(1)}, bf16[256,1024]{1,0:T(8,128)(2,1)}, u32[]{:S(2)}, u32[]{:S(2)}) collective-permute-start(bf16[256,1024]{1,0:T(8,128)(2,1)S(1)} %collective-permute-done.5.refs_2_), channel_id=1, source_target_pairs={{0,1},{1,0},{2,3},{3,2},{4,5},{5,4},{6,7},{7,6},{8,9},{9,8},{10,11... | collective-permute-start | bytes 1572872 | tf_op jit(solution)/shard_map/ppermute | solution.py:475
  176.5 11.4 %collective-permute-start.9 = (bf16[256,1024]{1,0:T(8,128)(2,1)S(1)}, bf16[256,1024]{1,0:T(8,128)(2,1)}, u32[]{:S(2)}, u32[]{:S(2)}) collective-permute-start(bf16[256,1024]{1,0:T(8,128)(2,1)S(1)} %collective-permute-done.4.refs_1_), channel_id=1, source_target_pairs={{0,1},{1,0},{2,3},{3,2},{4,5},{5,4},{6,7},{7,6},{8,9},{9,8},{10,11... | collective-permute-start | bytes 1572872 | tf_op jit(solution)/shard_map/ppermute | solution.py:475
  176.6 8.8 %collective-permute-start.6 = (bf16[128,1024]{1,0:T(8,128)(2,1)S(1)}, bf16[128,1024]{1,0:T(8,128)(2,1)}, u32[]{:S(2)}, u32[]{:S(2)}) collective-permute-start(bf16[128,1024]{1,0:T(8,128)(2,1)S(1)} %slice.16), channel_id=1, source_target_pairs={{0,2},{1,3},{2,4},{3,5},{4,6},{5,7},{6,0},{7,1},{8,10},{9,11},{10,... | collective-permute-start | bytes 786440 | tf_op jit(solution)/shard_map/ppermute | solution.py:475
  176.7 11.2 %collective-permute-start.12 = (bf16[128,1024]{1,0:T(8,128)(2,1)S(1)}, bf16[128,1024]{1,0:T(8,128)(2,1)}, u32[]{:S(2)}, u32[]{:S(2)}) collective-permute-start(bf16[128,1024]{1,0:T(8,128)(2,1)S(1)} %collective-permute-done.7.refs_4_), channel_id=1, source_target_pairs={{0,1},{1,0},{2,3},{3,2},{4,5},{5,4},{6,7},{7,6},{8,9},{9,8},{10,11... | collective-permute-start | bytes 786440 | tf_op jit(solution)/shard_map/ppermute | solution.py:475
  187.5 15.0 %collective-permute-start.13 = (bf16[128,1024]{1,0:T(8,128)(2,1)S(1)}, bf16[128,1024]{1,0:T(8,128)(2,1)S(1)}, u32[]{:S(2)}, u32[]{:S(2)}) collective-permute-start(bf16[128,1024]{1,0:T(8,128)(2,1)S(1)} %copy-done.4), channel_id=1, source_target_pairs={{0,8},{1,9},{2,10},{3,11},{4,12},{5,13},{6,14},{7,15},{8,0},{9,1},... | collective-permute-start | bytes 786440 | tf_op jit(solution)/shard_map/ppermute | solution.py:475
  197.0 42.8 %all-to-all-start.4 = ((bf16[8,768,128]{2,1,0:T(8,128)(2,1)}), bf16[8,768,128]{2,1,0:T(8,128)(2,1)S(1)}, u32[]{:S(2)}, u32[]{:S(2)}) async-start(bf16[8,768,128]{2,1,0:T(8,128)(2,1)} %get-tuple-element.33), calls=%async_computation.4 | async-start | bytes 3145728 | tf_op jit(solution)/shard_map/all_to_all | solution.py:407
  202.5 13.0 %collective-permute-start.15 = (bf16[256,1024]{1,0:T(8,128)(2,1)S(1)}, bf16[256,1024]{1,0:T(8,128)(2,1)S(1)}, u32[]{:S(2)}, u32[]{:S(2)}) collective-permute-start(bf16[256,1024]{1,0:T(8,128)(2,1)S(1)} %constant_dynamic-update-slice_fusion.2.refs_0_), channel_id=1, source_target_pairs={{0,6},{1,7},{2,0},{3,1},{4,2},{5,3},{6,4},{7,5},{8,14},{9,15},{10,... | collective-permute-start | bytes 1572872 | tf_op jit(solution)/shard_map/ppermute | solution.py:475
  202.6 15.9 %collective-permute-start.14 = (bf16[256,1024]{1,0:T(8,128)(2,1)S(1)}, bf16[256,1024]{1,0:T(8,128)(2,1)S(1)}, u32[]{:S(2)}, u32[]{:S(2)}) collective-permute-start(bf16[256,1024]{1,0:T(8,128)(2,1)S(1)} %constant_dynamic-update-slice_fusion.2.refs_0_), channel_id=1, source_target_pairs={{0,2},{1,3},{2,4},{3,5},{4,6},{5,7},{6,0},{7,1},{8,10},{9,11},{10,... | collective-permute-start | bytes 1572872 | tf_op jit(solution)/shard_map/ppermute | solution.py:475
  204.1 24.6 %collective-permute-start.18 = (bf16[256,1024]{1,0:T(8,128)(2,1)S(1)}, bf16[256,1024]{1,0:T(8,128)(2,1)S(1)}, u32[]{:S(2)}, u32[]{:S(2)}) collective-permute-start(bf16[256,1024]{1,0:T(8,128)(2,1)S(1)} %constant_dynamic-update-slice_fusion.2.refs_0_), channel_id=1, source_target_pairs={{0,1},{1,0},{2,3},{3,2},{4,5},{5,4},{6,7},{7,6},{8,9},{9,8},{10,11... | collective-permute-start | bytes 1572872 | tf_op jit(solution)/shard_map/ppermute | solution.py:475
  217.1 11.5 %collective-permute-start.20 = (bf16[256,1024]{1,0:T(8,128)(2,1)S(1)}, bf16[256,1024]{1,0:T(8,128)(2,1)S(1)}, u32[]{:S(2)}, u32[]{:S(2)}) collective-permute-start(bf16[256,1024]{1,0:T(8,128)(2,1)S(1)} %collective-permute-done.15.refs_2_), channel_id=1, source_target_pairs={{0,1},{1,0},{2,3},{3,2},{4,5},{5,4},{6,7},{7,6},{8,9},{9,8},{10,11... | collective-permute-start | bytes 1572872 | tf_op jit(solution)/shard_map/ppermute | solution.py:475
  218.5 10.1 %collective-permute-start.19 = (bf16[256,1024]{1,0:T(8,128)(2,1)S(1)}, bf16[256,1024]{1,0:T(8,128)(2,1)S(1)}, u32[]{:S(2)}, u32[]{:S(2)}) collective-permute-start(bf16[256,1024]{1,0:T(8,128)(2,1)S(1)} %collective-permute-done.14.refs_1_), channel_id=1, source_target_pairs={{0,1},{1,0},{2,3},{3,2},{4,5},{5,4},{6,7},{7,6},{8,9},{9,8},{10,11... | collective-permute-start | bytes 1572872 | tf_op jit(solution)/shard_map/ppermute | solution.py:475
  218.6 8.7 %collective-permute-start.16 = (bf16[128,1024]{1,0:T(8,128)(2,1)S(1)}, bf16[128,1024]{1,0:T(8,128)(2,1)S(1)}, u32[]{:S(2)}, u32[]{:S(2)}) collective-permute-start(bf16[128,1024]{1,0:T(8,128)(2,1)S(1)} %slice.18), channel_id=1, source_target_pairs={{0,2},{1,3},{2,4},{3,5},{4,6},{5,7},{6,0},{7,1},{8,10},{9,11},{10,... | collective-permute-start | bytes 786440 | tf_op jit(solution)/shard_map/ppermute | solution.py:475
  222.1 7.4 %collective-permute-start.22 = (bf16[128,1024]{1,0:T(8,128)(2,1)S(1)}, bf16[128,1024]{1,0:T(8,128)(2,1)S(1)}, u32[]{:S(2)}, u32[]{:S(2)}) collective-permute-start(bf16[128,1024]{1,0:T(8,128)(2,1)S(1)} %collective-permute-done.17.refs_4_), channel_id=1, source_target_pairs={{0,1},{1,0},{2,3},{3,2},{4,5},{5,4},{6,7},{7,6},{8,9},{9,8},{10,11... | collective-permute-start | bytes 786440 | tf_op jit(solution)/shard_map/ppermute | solution.py:475
  239.9 26.3 %all-to-all-start.5 = ((bf16[8,768,128]{2,1,0:T(8,128)(2,1)}), bf16[8,768,128]{2,1,0:T(8,128)(2,1)S(1)}, u32[]{:S(2)}, u32[]{:S(2)}) async-start(bf16[8,768,128]{2,1,0:T(8,128)(2,1)} %get-tuple-element.34), calls=%async_computation.5 | async-start | bytes 3145728 | tf_op jit(solution)/shard_map/all_to_all | solution.py:409
  (23 other events, 270.1 us)

commit v4 on v2

--- a/solution.py
+++ b/solution.py
@@ -137,7 +137,7 @@
             n = min(tile, hidden - lo)
             gate_val = lax.dot_general(x_ref[...], gate_ref[h, pl.ds(lo, n), :], contract, preferred_element_type=jnp.float32)
             up_val = lax.dot_general(x_ref[...], up_ref[h, pl.ds(lo, n), :], contract, preferred_element_type=jnp.float32)
-            hid_ref[h, :, lo : lo + n] = (gate_val / (1.0 + jnp.exp(-gate_val)) * up_val).astype(jnp.bfloat16)
+            hid_ref[h, :, lo : lo + n] = (0.5 * gate_val * (1.0 + jnp.tanh(0.5 * gate_val)) * up_val).astype(jnp.bfloat16)
     for c in downs:
         c.wait()
 
@@ -194,16 +194,13 @@
 VMEM_LIMIT = 60 * 1024 * 1024
 
 
-def terms_body(at_ref, *refs, pieces, scale):
+def terms_body(at_ref, *refs, pieces, blocks, scale):
     parts = refs[:pieces]
     cot_hbm, out_hbm, all_rows, rows_ref, cot_ref, cut_ref, sem, side_sem, out_sem = refs[pieces:]
-    count = rows_ref.shape[0]
-    block = count // (2 * pieces - 4)
     loads = []
-    for i, piece in enumerate(parts):
-        for k in range(piece.shape[0] // block):
-            to = pl.ds(pl.multiple_of(at_ref[2 * i + k], block), block)
-            loads.append(pltpu.make_async_copy(piece.at[pl.ds(k * block, block)], rows_ref.at[to], sem.at[2 * i + k]))
+    for i, (piece, start, size) in enumerate(blocks):
+        to = pl.ds(pl.multiple_of(at_ref[i], size), size)
+        loads.append(pltpu.make_async_copy(parts[piece].at[pl.ds(start, size)], rows_ref.at[to], sem.at[i]))
     cot_load = pltpu.make_async_copy(cot_hbm, cot_ref, side_sem.at[0])
     cot_load.start()
     for c in loads:
@@ -315,32 +312,46 @@
     bf16, f32 = jnp.bfloat16, jnp.float32
     dma = pltpu.SemaphoreType.DMA
     anywhere = pl.BlockSpec(memory_space=pl.ANY)
+    inside = pl.BlockSpec(memory_space=pltpu.VMEM)
 
     def row_of(y, at, c):
         return (y * ring + at % ring) * (2 * rows) + c * rows
 
-    spots = []
-    for c in (core, 1 - core):
-        for at in (x, x + ring - 1, x + 1):
-            spots += [row_of(y_hi, at, c), row_of(1 - y_hi, at, c)]
-        spots += [row_of(y_hi, x + 2, c), 0, row_of(1 - y_hi, x + 2, c), 0]
-    spots = jnp.stack(spots).astype(jnp.int32)
-
-    def gather(part, other):
-        both = jnp.concatenate([part, other], axis=0)
-        right = move(both, 0, 1, 0)
-        left = move(both, 0, -1, 0)
-        far_right = move(right[:rows], 0, 1, 0)
-        far_left = move(left[rows:], 0, -1, 0)
-        own = [both, right, left, far_right, far_left]
+    def spread(y, c):
+        half = rows // 2
+        near = [(0, rows, row_of(y, x + d, c)) for d in (0, ring - 1, 1)]
+        return near + [(0, half, row_of(y, x + 2, c) + k * half) for k in range(2)]
+
+    def gather(block):
+        half = block.shape[0] // 2
+        right = move(block, 0, 1, 0)
+        left = move(block, 0, -1, 0)
+        far_right = move(right[:half], 0, 1, 0)
+        far_left = move(left[half:], 0, -1, 0)
+        own = [block, right, left, far_right, far_left]
         swapped = []
         for piece in own:
             swapped.append(move(piece, 0, 0, 1))
         return own + swapped
 
-    def terms(pieces):
+    def single(y, first):
+        return [(first + i, *spot) for i, spot in enumerate(spread(y, core) + spread(y, 1 - core))]
+
+    def double(first):
+        out = []
+        for k, c in enumerate((core, 1 - core)):
+            at = first + 5 * k
+            for side, y in enumerate((y_hi, 1 - y_hi)):
+                out += [(at + i, side * rows, rows, row_of(y, x + d, c)) for i, d in enumerate((0, ring - 1, 1))]
+                out.append((at + 3 + side, 0, rows, row_of(y, x + 2, c)))
+        return out
+
+    def terms(pieces, spots):
+        blocks = tuple(spot[:3] for spot in spots)
         return pl.pallas_call(
-            functools.partial(terms_body, pieces=len(pieces), scale=1.0 / math.sqrt(count * owners)),
+            functools.partial(
+                terms_body, pieces=len(pieces), blocks=blocks, scale=1.0 / math.sqrt(count * owners)
+            ),
             name="terms",
             grid_spec=pltpu.PrefetchScalarGridSpec(
                 num_scalar_prefetch=1,
@@ -351,7 +362,7 @@
                     pltpu.VMEM((count, half_width), bf16),
                     pltpu.VMEM((cols, count), bf16),
                     pltpu.VMEM((owners, cols, LANES), bf16),
-                    dma((2 * len(pieces),)),
+                    dma((len(blocks),)),
                     dma((2,)),
                     dma((owners // 2,)),
                 ],
@@ -364,13 +375,13 @@
             cost_estimate=pl.CostEstimate(
                 flops=2 * count * half_width * cols, transcendentals=0, bytes_accessed=12 << 20
             ),
-        )(spots, *pieces, cots)
+        )(jnp.stack([spot[3] for spot in spots]).astype(jnp.int32), *pieces, cots)
 
     other0 = move(parts[0], 2, 0, 0)
     other1 = move(parts[1], 2, 0, 0)
-    cut0, rows0 = terms(gather(parts[0], other0))
+    cut0, rows0 = terms(gather(parts[0]) + gather(other0), single(y_hi, 0) + single(1 - y_hi, 10))
     cut0 = lax.all_to_all(cut0, "dp", split_axis=0, concat_axis=0, tiled=True)
-    cut1, rows1 = terms(gather(parts[1], other1))
+    cut1, rows1 = terms(gather(jnp.concatenate([parts[1], other1], axis=0)), double(0))
     cut1 = lax.all_to_all(cut1, "dp", split_axis=0, concat_axis=0, tiled=True)
     shape = (owners, 2, LANES)
     feat_one, feat_two = pl.pallas_call(
@@ -396,11 +407,17 @@
         cost_estimate=pl.CostEstimate(flops=4 * count * half_width * cols, transcendentals=0, bytes_accessed=14 << 20),
     )(rows0, rows1, student_one.reshape(*shape, split), student_two.reshape(*shape, cols - split))
     total0 = pl.pallas_call(
-        sum_first_body, name="sum_first", out_shape=jax.ShapeDtypeStruct((LANES, cols), f32)
+        sum_first_body,
+        name="sum_first",
+        in_specs=[inside],
+        out_specs=inside,
+        out_shape=jax.ShapeDtypeStruct((LANES, cols), f32),
     )(cut0)
     grad_one, grad_two = pl.pallas_call(
         sum_last_body,
         name="sum_last",
+        in_specs=[inside, inside],
+        out_specs=(inside, inside),
         out_shape=(
             jax.ShapeDtypeStruct((2 * LANES, split), f32),
             jax.ShapeDtypeStruct((2 * LANES, cols - split), f32),

time: 269 us -> 267 us (level)
  starting transfers between devices: 49.2 us -> 56.2 us
  waiting for transfers between devices: 78.3 us -> 71.5 us
    ppermute x23 -> x32, starting transfers between devices: 28.5 us -> 35.7 us  [move(): return lax.ppermute(array, axes, [(d, target(d)) for d in range(devices)])]
    ppermute x23 -> x32, waiting for transfers between devices: 40.1 us -> 33.3 us  [move(): return lax.ppermute(array, axes, [(d, target(d)) for d in range(devices)])]
    unnamed x40 -> x45, local copies, waits for them, and re-layouts: 8.97 us -> 6.56 us
  transfers between devices with their start and end apart: 26 -> 35, of which waited for: 12 -> 12; matrix products, arithmetic and copies ran while one was open for 3% -> 3% of each run, Pallas kernels for 12% -> 12%
where the time goes in v4:
time: 267 us
  Pallas kernels  75.3 us (28%)
  waiting for transfers between devices  71.5 us (27%)
  starting transfers between devices  56.2 us (21%)
  blocking collectives  52.9 us (20%)
  local copies, waits for them, and re-layouts  7.97 us (3%)
    all_to_all x1, blocking collectives, local(): lax.all_to_all(expert_out.reshape(devices, capacity // 2, sub, LANES), ('...  52.9 us
    ppermute x32, starting transfers between devices, move(): return lax.ppermute(array, axes, [(d, target(d)) for d in range(devices)])  35.7 us
    ppermute x32, waiting for transfers between devices, move(): return lax.ppermute(array, axes, [(d, target(d)) for d in range(devices)])  33.3 us
    all_to_all x1, waiting for transfers between devices, local(): lax.all_to_all(placed.reshape(devices, capacity // 2, sub, LANES), ('dp',...  32 us
    pallas_call x1, Pallas kernels, expert(): pl.pallas_call(functools.partial(expert_body, step=step, tile=tile, cols=...  29.1 us
    pallas_call x2, Pallas kernels, terms(): pl.pallas_call(functools.partial(terms_body, pieces=len(pieces), blocks=b...  17.7 us
    pallas_call x1, Pallas kernels, project(): pl.pallas_call(features_body, name='features', in_specs=[anywhere] * 4, o...  12.2 us
    all_to_all x1, starting transfers between devices, local(): lax.all_to_all(placed.reshape(devices, capacity // 2, sub, LANES), ('dp',...  11.9 us
  transfers between devices with their start and end apart: 35, of which 12 were waited for; matrix products, arithmetic and copies ran while one was open for 3% of the time, Pallas kernels for 12%

profile of v4, /device:TPU:1, one launch (start us, length us, event | category | flops | bytes accessed | tf_op | source)
XLA Modules:
  0.0 266.7 jit_solution(10578064242644217500)
XLA Ops:
  0.6 5.7 %dispatch.1 = (bf16[896,16,128]{2,1,0:T(8,128)(2,1)}, s32[6,128]{1,0:T(8,128)}) custom-call(s32[6,128]{1,0:T(8,128)} %bitcast.42, bf16[128,2048]{1,0:T(8,128)(2,1)} %tok_ref.1, f32[1,2048]{1,0:T(1,128)} %bitcast.41), custom_call_target="tpu_custom_call" | custom-call | tf_op jit(solution)/shard_map/dispatch/pallas_call | solution.py:54
  6.4 11.9 %all-to-all-start = ((bf16[128,7,16,128]{3,2,1,0:T(8,128)(2,1)}), bf16[128,7,16,128]{3,2,1,0:T(8,128)(2,1)}, u32[]{:S(2)}, u32[]{:S(2)}) async-start(bf16[128,7,16,128]{3,2,1,0:T(8,128)(2,1)} %bitcast.40), calls=%async_computation | async-start | bytes 7340032 | tf_op jit(solution)/shard_map/all_to_all | solution.py:465
  20.6 3.1 %copy.17 = bf16[2048,512]{0,1:T(8,128)(2,1)S(1)} copy(bf16[2048,512]{1,0:T(8,128)(2,1)} %param.21) | data formatting | bytes 4194304 | tf_op args[10]
  25.6 3.2 %collective-permute-done.gate1 = bf16[704,2048]{1,0:T(8,128)(2,1)} collective-permute-done((bf16[704,2048]{1,0:T(8,128)(2,1)}, bf16[704,2048]{1,0:T(8,128)(2,1)}, u32[]{:S(2)}, u32[]{:S(2)}) %collective-permute-start) | collective-permute-done | bytes 2883616 | tf_op jit(solution)/shard_map/ppermute | solution.py:457
  28.8 4.1 %collective-permute-done.1.up1 = bf16[704,2048]{1,0:T(8,128)(2,1)} collective-permute-done((bf16[704,2048]{1,0:T(8,128)(2,1)}, bf16[704,2048]{1,0:T(8,128)(2,1)}, u32[]{:S(2)}, u32[]{:S(2)}) %collective-permute-start.1) | collective-permute-done | bytes 2883616 | tf_op jit(solution)/shard_map/ppermute | solution.py:457
  33.0 32.0 %all-to-all-done = bf16[128,7,16,128]{3,2,1,0:T(8,128)(2,1)} async-done(((bf16[128,7,16,128]{3,2,1,0:T(8,128)(2,1)}), bf16[128,7,16,128]{3,2,1,0:T(8,128)(2,1)}, u32[]{:S(2)}, u32[]{:S(2)}) %all-to-all-start) | async-done | bytes 3670048 | tf_op jit(solution)/shard_map/all_to_all | solution.py:465
  65.0 29.1 %expert.1 = bf16[896,16,128]{2,1,0:T(8,128)(2,1)} custom-call(bf16[896,16,128]{2,1,0:T(8,128)(2,1)} %bitcast.4.rows_hbm, bf16[704,2048]{1,0:T(8,128)(2,1)} %bitcast.6.gate0, bf16[704,2048]{1,0:T(8,128)(2,1)} %bitcast.8.up0, bf16[704,2048]{1,0:T(8,128)(2,1)} %bitcast.9.down0, bf16[704,2048]{1,0:T(8,128)(2,1)} %collective-permute-done.gate1, ...), custom_call_target="tpu_custom_call" | custom-call | tf_op jit(solution)/shard_map/expert/pallas_call | solution.py:172
  94.0 52.9 %all_to_all.20 = bf16[128,7,16,128]{3,2,1,0:T(8,128)(2,1)} all-to-all(bf16[128,7,16,128]{3,2,1,0:T(8,128)(2,1)} %bitcast.39), channel_id=1, replica_groups=mesh['dp'=8,'expert'=16] {'dp','expert'}, dimensions={0} | all-to-all | bytes 7340032 | tf_op jit(solution)/shard_map/all_to_all | solution.py:481
  146.9 5.6 %combine.1 = (bf16[128,2048]{1,0:T(8,128)(2,1)}, bf16[128,1024]{1,0:T(8,128)(2,1)}, bf16[128,1024]{1,0:T(8,128)(2,1)}) custom-call(s32[6,128]{1,0:T(8,128)} %get-tuple-element.20.pos_ref, f32[6,128]{1,0:T(8,128)} %bitcast.43, bf16[896,16,128]{2,1,0:T(8,128)(2,1)} %bitcast.38), custom_call_target="tpu_custom_call" | custom-call | tf_op jit(solution)/shard_map/combine/pallas_call | solution.py:92
  154.7 4.6 %collective-permute-done.4.refs_2_ = bf16[128,1024]{1,0:T(8,128)(2,1)S(1)} collective-permute-done((bf16[128,1024]{1,0:T(8,128)(2,1)}, bf16[128,1024]{1,0:T(8,128)(2,1)S(1)}, u32[]{:S(2)}, u32[]{:S(2)}) %collective-permute-start.4) | collective-permute-done | bytes 262176 | tf_op jit(solution)/shard_map/ppermute | solution.py:457
  159.4 3.2 %collective-permute-start.6 = (bf16[64,1024]{1,0:T(8,128)(2,1)S(1)}, bf16[64,1024]{1,0:T(8,128)(2,1)S(1)}, u32[]{:S(2)}, u32[]{:S(2)}) collective-permute-start(bf16[64,1024]{1,0:T(8,128)(2,1)S(1)} %slice.25), channel_id=1, source_target_pairs={{0,6},{1,7},{2,0},{3,1},{4,2},{5,3},{6,4},{7,5},{8,14},{9,15},{10,... | collective-permute-start | bytes 393224 | tf_op jit(solution)/shard_map/ppermute | solution.py:457
  164.2 2.6 collective-permute-start.7
  168.0 4.2 %collective-permute-start.9 = (bf16[128,1024]{1,0:T(8,128)(2,1)S(1)}, bf16[128,1024]{1,0:T(8,128)(2,1)S(1)}, u32[]{:S(2)}, u32[]{:S(2)}) collective-permute-start(bf16[128,1024]{1,0:T(8,128)(2,1)S(1)} %collective-permute-done.4.refs_2_), channel_id=1, source_target_pairs={{0,1},{1,0},{2,3},{3,2},{4,5},{5,4},{6,7},{7,6},{8,9},{9,8},{10,11... | collective-permute-start | bytes 786440 | tf_op jit(solution)/shard_map/ppermute | solution.py:457
  172.9 2.6 collective-permute-start.10
  187.7 8.9 %terms.2 = (bf16[8,768,128]{2,1,0:T(8,128)(2,1)}, bf16[2048,1024]{1,0:T(8,128)(2,1)}) custom-call(s32[20]{0:T(128)} %stack.102.at_ref, bf16[128,1024]{1,0:T(8,128)(2,1)} %get-tuple-element.24.refs_0_, bf16[128,1024]{1,0:T(8,128)(2,1)} %copy-done.7, bf16[128,1024]{1,0:T(8,128)(2,1)} %copy-done.6, bf16[64,1024]{1,0:T(8,128)(2,1)} %copy-done.18, ...), custom_call_target="tpu_custom_call" | custom-call | flops 3221225472 | bytes 12582912 | tf_op jit(solution)/shard_map/terms/pallas_call | solution.py:351
  196.6 3.6 %all-to-all-start.2 = ((bf16[8,768,128]{2,1,0:T(8,128)(2,1)}), bf16[8,768,128]{2,1,0:T(8,128)(2,1)S(1)}, u32[]{:S(2)}, u32[]{:S(2)}) async-start(bf16[8,768,128]{2,1,0:T(8,128)(2,1)} %get-tuple-element.31), calls=%async_computation.2 | async-start | bytes 3145728 | tf_op jit(solution)/shard_map/all_to_all | solution.py:383
  202.6 10.9 %collective-permute-done.24.refs_2_ = bf16[256,1024]{1,0:T(8,128)(2,1)S(1)} collective-permute-done((bf16[256,1024]{1,0:T(8,128)(2,1)S(1)}, bf16[256,1024]{1,0:T(8,128)(2,1)S(1)}, u32[]{:S(2)}, u32[]{:S(2)}) %collective-permute-start.24) | collective-permute-done | bytes 524320 | tf_op jit(solution)/shard_map/ppermute | solution.py:457
  217.1 3.2 %collective-permute-done.26.refs_4_ = bf16[128,1024]{1,0:T(8,128)(2,1)S(1)} collective-permute-done((bf16[128,1024]{1,0:T(8,128)(2,1)S(1)}, bf16[128,1024]{1,0:T(8,128)(2,1)S(1)}, u32[]{:S(2)}, u32[]{:S(2)}) %collective-permute-start.26) | collective-permute-done | bytes 262176 | tf_op jit(solution)/shard_map/ppermute | solution.py:457
  222.3 3.4 %collective-permute-done.25.refs_3_ = bf16[128,1024]{1,0:T(8,128)(2,1)} collective-permute-done((bf16[128,1024]{1,0:T(8,128)(2,1)S(1)}, bf16[128,1024]{1,0:T(8,128)(2,1)}, u32[]{:S(2)}, u32[]{:S(2)}) %collective-permute-start.25) | collective-permute-done | bytes 262176 | tf_op jit(solution)/shard_map/ppermute | solution.py:457
  228.2 8.8 %terms.3 = (bf16[8,768,128]{2,1,0:T(8,128)(2,1)}, bf16[2048,1024]{1,0:T(8,128)(2,1)}) custom-call(s32[16]{0:T(128)} %stack.103.at_ref, bf16[256,1024]{1,0:T(8,128)(2,1)} %copy-done.5, bf16[256,1024]{1,0:T(8,128)(2,1)} %copy-done.4, bf16[256,1024]{1,0:T(8,128)(2,1)} %copy-done.3, bf16[128,1024]{1,0:T(8,128)(2,1)} %collective-permute-done.25.refs_3_, ...), custom_call_target="tpu_custom_call" | custom-call | flops 3221225472 | bytes 12582912 | tf_op jit(solution)/shard_map/terms/pallas_call | solution.py:351
  237.0 5.1 %all-to-all-start.3 = ((bf16[8,768,128]{2,1,0:T(8,128)(2,1)}), bf16[8,768,128]{2,1,0:T(8,128)(2,1)S(1)}, u32[]{:S(2)}, u32[]{:S(2)}) async-start(bf16[8,768,128]{2,1,0:T(8,128)(2,1)} %get-tuple-element.32), calls=%async_computation.3 | async-start | bytes 3145728 | tf_op jit(solution)/shard_map/all_to_all | solution.py:385
  242.1 12.2 %features.1 = (bf16[2048,256]{1,0:T(8,128)(2,1)}, bf16[2048,512]{1,0:T(8,128)(2,1)}) custom-call(bf16[2048,1024]{1,0:T(8,128)(2,1)} %get-tuple-element.26.rows0, bf16[2048,1024]{1,0:T(8,128)(2,1)} %get-tuple-element.28.rows1, bf16[8,2,128,256]{3,2,1,0:T(8,128)(2,1)} %bitcast.45, bf16[8,2,128,512]{3,2,1,0:T(8,128)(2,1)} %bitcast.44), custom_call_target="tpu_custom_call" | custom-call | flops 6442450944 | bytes 14680064 | tf_op jit(solution)/shard_map/features/pallas_call | solution.py:387
  256.7 6.2 %all-to-all-done.3.pieces_ref = bf16[8,768,128]{2,1,0:T(8,128)(2,1)S(1)} async-done(((bf16[8,768,128]{2,1,0:T(8,128)(2,1)}), bf16[8,768,128]{2,1,0:T(8,128)(2,1)S(1)}, u32[]{:S(2)}, u32[]{:S(2)}) %all-to-all-start.3) | async-done | bytes 1572896 | tf_op jit(solution)/shard_map/all_to_all | solution.py:385
  264.1 2.6 sum_last.1
  (110 shorter events, 36.0 us)
Async XLA Ops:
  6.4 58.6 %all-to-all-start = ((bf16[128,7,16,128]{3,2,1,0:T(8,128)(2,1)}), bf16[128,7,16,128]{3,2,1,0:T(8,128)(2,1)}, u32[]{:S(2)}, u32[]{:S(2)}) async-start(bf16[128,7,16,128]{3,2,1,0:T(8,128)(2,1)} %bitcast.40), calls=%async_computation | async-start | bytes 7340032 | tf_op jit(solution)/shard_map/all_to_all | solution.py:465
  18.3 7.3 %collective-permute-start.2 = (bf16[704,2048]{1,0:T(8,128)(2,1)}, bf16[704,2048]{1,0:T(8,128)(2,1)}, u32[]{:S(2)}, u32[]{:S(2)}) collective-permute-start(bf16[704,2048]{1,0:T(8,128)(2,1)} %bitcast.9.down0), channel_id=1, source_target_pairs={{0,1},{1,0},{2,3},{3,2},{4,5},{5,4},{6,7},{7,6},{8,9},{9,8},{10,11... | collective-permute-start | bytes 8650760 | tf_op jit(solution)/shard_map/ppermute | solution.py:457
  19.5 9.4 %collective-permute-start = (bf16[704,2048]{1,0:T(8,128)(2,1)}, bf16[704,2048]{1,0:T(8,128)(2,1)}, u32[]{:S(2)}, u32[]{:S(2)}) collective-permute-start(bf16[704,2048]{1,0:T(8,128)(2,1)} %bitcast.6.gate0), channel_id=1, source_target_pairs={{0,1},{1,0},{2,3},{3,2},{4,5},{5,4},{6,7},{7,6},{8,9},{9,8},{10,11... | collective-permute-start | bytes 8650760 | tf_op jit(solution)/shard_map/ppermute | solution.py:457
  19.6 13.4 %collective-permute-start.1 = (bf16[704,2048]{1,0:T(8,128)(2,1)}, bf16[704,2048]{1,0:T(8,128)(2,1)}, u32[]{:S(2)}, u32[]{:S(2)}) collective-permute-start(bf16[704,2048]{1,0:T(8,128)(2,1)} %bitcast.8.up0), channel_id=1, source_target_pairs={{0,1},{1,0},{2,3},{3,2},{4,5},{5,4},{6,7},{7,6},{8,9},{9,8},{10,11... | collective-permute-start | bytes 8650760 | tf_op jit(solution)/shard_map/ppermute | solution.py:457
  153.6 9.0 %collective-permute-start.12 = (bf16[128,1024]{1,0:T(8,128)(2,1)}, bf16[128,1024]{1,0:T(8,128)(2,1)S(1)}, u32[]{:S(2)}, u32[]{:S(2)}) collective-permute-start(bf16[128,1024]{1,0:T(8,128)(2,1)} %get-tuple-element.24.refs_0_), channel_id=1, source_target_pairs={{0,8},{1,9},{2,10},{3,11},{4,12},{5,13},{6,14},{7,15},{8,0},{9,1},... | collective-permute-start | bytes 786440 | tf_op jit(solution)/shard_map/ppermute | solution.py:457
  153.9 8.8 %collective-permute-start.3 = (bf16[128,1024]{1,0:T(8,128)(2,1)}, bf16[128,1024]{1,0:T(8,128)(2,1)S(1)}, u32[]{:S(2)}, u32[]{:S(2)}) collective-permute-start(bf16[128,1024]{1,0:T(8,128)(2,1)} %get-tuple-element.24.refs_0_), channel_id=1, source_target_pairs={{0,2},{1,3},{2,4},{3,5},{4,6},{5,7},{6,0},{7,1},{8,10},{9,11},{10,... | collective-permute-start | bytes 786440 | tf_op jit(solution)/shard_map/ppermute | solution.py:457
  159.4 7.5 %collective-permute-start.6 = (bf16[64,1024]{1,0:T(8,128)(2,1)S(1)}, bf16[64,1024]{1,0:T(8,128)(2,1)S(1)}, u32[]{:S(2)}, u32[]{:S(2)}) collective-permute-start(bf16[64,1024]{1,0:T(8,128)(2,1)S(1)} %slice.25), channel_id=1, source_target_pairs={{0,6},{1,7},{2,0},{3,1},{4,2},{5,3},{6,4},{7,5},{8,14},{9,15},{10,... | collective-permute-start | bytes 393224 | tf_op jit(solution)/shard_map/ppermute | solution.py:457
  162.6 9.5 %collective-permute-start.14 = (bf16[128,1024]{1,0:T(8,128)(2,1)S(1)}, bf16[128,1024]{1,0:T(8,128)(2,1)S(1)}, u32[]{:S(2)}, u32[]{:S(2)}) collective-permute-start(bf16[128,1024]{1,0:T(8,128)(2,1)S(1)} %collective-permute-done.12.refs_10_), channel_id=1, source_target_pairs={{0,6},{1,7},{2,0},{3,1},{4,2},{5,3},{6,4},{7,5},{8,14},{9,15},{10,... | collective-permute-start | bytes 786440 | tf_op jit(solution)/shard_map/ppermute | solution.py:457
  164.1 8.7 %collective-permute-start.13 = (bf16[128,1024]{1,0:T(8,128)(2,1)S(1)}, bf16[128,1024]{1,0:T(8,128)(2,1)S(1)}, u32[]{:S(2)}, u32[]{:S(2)}) collective-permute-start(bf16[128,1024]{1,0:T(8,128)(2,1)S(1)} %collective-permute-done.12.refs_10_), channel_id=1, source_target_pairs={{0,2},{1,3},{2,4},{3,5},{4,6},{5,7},{6,0},{7,1},{8,10},{9,11},{10,... | collective-permute-start | bytes 786440 | tf_op jit(solution)/shard_map/ppermute | solution.py:457
  164.2 11.3 %collective-permute-start.7 = (bf16[128,1024]{1,0:T(8,128)(2,1)}, bf16[128,1024]{1,0:T(8,128)(2,1)S(1)}, u32[]{:S(2)}, u32[]{:S(2)}) collective-permute-start(bf16[128,1024]{1,0:T(8,128)(2,1)} %get-tuple-element.24.refs_0_), channel_id=1, source_target_pairs={{0,1},{1,0},{2,3},{3,2},{4,5},{5,4},{6,7},{7,6},{8,9},{9,8},{10,11... | collective-permute-start | bytes 786440 | tf_op jit(solution)/shard_map/ppermute | solution.py:457
  166.9 8.8 %collective-permute-start.17 = (bf16[128,1024]{1,0:T(8,128)(2,1)S(1)}, bf16[128,1024]{1,0:T(8,128)(2,1)S(1)}, u32[]{:S(2)}, u32[]{:S(2)}) collective-permute-start(bf16[128,1024]{1,0:T(8,128)(2,1)S(1)} %collective-permute-done.12.refs_10_), channel_id=1, source_target_pairs={{0,1},{1,0},{2,3},{3,2},{4,5},{5,4},{6,7},{7,6},{8,9},{9,8},{10,11... | collective-permute-start | bytes 786440 | tf_op jit(solution)/shard_map/ppermute | solution.py:457
  168.0 9.3 %collective-permute-start.9 = (bf16[128,1024]{1,0:T(8,128)(2,1)S(1)}, bf16[128,1024]{1,0:T(8,128)(2,1)S(1)}, u32[]{:S(2)}, u32[]{:S(2)}) collective-permute-start(bf16[128,1024]{1,0:T(8,128)(2,1)S(1)} %collective-permute-done.4.refs_2_), channel_id=1, source_target_pairs={{0,1},{1,0},{2,3},{3,2},{4,5},{5,4},{6,7},{7,6},{8,9},{9,8},{10,11... | collective-permute-start | bytes 786440 | tf_op jit(solution)/shard_map/ppermute | solution.py:457
  175.6 9.3 %collective-permute-start.8 = (bf16[128,1024]{1,0:T(8,128)(2,1)S(1)}, bf16[128,1024]{1,0:T(8,128)(2,1)S(1)}, u32[]{:S(2)}, u32[]{:S(2)}) collective-permute-start(bf16[128,1024]{1,0:T(8,128)(2,1)S(1)} %collective-permute-done.3.refs_1_), channel_id=1, source_target_pairs={{0,1},{1,0},{2,3},{3,2},{4,5},{5,4},{6,7},{7,6},{8,9},{9,8},{10,11... | collective-permute-start | bytes 786440 | tf_op jit(solution)/shard_map/ppermute | solution.py:457
  177.2 9.8 %collective-permute-start.19 = (bf16[128,1024]{1,0:T(8,128)(2,1)S(1)}, bf16[128,1024]{1,0:T(8,128)(2,1)S(1)}, u32[]{:S(2)}, u32[]{:S(2)}) collective-permute-start(bf16[128,1024]{1,0:T(8,128)(2,1)S(1)} %collective-permute-done.14.refs_12_), channel_id=1, source_target_pairs={{0,1},{1,0},{2,3},{3,2},{4,5},{5,4},{6,7},{7,6},{8,9},{9,8},{10,11... | collective-permute-start | bytes 786440 | tf_op jit(solution)/shard_map/ppermute | solution.py:457
  178.2 8.9 %collective-permute-start.18 = (bf16[128,1024]{1,0:T(8,128)(2,1)S(1)}, bf16[128,1024]{1,0:T(8,128)(2,1)}, u32[]{:S(2)}, u32[]{:S(2)}) collective-permute-start(bf16[128,1024]{1,0:T(8,128)(2,1)S(1)} %collective-permute-done.13.refs_11_), channel_id=1, source_target_pairs={{0,1},{1,0},{2,3},{3,2},{4,5},{5,4},{6,7},{7,6},{8,9},{9,8},{10,11... | collective-permute-start | bytes 786440 | tf_op jit(solution)/shard_map/ppermute | solution.py:457
  184.9 15.3 %collective-permute-start.22 = (bf16[128,1024]{1,0:T(8,128)(2,1)}, bf16[128,1024]{1,0:T(8,128)(2,1)S(1)}, u32[]{:S(2)}, u32[]{:S(2)}) collective-permute-start(bf16[128,1024]{1,0:T(8,128)(2,1)} %get-tuple-element.27), channel_id=1, source_target_pairs={{0,8},{1,9},{2,10},{3,11},{4,12},{5,13},{6,14},{7,15},{8,0},{9,1},... | collective-permute-start | bytes 786440 | tf_op jit(solution)/shard_map/ppermute | solution.py:457
  196.6 40.4 %all-to-all-start.2 = ((bf16[8,768,128]{2,1,0:T(8,128)(2,1)}), bf16[8,768,128]{2,1,0:T(8,128)(2,1)S(1)}, u32[]{:S(2)}, u32[]{:S(2)}) async-start(bf16[8,768,128]{2,1,0:T(8,128)(2,1)} %get-tuple-element.31), calls=%async_computation.2 | async-start | bytes 3145728 | tf_op jit(solution)/shard_map/all_to_all | solution.py:383
  200.3 13.3 %collective-permute-start.24 = (bf16[256,1024]{1,0:T(8,128)(2,1)S(1)}, bf16[256,1024]{1,0:T(8,128)(2,1)S(1)}, u32[]{:S(2)}, u32[]{:S(2)}) collective-permute-start(bf16[256,1024]{1,0:T(8,128)(2,1)S(1)} %constant_dynamic-update-slice_fusion.refs_0_), channel_id=1, source_target_pairs={{0,6},{1,7},{2,0},{3,1},{4,2},{5,3},{6,4},{7,5},{8,14},{9,15},{10,... | collective-permute-start | bytes 1572872 | tf_op jit(solution)/shard_map/ppermute | solution.py:457
  200.3 15.9 %collective-permute-start.23 = (bf16[256,1024]{1,0:T(8,128)(2,1)S(1)}, bf16[256,1024]{1,0:T(8,128)(2,1)S(1)}, u32[]{:S(2)}, u32[]{:S(2)}) collective-permute-start(bf16[256,1024]{1,0:T(8,128)(2,1)S(1)} %constant_dynamic-update-slice_fusion.refs_0_), channel_id=1, source_target_pairs={{0,2},{1,3},{2,4},{3,5},{4,6},{5,7},{6,0},{7,1},{8,10},{9,11},{10,... | collective-permute-start | bytes 1572872 | tf_op jit(solution)/shard_map/ppermute | solution.py:457
  201.8 25.5 %collective-permute-start.27 = (bf16[256,1024]{1,0:T(8,128)(2,1)S(1)}, bf16[256,1024]{1,0:T(8,128)(2,1)}, u32[]{:S(2)}, u32[]{:S(2)}) collective-permute-start(bf16[256,1024]{1,0:T(8,128)(2,1)S(1)} %constant_dynamic-update-slice_fusion.refs_0_), channel_id=1, source_target_pairs={{0,1},{1,0},{2,3},{3,2},{4,5},{5,4},{6,7},{7,6},{8,9},{9,8},{10,11... | collective-permute-start | bytes 1572872 | tf_op jit(solution)/shard_map/ppermute | solution.py:457
  214.4 12.9 %collective-permute-start.29 = (bf16[256,1024]{1,0:T(8,128)(2,1)S(1)}, bf16[256,1024]{1,0:T(8,128)(2,1)}, u32[]{:S(2)}, u32[]{:S(2)}) collective-permute-start(bf16[256,1024]{1,0:T(8,128)(2,1)S(1)} %collective-permute-done.24.refs_2_), channel_id=1, source_target_pairs={{0,1},{1,0},{2,3},{3,2},{4,5},{5,4},{6,7},{7,6},{8,9},{9,8},{10,11... | collective-permute-start | bytes 1572872 | tf_op jit(solution)/shard_map/ppermute | solution.py:457
  216.3 9.5 %collective-permute-start.25 = (bf16[128,1024]{1,0:T(8,128)(2,1)S(1)}, bf16[128,1024]{1,0:T(8,128)(2,1)}, u32[]{:S(2)}, u32[]{:S(2)}) collective-permute-start(bf16[128,1024]{1,0:T(8,128)(2,1)S(1)} %slice.28), channel_id=1, source_target_pairs={{0,2},{1,3},{2,4},{3,5},{4,6},{5,7},{6,0},{7,1},{8,10},{9,11},{10,... | collective-permute-start | bytes 786440 | tf_op jit(solution)/shard_map/ppermute | solution.py:457
  216.9 11.3 %collective-permute-start.28 = (bf16[256,1024]{1,0:T(8,128)(2,1)S(1)}, bf16[256,1024]{1,0:T(8,128)(2,1)}, u32[]{:S(2)}, u32[]{:S(2)}) collective-permute-start(bf16[256,1024]{1,0:T(8,128)(2,1)S(1)} %collective-permute-done.23.refs_1_), channel_id=1, source_target_pairs={{0,1},{1,0},{2,3},{3,2},{4,5},{5,4},{6,7},{7,6},{8,9},{9,8},{10,11... | collective-permute-start | bytes 1572872 | tf_op jit(solution)/shard_map/ppermute | solution.py:457
  237.0 25.9 %all-to-all-start.3 = ((bf16[8,768,128]{2,1,0:T(8,128)(2,1)}), bf16[8,768,128]{2,1,0:T(8,128)(2,1)S(1)}, u32[]{:S(2)}, u32[]{:S(2)}) async-start(bf16[8,768,128]{2,1,0:T(8,128)(2,1)} %get-tuple-element.32), calls=%async_computation.3 | async-start | bytes 3145728 | tf_op jit(solution)/shard_map/all_to_all | solution.py:385
  (32 other events, 347.6 us)

commit v5 on v4

--- a/solution.py
+++ b/solution.py
@@ -194,9 +194,9 @@
 VMEM_LIMIT = 60 * 1024 * 1024
 
 
-def terms_body(at_ref, *refs, pieces, blocks, scale):
+def terms_body(at_ref, *refs, pieces, blocks, scale, apart):
     parts = refs[:pieces]
-    cot_hbm, out_hbm, all_rows, rows_ref, cot_ref, cut_ref, sem, side_sem, out_sem = refs[pieces:]
+    cot_hbm, *out_hbm, all_rows, rows_ref, cot_ref, cut_ref, sem, side_sem, out_sem = refs[pieces:]
     loads = []
     for i, (piece, start, size) in enumerate(blocks):
         to = pl.ds(pl.multiple_of(at_ref[i], size), size)
@@ -217,12 +217,19 @@
         terms = jnp.dot(cot_ref[...], rows_ref[:, at], preferred_element_type=jnp.float32) * scale
         cut_ref[2 * d] = terms[:, :LANES].astype(jnp.bfloat16)
         cut_ref[2 * d + 1] = terms[:, LANES:].astype(jnp.bfloat16)
-        pltpu.make_async_copy(cut_ref.at[pl.ds(2 * d, 2)], out_hbm.at[pl.ds(2 * d, 2)], out_sem.at[d]).start()
         return carry
 
     lax.fori_loop(0, owners // 2, step, 0)
-    for d in range(owners // 2):
-        pltpu.make_async_copy(cut_ref.at[pl.ds(2 * d, 2)], out_hbm.at[pl.ds(2 * d, 2)], out_sem.at[d]).wait()
+    if apart:
+        outs = [
+            pltpu.make_async_copy(cut_ref.at[at_ref[len(blocks) + i]], out, out_sem.at[i]) for i, out in enumerate(out_hbm)
+        ]
+    else:
+        outs = [pltpu.make_async_copy(cut_ref, out_hbm[0], out_sem.at[0])]
+    for c in outs:
+        c.start()
+    for c in outs:
+        c.wait()
     keep.wait()
 
 
@@ -281,30 +288,31 @@
             c.wait()
 
 
-def total_of(pieces_ref):
-    total = pieces_ref[0].astype(jnp.float32)
-    for i in range(1, pieces_ref.shape[0]):
-        total = total + pieces_ref[i].astype(jnp.float32)
+def total_of(pieces):
+    total = pieces[0].astype(jnp.float32)
+    for piece in pieces[1:]:
+        total = total + piece.astype(jnp.float32)
     return total.T
 
 
 def sum_first_body(pieces_ref, out_ref):
-    out_ref[...] = total_of(pieces_ref)
-
-
-def sum_last_body(first_ref, pieces_ref, one_ref, two_ref):
+    out_ref[...] = total_of([pieces_ref[i] for i in range(pieces_ref.shape[0])])
+
+
+def sum_last_body(first_ref, *refs):
+    *pieces, one_ref, two_ref = refs
     split = one_ref.shape[1]
     half = first_ref.shape[0]
     one_ref[:half] = first_ref[:, :split]
     two_ref[:half] = first_ref[:, split:]
-    total = total_of(pieces_ref)
+    total = total_of([piece[...] for piece in pieces])
     one_ref[half:] = total[:, :split]
     two_ref[half:] = total[:, split:]
 
 
-def project(parts, student_one, student_two, cots, move, place):
+def project(parts, student_one, student_two, cots, move, pass_on, place):
     rows, half_width = parts[0].shape
-    y_hi, x, core = place
+    z, y_lo, y_hi, x, core = place
     ring, owners = 4, 8
     count = 4 * ring * rows
     split = student_one.shape[1]
@@ -346,43 +354,51 @@
                 out.append((at + 3 + side, 0, rows, row_of(y, x + 2, c)))
         return out
 
-    def terms(pieces, spots):
+    steps = [(0, 0), (2, 1), (2, 0), (1, 1), (3, 1), (1, 0), (3, 0), (0, 1)]
+    owner_of = [(z + dz) % 4 * 2 + (y_lo + dy) % 2 for dz, dy in steps]
+
+    def terms(pieces, spots, apart):
+        cuts = (owners * [jax.ShapeDtypeStruct((cols, LANES), bf16)]) if apart else [
+            jax.ShapeDtypeStruct((owners, cols, LANES), bf16)
+        ]
         blocks = tuple(spot[:3] for spot in spots)
         return pl.pallas_call(
             functools.partial(
-                terms_body, pieces=len(pieces), blocks=blocks, scale=1.0 / math.sqrt(count * owners)
+                terms_body,
+                pieces=len(pieces),
+                blocks=blocks,
+                scale=1.0 / math.sqrt(count * owners),
+                apart=apart,
             ),
             name="terms",
             grid_spec=pltpu.PrefetchScalarGridSpec(
                 num_scalar_prefetch=1,
                 grid=(1,),
                 in_specs=[anywhere] * (len(pieces) + 1),
-                out_specs=(anywhere, anywhere),
+                out_specs=(anywhere,) * (len(cuts) + 1),
                 scratch_shapes=[
                     pltpu.VMEM((count, half_width), bf16),
                     pltpu.VMEM((cols, count), bf16),
                     pltpu.VMEM((owners, cols, LANES), bf16),
                     dma((len(blocks),)),
                     dma((2,)),
-                    dma((owners // 2,)),
+                    dma((owners,)),
                 ],
             ),
-            out_shape=(
-                jax.ShapeDtypeStruct((owners, cols, LANES), bf16),
-                jax.ShapeDtypeStruct((count, half_width), bf16),
-            ),
+            out_shape=(*cuts, jax.ShapeDtypeStruct((count, half_width), bf16)),
             compiler_params=pltpu.CompilerParams(vmem_limit_bytes=VMEM_LIMIT),
             cost_estimate=pl.CostEstimate(
                 flops=2 * count * half_width * cols, transcendentals=0, bytes_accessed=12 << 20
             ),
-        )(jnp.stack([spot[3] for spot in spots]).astype(jnp.int32), *pieces, cots)
+        )(jnp.stack([spot[3] for spot in spots] + owner_of).astype(jnp.int32), *pieces, cots)
 
     other0 = move(parts[0], 2, 0, 0)
     other1 = move(parts[1], 2, 0, 0)
-    cut0, rows0 = terms(gather(parts[0]) + gather(other0), single(y_hi, 0) + single(1 - y_hi, 10))
+    cut0, rows0 = terms(gather(parts[0]) + gather(other0), single(y_hi, 0) + single(1 - y_hi, 10), False)
     cut0 = lax.all_to_all(cut0, "dp", split_axis=0, concat_axis=0, tiled=True)
-    cut1, rows1 = terms(gather(jnp.concatenate([parts[1], other1], axis=0)), double(0))
-    cut1 = lax.all_to_all(cut1, "dp", split_axis=0, concat_axis=0, tiled=True)
+    *cut1, rows1 = terms(gather(jnp.concatenate([parts[1], other1], axis=0)), double(0), True)
+    for i, (dz, dy) in enumerate(steps[1:], 1):
+        cut1[i] = pass_on(cut1[i], dz, dy)
     shape = (owners, 2, LANES)
     feat_one, feat_two = pl.pallas_call(
         features_body,
@@ -416,13 +432,13 @@
     grad_one, grad_two = pl.pallas_call(
         sum_last_body,
         name="sum_last",
-        in_specs=[inside, inside],
+        in_specs=[inside] * (1 + owners),
         out_specs=(inside, inside),
         out_shape=(
             jax.ShapeDtypeStruct((2 * LANES, split), f32),
             jax.ShapeDtypeStruct((2 * LANES, cols - split), f32),
         ),
-    )(total0, cut1)
+    )(total0, *cut1)
     return feat_one, feat_two, grad_one, grad_two
 
 
@@ -453,6 +469,12 @@
             z, y_lo, y_hi, at_x, at_core = d // 32, d // 16 % 2, d // 8 % 2, d // 2 % 4, d % 2
             to_y = (y_hi * 2 + y_lo + y) % 4
             return z * 32 + to_y % 2 * 16 + to_y // 2 * 8 + (at_x + x) % 4 * 2 + (at_core + core) % 2
+
+        return lax.ppermute(array, axes, [(d, target(d)) for d in range(devices)])
+
+    def pass_on(array, z, y_lo):
+        def target(d):
+            return (d // 32 + z) % 4 * 32 + (d // 16 + y_lo) % 2 * 16 + d % 16
 
         return lax.ppermute(array, axes, [(d, target(d)) for d in range(devices)])
 
@@ -487,7 +509,13 @@
     )
     layer_out, *parts = combine(positions, gate_weights.T, returned.reshape(experts * capacity, sub, LANES))
     feat_one, feat_two, grad_one, grad_two = project(
-        parts, student_one, student_two, cots, move, (index // 8 % 2, index // 2 % 4, index % 2)
+        parts,
+        student_one,
+        student_two,
+        cots,
+        move,
+        pass_on,
+        (index // 32, index // 16 % 2, index // 8 % 2, index // 2 % 4, index % 2),
     )
     return (layer_out, feat_one, feat_two, grad_one, grad_two)
 

time: 267 us -> 267 us (level)
  waiting for transfers between devices: 71.5 us -> 62.6 us
  starting transfers between devices: 56.2 us -> 60.8 us
    ppermute x32, waiting for transfers between devices: 33.3 us -> 15.6 us  [move(): return lax.ppermute(array, axes, [(d, target(d)) for d in range(devices)])]
    ppermute x0 -> x7, waiting for transfers between devices: none -> 15 us  [pass_on(): return lax.ppermute(array, axes, [(d, target(d)) for d in range(devices)])]
    ppermute x0 -> x7, starting transfers between devices: none -> 7.93 us  [pass_on(): return lax.ppermute(array, axes, [(d, target(d)) for d in range(devices)])]
    all_to_all x1 -> x0, waiting for transfers between devices: 6.21 us -> none  [project(): cut1 = lax.all_to_all(cut1, 'dp', split_axis=0, concat_axis=0, tiled=True)]
    all_to_all x1 -> x0, starting transfers between devices: 5.07 us -> none  [project(): cut1 = lax.all_to_all(cut1, 'dp', split_axis=0, concat_axis=0, tiled=True)]
    unnamed x45 -> x53, local copies, waits for them, and re-layouts: 6.56 us -> 8.24 us
  transfers between devices with their start and end apart: 35 -> 41, of which waited for: 12 -> 11; matrix products, arithmetic and copies ran while one was open for 3% -> 4% of each run, Pallas kernels for 12% -> 13%
where the time goes in v5:
time: 267 us; the launch traced here: 266 us
  Pallas kernels  76.4 us (29%)
  waiting for transfers between devices  62.6 us (23%)
  starting transfers between devices  60.8 us (23%)
  blocking collectives  52.8 us (20%)
  local copies, waits for them, and re-layouts  10.5 us (4%)
    all_to_all x1, blocking collectives, local(): lax.all_to_all(expert_out.reshape(devices, capacity // 2, sub, LANES), ('...  52.8 us
    ppermute x32, starting transfers between devices, move(): return lax.ppermute(array, axes, [(d, target(d)) for d in range(devices)])  37.4 us
    all_to_all x1, waiting for transfers between devices, local(): lax.all_to_all(placed.reshape(devices, capacity // 2, sub, LANES), ('dp',...  32 us
    pallas_call x1, Pallas kernels, expert(): pl.pallas_call(functools.partial(expert_body, step=step, tile=tile, cols=...  29 us
    pallas_call x2, Pallas kernels, terms(): pl.pallas_call(functools.partial(terms_body, pieces=len(pieces), blocks=b...  18.8 us
    ppermute x32, waiting for transfers between devices, move(): return lax.ppermute(array, axes, [(d, target(d)) for d in range(devices)])  15.6 us
    ppermute x7, waiting for transfers between devices, pass_on(): return lax.ppermute(array, axes, [(d, target(d)) for d in range(devices)])  15 us
    pallas_call x1, Pallas kernels, project(): pl.pallas_call(features_body, name='features', in_specs=[anywhere] * 4, o...  12.2 us
  transfers between devices with their start and end apart: 41, of which 11 were waited for; matrix products, arithmetic and copies ran while one was open for 4% of the time, Pallas kernels for 13%

profile of v5, /device:TPU:1, one launch (start us, length us, event | category | flops | bytes accessed | tf_op | source)
XLA Modules:
  0.0 266.0 jit_solution(875174869651680322)
XLA Ops:
  0.6 5.7 %dispatch.1 = (bf16[896,16,128]{2,1,0:T(8,128)(2,1)}, s32[6,128]{1,0:T(8,128)}) custom-call(s32[6,128]{1,0:T(8,128)} %bitcast.50, bf16[128,2048]{1,0:T(8,128)(2,1)} %tok_ref.1, f32[1,2048]{1,0:T(1,128)} %bitcast.49), custom_call_target="tpu_custom_call" | custom-call | tf_op jit(solution)/shard_map/dispatch/pallas_call | solution.py:54
  6.3 11.9 %all-to-all-start = ((bf16[128,7,16,128]{3,2,1,0:T(8,128)(2,1)}), bf16[128,7,16,128]{3,2,1,0:T(8,128)(2,1)}, u32[]{:S(2)}, u32[]{:S(2)}) async-start(bf16[128,7,16,128]{3,2,1,0:T(8,128)(2,1)} %bitcast.48), calls=%async_computation | async-start | bytes 7340032 | tf_op jit(solution)/shard_map/all_to_all | solution.py:487
  20.6 3.1 %copy.17 = bf16[2048,512]{0,1:T(8,128)(2,1)S(1)} copy(bf16[2048,512]{1,0:T(8,128)(2,1)} %param.21) | data formatting | bytes 4194304 | tf_op args[10]
  25.6 3.2 %collective-permute-done.gate1 = bf16[704,2048]{1,0:T(8,128)(2,1)} collective-permute-done((bf16[704,2048]{1,0:T(8,128)(2,1)}, bf16[704,2048]{1,0:T(8,128)(2,1)}, u32[]{:S(2)}, u32[]{:S(2)}) %collective-permute-start) | collective-permute-done | bytes 2883616 | tf_op jit(solution)/shard_map/ppermute | solution.py:473
  28.8 4.1 %collective-permute-done.1.up1 = bf16[704,2048]{1,0:T(8,128)(2,1)} collective-permute-done((bf16[704,2048]{1,0:T(8,128)(2,1)}, bf16[704,2048]{1,0:T(8,128)(2,1)}, u32[]{:S(2)}, u32[]{:S(2)}) %collective-permute-start.1) | collective-permute-done | bytes 2883616 | tf_op jit(solution)/shard_map/ppermute | solution.py:473
  33.0 32.0 %all-to-all-done = bf16[128,7,16,128]{3,2,1,0:T(8,128)(2,1)} async-done(((bf16[128,7,16,128]{3,2,1,0:T(8,128)(2,1)}), bf16[128,7,16,128]{3,2,1,0:T(8,128)(2,1)}, u32[]{:S(2)}, u32[]{:S(2)}) %all-to-all-start) | async-done | bytes 3670048 | tf_op jit(solution)/shard_map/all_to_all | solution.py:487
  65.0 29.0 %expert.1 = bf16[896,16,128]{2,1,0:T(8,128)(2,1)} custom-call(bf16[896,16,128]{2,1,0:T(8,128)(2,1)} %bitcast.4.rows_hbm, bf16[704,2048]{1,0:T(8,128)(2,1)} %bitcast.6.gate0, bf16[704,2048]{1,0:T(8,128)(2,1)} %bitcast.8.up0, bf16[704,2048]{1,0:T(8,128)(2,1)} %bitcast.9.down0, bf16[704,2048]{1,0:T(8,128)(2,1)} %collective-permute-done.gate1, ...), custom_call_target="tpu_custom_call" | custom-call | tf_op jit(solution)/shard_map/expert/pallas_call | solution.py:172
  94.0 52.8 %all_to_all.15 = bf16[128,7,16,128]{3,2,1,0:T(8,128)(2,1)} all-to-all(bf16[128,7,16,128]{3,2,1,0:T(8,128)(2,1)} %bitcast.47), channel_id=1, replica_groups=mesh['dp'=8,'expert'=16] {'dp','expert'}, dimensions={0} | all-to-all | bytes 7340032 | tf_op jit(solution)/shard_map/all_to_all | solution.py:503
  146.8 5.6 %combine.1 = (bf16[128,2048]{1,0:T(8,128)(2,1)}, bf16[128,1024]{1,0:T(8,128)(2,1)}, bf16[128,1024]{1,0:T(8,128)(2,1)}) custom-call(s32[6,128]{1,0:T(8,128)} %get-tuple-element.27.pos_ref, f32[6,128]{1,0:T(8,128)} %bitcast.51, bf16[896,16,128]{2,1,0:T(8,128)(2,1)} %bitcast.46), custom_call_target="tpu_custom_call" | custom-call | tf_op jit(solution)/shard_map/combine/pallas_call | solution.py:92
  160.8 3.8 %collective-permute-start.17 = (bf16[128,1024]{1,0:T(8,128)(2,1)S(1)}, bf16[128,1024]{1,0:T(8,128)(2,1)S(1)}, u32[]{:S(2)}, u32[]{:S(2)}) collective-permute-start(bf16[128,1024]{1,0:T(8,128)(2,1)S(1)} %collective-permute-done.12.refs_10_), channel_id=1, source_target_pairs={{0,1},{1,0},{2,3},{3,2},{4,5},{5,4},{6,7},{7,6},{8,9},{9,8},{10,11... | collective-permute-start | bytes 786440 | tf_op jit(solution)/shard_map/ppermute | solution.py:473
  170.8 2.6 collective-permute-start.24
  177.7 4.2 %collective-permute-start.10 = (bf16[64,1024]{1,0:T(8,128)(2,1)S(1)}, bf16[64,1024]{1,0:T(8,128)(2,1)S(1)}, u32[]{:S(2)}, u32[]{:S(2)}) collective-permute-start(bf16[64,1024]{1,0:T(8,128)(2,1)S(1)} %collective-permute-done.5.refs_3_), channel_id=1, source_target_pairs={{0,1},{1,0},{2,3},{3,2},{4,5},{5,4},{6,7},{7,6},{8,9},{9,8},{10,11... | collective-permute-start | bytes 393224 | tf_op jit(solution)/shard_map/ppermute | solution.py:473
  184.1 4.3 %collective-permute-done.16.refs_14_ = bf16[64,1024]{1,0:T(8,128)(2,1)} collective-permute-done((bf16[64,1024]{1,0:T(8,128)(2,1)S(1)}, bf16[64,1024]{1,0:T(8,128)(2,1)}, u32[]{:S(2)}, u32[]{:S(2)}) %collective-permute-start.16) | collective-permute-done | bytes 131104 | tf_op jit(solution)/shard_map/ppermute | solution.py:473
  191.7 2.4 collective-permute-start.18
  198.2 9.3 %terms.2 = (bf16[8,768,128]{2,1,0:T(8,128)(2,1)}, bf16[2048,1024]{1,0:T(8,128)(2,1)}) custom-call(s32[28]{0:T(128)} %stack.142.at_ref, bf16[128,1024]{1,0:T(8,128)(2,1)} %get-tuple-element.31.refs_0_, bf16[128,1024]{1,0:T(8,128)(2,1)} %copy-done.12, bf16[128,1024]{1,0:T(8,128)(2,1)} %copy-done.11, bf16[64,1024]{1,0:T(8,128)(2,1)} %copy-done.22, ...), custom_call_target="tpu_custom_call" | custom-call | flops 3221225472 | bytes 12582912 | tf_op jit(solution)/shard_map/terms/pallas_call | solution.py:365
  207.6 3.6 %all-to-all-start.2 = ((bf16[8,768,128]{2,1,0:T(8,128)(2,1)}), bf16[8,768,128]{2,1,0:T(8,128)(2,1)S(1)}, u32[]{:S(2)}, u32[]{:S(2)}) async-start(bf16[8,768,128]{2,1,0:T(8,128)(2,1)} %get-tuple-element.38), calls=%async_computation.2 | async-start | bytes 3145728 | tf_op jit(solution)/shard_map/all_to_all | solution.py:398
  214.2 9.4 %terms.3 = (bf16[768,128]{1,0:T(8,128)(2,1)}, bf16[768,128]{1,0:T(8,128)(2,1)}, bf16[768,128]{1,0:T(8,128)(2,1)}, bf16[768,128]{1,0:T(8,128)(2,1)}, bf16[768,128...) custom-call(s32[24]{0:T(128)} %stack.143.at_ref, ...), custom_call_target="tpu_custom_call" | custom-call | flops 3221225472 | bytes 12582912 | tf_op jit(solution)/shard_map/terms/pallas_call | solution.py:365
  223.6 4.1 %collective-permute-start.32 = (bf16[768,128]{1,0:T(8,128)(2,1)}, bf16[768,128]{1,0:T(8,128)(2,1)S(1)}, u32[]{:S(2)}, u32[]{:S(2)}) collective-permute-start(bf16[768,128]{1,0:T(8,128)(2,1)} %get-tuple-element.40), channel_id=1, source_target_pairs={{0,80},{1,81},{2,82},{3,83},{4,84},{5,85},{6,86},{7,87},{8,88},{9,... | collective-permute-start | bytes 589832 | tf_op jit(solution)/shard_map/ppermute | solution.py:479
  229.1 2.4 collective-permute-start.35
  231.5 6.0 %collective-permute-done.32.refs_1_ = bf16[768,128]{1,0:T(8,128)(2,1)S(1)} collective-permute-done((bf16[768,128]{1,0:T(8,128)(2,1)}, bf16[768,128]{1,0:T(8,128)(2,1)S(1)}, u32[]{:S(2)}, u32[]{:S(2)}) %collective-permute-start.32) | collective-permute-done | bytes 196640 | tf_op jit(solution)/shard_map/ppermute | solution.py:479
  237.6 8.9 %collective-permute-done.33.refs_2_ = bf16[768,128]{1,0:T(8,128)(2,1)S(1)} collective-permute-done((bf16[768,128]{1,0:T(8,128)(2,1)}, bf16[768,128]{1,0:T(8,128)(2,1)S(1)}, u32[]{:S(2)}, u32[]{:S(2)}) %collective-permute-start.33) | collective-permute-done | bytes 196640 | tf_op jit(solution)/shard_map/ppermute | solution.py:479
  246.5 12.2 %features.1 = (bf16[2048,256]{1,0:T(8,128)(2,1)}, bf16[2048,512]{1,0:T(8,128)(2,1)}) custom-call(bf16[2048,1024]{1,0:T(8,128)(2,1)} %get-tuple-element.33.rows0, bf16[2048,1024]{1,0:T(8,128)(2,1)} %get-tuple-element.35.rows1, bf16[8,2,128,256]{3,2,1,0:T(8,128)(2,1)} %bitcast.53, bf16[8,2,128,512]{3,2,1,0:T(8,128)(2,1)} %bitcast.52), custom_call_target="tpu_custom_call" | custom-call | flops 6442450944 | bytes 14680064 | tf_op jit(solution)/shard_map/features/pallas_call | solution.py:403
  259.9 2.4 sum_first.1.first_ref
  263.3 2.7 sum_last.1
  (130 shorter events, 38.9 us)
Async XLA Ops:
  6.3 58.6 %all-to-all-start = ((bf16[128,7,16,128]{3,2,1,0:T(8,128)(2,1)}), bf16[128,7,16,128]{3,2,1,0:T(8,128)(2,1)}, u32[]{:S(2)}, u32[]{:S(2)}) async-start(bf16[128,7,16,128]{3,2,1,0:T(8,128)(2,1)} %bitcast.48), calls=%async_computation | async-start | bytes 7340032 | tf_op jit(solution)/shard_map/all_to_all | solution.py:487
  19.6 13.4 %collective-permute-start.1 = (bf16[704,2048]{1,0:T(8,128)(2,1)}, bf16[704,2048]{1,0:T(8,128)(2,1)}, u32[]{:S(2)}, u32[]{:S(2)}) collective-permute-start(bf16[704,2048]{1,0:T(8,128)(2,1)} %bitcast.8.up0), channel_id=1, source_target_pairs={{0,1},{1,0},{2,3},{3,2},{4,5},{5,4},{6,7},{7,6},{8,9},{9,8},{10,11... | collective-permute-start | bytes 8650760 | tf_op jit(solution)/shard_map/ppermute | solution.py:473
  153.2 11.4 %collective-permute-start.4 = (bf16[128,1024]{1,0:T(8,128)(2,1)}, bf16[128,1024]{1,0:T(8,128)(2,1)S(1)}, u32[]{:S(2)}, u32[]{:S(2)}) collective-permute-start(bf16[128,1024]{1,0:T(8,128)(2,1)} %get-tuple-element.31.refs_0_), channel_id=1, source_target_pairs={{0,6},{1,7},{2,0},{3,1},{4,2},{5,3},{6,4},{7,5},{8,14},{9,15},{10,... | collective-permute-start | bytes 786440 | tf_op jit(solution)/shard_map/ppermute | solution.py:473
  153.9 11.0 %collective-permute-start.3 = (bf16[128,1024]{1,0:T(8,128)(2,1)}, bf16[128,1024]{1,0:T(8,128)(2,1)S(1)}, u32[]{:S(2)}, u32[]{:S(2)}) collective-permute-start(bf16[128,1024]{1,0:T(8,128)(2,1)} %get-tuple-element.31.refs_0_), channel_id=1, source_target_pairs={{0,2},{1,3},{2,4},{3,5},{4,6},{5,7},{6,0},{7,1},{8,10},{9,11},{10,... | collective-permute-start | bytes 786440 | tf_op jit(solution)/shard_map/ppermute | solution.py:473
  154.7 11.8 %collective-permute-start.22 = (bf16[128,1024]{1,0:T(8,128)(2,1)}, bf16[128,1024]{1,0:T(8,128)(2,1)S(1)}, u32[]{:S(2)}, u32[]{:S(2)}) collective-permute-start(bf16[128,1024]{1,0:T(8,128)(2,1)} %get-tuple-element.34), channel_id=1, source_target_pairs={{0,8},{1,9},{2,10},{3,11},{4,12},{5,13},{6,14},{7,15},{8,0},{9,1},... | collective-permute-start | bytes 786440 | tf_op jit(solution)/shard_map/ppermute | solution.py:473
  156.9 13.1 %collective-permute-start.7 = (bf16[128,1024]{1,0:T(8,128)(2,1)}, bf16[128,1024]{1,0:T(8,128)(2,1)S(1)}, u32[]{:S(2)}, u32[]{:S(2)}) collective-permute-start(bf16[128,1024]{1,0:T(8,128)(2,1)} %get-tuple-element.31.refs_0_), channel_id=1, source_target_pairs={{0,1},{1,0},{2,3},{3,2},{4,5},{5,4},{6,7},{7,6},{8,9},{9,8},{10,11... | collective-permute-start | bytes 786440 | tf_op jit(solution)/shard_map/ppermute | solution.py:473
  160.8 12.6 %collective-permute-start.17 = (bf16[128,1024]{1,0:T(8,128)(2,1)S(1)}, bf16[128,1024]{1,0:T(8,128)(2,1)S(1)}, u32[]{:S(2)}, u32[]{:S(2)}) collective-permute-start(bf16[128,1024]{1,0:T(8,128)(2,1)S(1)} %collective-permute-done.12.refs_10_), channel_id=1, source_target_pairs={{0,1},{1,0},{2,3},{3,2},{4,5},{5,4},{6,7},{7,6},{8,9},{9,8},{10,11... | collective-permute-start | bytes 786440 | tf_op jit(solution)/shard_map/ppermute | solution.py:473
  170.8 23.3 %collective-permute-start.24 = (bf16[256,1024]{1,0:T(8,128)(2,1)}, bf16[256,1024]{1,0:T(8,128)(2,1)S(1)}, u32[]{:S(2)}, u32[]{:S(2)}) collective-permute-start(bf16[256,1024]{1,0:T(8,128)(2,1)} %constant_dynamic-update-slice_fusion.refs_0_), channel_id=1, source_target_pairs={{0,6},{1,7},{2,0},{3,1},{4,2},{5,3},{6,4},{7,5},{8,14},{9,15},{10,... | collective-permute-start | bytes 1572872 | tf_op jit(solution)/shard_map/ppermute | solution.py:473
  173.4 20.8 %collective-permute-start.23 = (bf16[256,1024]{1,0:T(8,128)(2,1)}, bf16[256,1024]{1,0:T(8,128)(2,1)S(1)}, u32[]{:S(2)}, u32[]{:S(2)}) collective-permute-start(bf16[256,1024]{1,0:T(8,128)(2,1)} %constant_dynamic-update-slice_fusion.refs_0_), channel_id=1, source_target_pairs={{0,2},{1,3},{2,4},{3,5},{4,6},{5,7},{6,0},{7,1},{8,10},{9,11},{10,... | collective-permute-start | bytes 1572872 | tf_op jit(solution)/shard_map/ppermute | solution.py:473
  182.0 9.6 %collective-permute-start.15 = (bf16[64,1024]{1,0:T(8,128)(2,1)S(1)}, bf16[64,1024]{1,0:T(8,128)(2,1)}, u32[]{:S(2)}, u32[]{:S(2)}) collective-permute-start(bf16[64,1024]{1,0:T(8,128)(2,1)S(1)} %slice.26), channel_id=1, source_target_pairs={{0,2},{1,3},{2,4},{3,5},{4,6},{5,7},{6,0},{7,1},{8,10},{9,11},{10,... | collective-permute-start | bytes 393224 | tf_op jit(solution)/shard_map/ppermute | solution.py:473
  183.6 11.9 %collective-permute-start.8 = (bf16[128,1024]{1,0:T(8,128)(2,1)S(1)}, bf16[128,1024]{1,0:T(8,128)(2,1)}, u32[]{:S(2)}, u32[]{:S(2)}) collective-permute-start(bf16[128,1024]{1,0:T(8,128)(2,1)S(1)} %collective-permute-done.3.refs_1_), channel_id=1, source_target_pairs={{0,1},{1,0},{2,3},{3,2},{4,5},{5,4},{6,7},{7,6},{8,9},{9,8},{10,11... | collective-permute-start | bytes 786440 | tf_op jit(solution)/shard_map/ppermute | solution.py:473
  195.4 17.1 %collective-permute-start.27 = (bf16[256,1024]{1,0:T(8,128)(2,1)}, bf16[256,1024]{1,0:T(8,128)(2,1)}, u32[]{:S(2)}, u32[]{:S(2)}) collective-permute-start(bf16[256,1024]{1,0:T(8,128)(2,1)} %constant_dynamic-update-slice_fusion.refs_0_), channel_id=1, source_target_pairs={{0,1},{1,0},{2,3},{3,2},{4,5},{5,4},{6,7},{7,6},{8,9},{9,8},{10,11... | collective-permute-start | bytes 1572872 | tf_op jit(solution)/shard_map/ppermute | solution.py:473
  195.8 15.4 %collective-permute-start.26 = (bf16[128,1024]{1,0:T(8,128)(2,1)S(1)}, bf16[128,1024]{1,0:T(8,128)(2,1)}, u32[]{:S(2)}, u32[]{:S(2)}) collective-permute-start(bf16[128,1024]{1,0:T(8,128)(2,1)S(1)} %slice.29), channel_id=1, source_target_pairs={{0,6},{1,7},{2,0},{3,1},{4,2},{5,3},{6,4},{7,5},{8,14},{9,15},{10,... | collective-permute-start | bytes 786440 | tf_op jit(solution)/shard_map/ppermute | solution.py:473
  195.8 15.9 %collective-permute-start.25 = (bf16[128,1024]{1,0:T(8,128)(2,1)S(1)}, bf16[128,1024]{1,0:T(8,128)(2,1)}, u32[]{:S(2)}, u32[]{:S(2)}) collective-permute-start(bf16[128,1024]{1,0:T(8,128)(2,1)S(1)} %slice.28), channel_id=1, source_target_pairs={{0,2},{1,3},{2,4},{3,5},{4,6},{5,7},{6,0},{7,1},{8,10},{9,11},{10,... | collective-permute-start | bytes 786440 | tf_op jit(solution)/shard_map/ppermute | solution.py:473
  197.3 15.8 %collective-permute-start.29 = (bf16[256,1024]{1,0:T(8,128)(2,1)S(1)}, bf16[256,1024]{1,0:T(8,128)(2,1)}, u32[]{:S(2)}, u32[]{:S(2)}) collective-permute-start(bf16[256,1024]{1,0:T(8,128)(2,1)S(1)} %collective-permute-done.24.refs_2_), channel_id=1, source_target_pairs={{0,1},{1,0},{2,3},{3,2},{4,5},{5,4},{6,7},{7,6},{8,9},{9,8},{10,11... | collective-permute-start | bytes 1572872 | tf_op jit(solution)/shard_map/ppermute | solution.py:473
  198.1 15.4 %collective-permute-start.28 = (bf16[256,1024]{1,0:T(8,128)(2,1)S(1)}, bf16[256,1024]{1,0:T(8,128)(2,1)}, u32[]{:S(2)}, u32[]{:S(2)}) collective-permute-start(bf16[256,1024]{1,0:T(8,128)(2,1)S(1)} %collective-permute-done.23.refs_1_), channel_id=1, source_target_pairs={{0,1},{1,0},{2,3},{3,2},{4,5},{5,4},{6,7},{7,6},{8,9},{9,8},{10,11... | collective-permute-start | bytes 1572872 | tf_op jit(solution)/shard_map/ppermute | solution.py:473
  207.6 51.2 %all-to-all-start.2 = ((bf16[8,768,128]{2,1,0:T(8,128)(2,1)}), bf16[8,768,128]{2,1,0:T(8,128)(2,1)S(1)}, u32[]{:S(2)}, u32[]{:S(2)}) async-start(bf16[8,768,128]{2,1,0:T(8,128)(2,1)} %get-tuple-element.38), calls=%async_computation.2 | async-start | bytes 3145728 | tf_op jit(solution)/shard_map/all_to_all | solution.py:398
  223.6 13.9 %collective-permute-start.32 = (bf16[768,128]{1,0:T(8,128)(2,1)}, bf16[768,128]{1,0:T(8,128)(2,1)S(1)}, u32[]{:S(2)}, u32[]{:S(2)}) collective-permute-start(bf16[768,128]{1,0:T(8,128)(2,1)} %get-tuple-element.40), channel_id=1, source_target_pairs={{0,80},{1,81},{2,82},{3,83},{4,84},{5,85},{6,86},{7,87},{8,88},{9,... | collective-permute-start | bytes 589832 | tf_op jit(solution)/shard_map/ppermute | solution.py:479
  227.6 18.8 %collective-permute-start.33 = (bf16[768,128]{1,0:T(8,128)(2,1)}, bf16[768,128]{1,0:T(8,128)(2,1)S(1)}, u32[]{:S(2)}, u32[]{:S(2)}) collective-permute-start(bf16[768,128]{1,0:T(8,128)(2,1)} %get-tuple-element.41), channel_id=1, source_target_pairs={{0,64},{1,65},{2,66},{3,67},{4,68},{5,69},{6,70},{7,71},{8,72},{9,... | collective-permute-start | bytes 589832 | tf_op jit(solution)/shard_map/ppermute | solution.py:479
  227.9 34.5 %collective-permute-start.34 = (bf16[768,128]{1,0:T(8,128)(2,1)}, bf16[768,128]{1,0:T(8,128)(2,1)S(1)}, u32[]{:S(2)}, u32[]{:S(2)}) collective-permute-start(bf16[768,128]{1,0:T(8,128)(2,1)} %get-tuple-element.42), channel_id=1, source_target_pairs={{0,48},{1,49},{2,50},{3,51},{4,52},{5,53},{6,54},{7,55},{8,56},{9,... | collective-permute-start | bytes 589832 | tf_op jit(solution)/shard_map/ppermute | solution.py:479
  229.1 33.3 %collective-permute-start.35 = (bf16[768,128]{1,0:T(8,128)(2,1)}, bf16[768,128]{1,0:T(8,128)(2,1)S(1)}, u32[]{:S(2)}, u32[]{:S(2)}) collective-permute-start(bf16[768,128]{1,0:T(8,128)(2,1)} %get-tuple-element.43), channel_id=1, source_target_pairs={{0,112},{1,113},{2,114},{3,115},{4,116},{5,117},{6,118},{7,119},{8... | collective-permute-start | bytes 589832 | tf_op jit(solution)/shard_map/ppermute | solution.py:479
  231.5 30.9 %collective-permute-start.36 = (bf16[768,128]{1,0:T(8,128)(2,1)}, bf16[768,128]{1,0:T(8,128)(2,1)S(1)}, u32[]{:S(2)}, u32[]{:S(2)}) collective-permute-start(bf16[768,128]{1,0:T(8,128)(2,1)} %get-tuple-element.44), channel_id=1, source_target_pairs={{0,32},{1,33},{2,34},{3,35},{4,36},{5,37},{6,38},{7,39},{8,40},{9,... | collective-permute-start | bytes 589832 | tf_op jit(solution)/shard_map/ppermute | solution.py:479
  237.5 24.9 %collective-permute-start.37 = (bf16[768,128]{1,0:T(8,128)(2,1)}, bf16[768,128]{1,0:T(8,128)(2,1)S(1)}, u32[]{:S(2)}, u32[]{:S(2)}) collective-permute-start(bf16[768,128]{1,0:T(8,128)(2,1)} %get-tuple-element.45), channel_id=1, source_target_pairs={{0,96},{1,97},{2,98},{3,99},{4,100},{5,101},{6,102},{7,103},{8,104... | collective-permute-start | bytes 589832 | tf_op jit(solution)/shard_map/ppermute | solution.py:479
  246.5 15.9 %collective-permute-start.38 = (bf16[768,128]{1,0:T(8,128)(2,1)}, bf16[768,128]{1,0:T(8,128)(2,1)S(1)}, u32[]{:S(2)}, u32[]{:S(2)}) collective-permute-start(bf16[768,128]{1,0:T(8,128)(2,1)} %get-tuple-element.46), channel_id=1, source_target_pairs={{0,16},{1,17},{2,18},{3,19},{4,20},{5,21},{6,22},{7,23},{8,24},{9,... | collective-permute-start | bytes 589832 | tf_op jit(solution)/shard_map/ppermute | solution.py:479
  (42 other events, 472.3 us)

commit v6 on v5

--- a/solution.py
+++ b/solution.py
@@ -194,9 +194,9 @@
 VMEM_LIMIT = 60 * 1024 * 1024
 
 
-def terms_body(at_ref, *refs, pieces, blocks, scale, apart):
+def terms_body(at_ref, *refs, pieces, blocks, scale):
     parts = refs[:pieces]
-    cot_hbm, *out_hbm, all_rows, rows_ref, cot_ref, cut_ref, sem, side_sem, out_sem = refs[pieces:]
+    cot_hbm, out_hbm, all_rows, rows_ref, cot_ref, cut_ref, sem, side_sem, out_sem = refs[pieces:]
     loads = []
     for i, (piece, start, size) in enumerate(blocks):
         to = pl.ds(pl.multiple_of(at_ref[i], size), size)
@@ -220,17 +220,74 @@
         return carry
 
     lax.fori_loop(0, owners // 2, step, 0)
-    if apart:
+    out = pltpu.make_async_copy(cut_ref, out_hbm, out_sem)
+    out.start()
+    out.wait()
+    keep.wait()
+
+
+def part_body(at_ref, *refs, pieces, blocks, scale, last):
+    parts = refs[:pieces]
+    if last:
+        cot_hbm, near_hbm, _, *out_hbm, all_rows = refs[pieces : pieces + 12]
+    else:
+        cot_hbm, near_hbm, all_rows = refs[pieces : pieces + 3]
+    rows_ref, cot_ref, acc_ref, cut_ref, sem, cot_sem, keep_sem, acc_sem, out_sem = refs[-9:]
+    size = LANES
+    loads, cot_loads, keeps = [], [], []
+    for i, (piece, start, _) in enumerate(blocks):
+        to = pl.ds(pl.multiple_of(at_ref[i], size), size)
+        here = pl.ds(i * size, size)
+        loads.append(pltpu.make_async_copy(parts[piece].at[pl.ds(start, size)], rows_ref.at[here], sem.at[i]))
+        cot_loads.append(pltpu.make_async_copy(cot_hbm.at[:, to], cot_ref.at[:, here], cot_sem.at[i]))
+        keeps.append(pltpu.make_async_copy(rows_ref.at[here], all_rows.at[to], keep_sem.at[i]))
+    owners = cut_ref.shape[0]
+    wide = 2 * LANES
+    for c in loads + cot_loads:
+        c.start()
+
+    def sums(d):
+        at = pl.ds(d * wide if isinstance(d, int) else pl.multiple_of(d * wide, wide), wide)
+        ends = (near_hbm.at[:, at], acc_ref.at[:, at]) if last else (acc_ref.at[:, at], near_hbm.at[:, at])
+        return pltpu.make_async_copy(*ends, acc_sem.at[d])
+
+    if last:
+        for d in range(owners // 2):
+            sums(d).start()
+    for c in loads:
+        c.wait()
+    for c in keeps:
+        c.start()
+    for c in cot_loads:
+        c.wait()
+
+    def step(d, carry):
+        at = pl.ds(pl.multiple_of(d * wide, wide), wide)
+        terms = jnp.dot(cot_ref[...], rows_ref[:, at], preferred_element_type=jnp.float32)
+        if last:
+            sums(d).wait()
+            terms = (terms + acc_ref[:, at]) * scale
+            cut_ref[2 * d] = terms[:, :LANES].astype(jnp.bfloat16)
+            cut_ref[2 * d + 1] = terms[:, LANES:].astype(jnp.bfloat16)
+        else:
+            acc_ref[:, at] = terms
+            sums(d).start()
+        return carry
+
+    lax.fori_loop(0, owners // 2, step, 0)
+    if last:
         outs = [
             pltpu.make_async_copy(cut_ref.at[at_ref[len(blocks) + i]], out, out_sem.at[i]) for i, out in enumerate(out_hbm)
         ]
+        for c in outs:
+            c.start()
+        for c in outs:
+            c.wait()
     else:
-        outs = [pltpu.make_async_copy(cut_ref, out_hbm[0], out_sem.at[0])]
-    for c in outs:
-        c.start()
-    for c in outs:
+        for d in range(owners // 2):
+            sums(d).wait()
+    for c in keeps:
         c.wait()
-    keep.wait()
 
 
 def features_body(rows0, rows1, one_hbm, two_hbm, feat_one, feat_two, rows_ref, one_ref, two_ref, out_one, out_two, sem, row_sem, out_sem):
@@ -357,46 +414,72 @@
     steps = [(0, 0), (2, 1), (2, 0), (1, 1), (3, 1), (1, 0), (3, 0), (0, 1)]
     owner_of = [(z + dz) % 4 * 2 + (y_lo + dy) % 2 for dz, dy in steps]
 
-    def terms(pieces, spots, apart):
-        cuts = (owners * [jax.ShapeDtypeStruct((cols, LANES), bf16)]) if apart else [
-            jax.ShapeDtypeStruct((owners, cols, LANES), bf16)
-        ]
-        blocks = tuple(spot[:3] for spot in spots)
+    scale = 1.0 / math.sqrt(count * owners)
+
+    def call(body, pieces, spots, others, outs, scratch, aliases, flops):
+        rows_of = jnp.stack([spot[3] for spot in spots] + owner_of).astype(jnp.int32)
         return pl.pallas_call(
-            functools.partial(
-                terms_body,
-                pieces=len(pieces),
-                blocks=blocks,
-                scale=1.0 / math.sqrt(count * owners),
-                apart=apart,
-            ),
-            name="terms",
+            functools.partial(body, pieces=len(pieces), blocks=tuple(spot[:3] for spot in spots), scale=scale),
             grid_spec=pltpu.PrefetchScalarGridSpec(
                 num_scalar_prefetch=1,
                 grid=(1,),
-                in_specs=[anywhere] * (len(pieces) + 1),
-                out_specs=(anywhere,) * (len(cuts) + 1),
-                scratch_shapes=[
-                    pltpu.VMEM((count, half_width), bf16),
-                    pltpu.VMEM((cols, count), bf16),
-                    pltpu.VMEM((owners, cols, LANES), bf16),
-                    dma((len(blocks),)),
-                    dma((2,)),
-                    dma((owners,)),
-                ],
+                in_specs=[anywhere] * (len(pieces) + len(others)),
+                out_specs=(anywhere,) * len(outs),
+                scratch_shapes=scratch,
             ),
-            out_shape=(*cuts, jax.ShapeDtypeStruct((count, half_width), bf16)),
+            out_shape=outs,
+            input_output_aliases=aliases,
             compiler_params=pltpu.CompilerParams(vmem_limit_bytes=VMEM_LIMIT),
-            cost_estimate=pl.CostEstimate(
-                flops=2 * count * half_width * cols, transcendentals=0, bytes_accessed=12 << 20
-            ),
-        )(jnp.stack([spot[3] for spot in spots] + owner_of).astype(jnp.int32), *pieces, cots)
+            cost_estimate=pl.CostEstimate(flops=flops, transcendentals=0, bytes_accessed=10 << 20),
+        )(rows_of, *pieces, *others)
+
+    rows_shape = jax.ShapeDtypeStruct((count, half_width), bf16)
+    near_shape = jax.ShapeDtypeStruct((cols, half_width), f32)
+    cut_vmem = pltpu.VMEM((owners, cols, LANES), bf16)
+
+    def terms(pieces, spots):
+        scratch = [pltpu.VMEM((count, half_width), bf16), pltpu.VMEM((cols, count), bf16), cut_vmem]
+        return call(
+            terms_body,
+            pieces,
+            spots,
+            [cots],
+            (jax.ShapeDtypeStruct((owners, cols, LANES), bf16), rows_shape),
+            scratch + [dma((len(spots),)), dma((2,)), dma],
+            {},
+            2 * count * half_width * cols,
+        )
+
+    def part(pieces, spots, others, outs, aliases, last):
+        number = len(spots)
+        scratch = [
+            pltpu.VMEM((number * LANES, half_width), bf16),
+            pltpu.VMEM((cols, number * LANES), bf16),
+            pltpu.VMEM((cols, half_width), f32),
+            cut_vmem,
+        ]
+        scratch += [dma((number,)), dma((number,)), dma((number,)), dma((owners // 2,)), dma((owners,))]
+        body = functools.partial(part_body, last=last)
+        return call(body, pieces, spots, others, outs, scratch, aliases, 2 * number * LANES * half_width * cols)
 
     other0 = move(parts[0], 2, 0, 0)
     other1 = move(parts[1], 2, 0, 0)
-    cut0, rows0 = terms(gather(parts[0]) + gather(other0), single(y_hi, 0) + single(1 - y_hi, 10), False)
+    cut0, rows0 = terms(gather(parts[0]) + gather(other0), single(y_hi, 0) + single(1 - y_hi, 10))
     cut0 = lax.all_to_all(cut0, "dp", split_axis=0, concat_axis=0, tiled=True)
-    *cut1, rows1 = terms(gather(jnp.concatenate([parts[1], other1], axis=0)), double(0), True)
+    pieces, spots = gather(jnp.concatenate([parts[1], other1], axis=0)), double(0)
+    at_once = [spot for spot in spots if spot[0] % 5 < 3]
+    later = [(spot[0] // 5 * 2 + spot[0] % 5 - 3, *spot[1:]) for spot in spots if spot[0] % 5 >= 3]
+    near_pieces = pieces[0:3] + pieces[5:8]
+    at_once = [(spot[0] // 5 * 3 + spot[0] % 5, *spot[1:]) for spot in at_once]
+    near_terms, rows1 = part(near_pieces, at_once, [cots], (near_shape, rows_shape), {}, False)
+    *cut1, rows1 = part(
+        pieces[3:5] + pieces[8:10],
+        later,
+        [cots, near_terms, rows1],
+        owners * (jax.ShapeDtypeStruct((cols, LANES), bf16),) + (rows_shape,),
+        {7: owners},
+        True,
+    )
     for i, (dz, dy) in enumerate(steps[1:], 1):
         cut1[i] = pass_on(cut1[i], dz, dy)
     shape = (owners, 2, LANES)

time: 267 us -> 267 us (level)
  waiting for transfers between devices: 62.6 us -> 54.8 us
  Pallas kernels: 76.4 us -> 80.8 us
    ppermute x7, waiting for transfers between devices: 15 us -> 9.04 us  [pass_on(): return lax.ppermute(array, axes, [(d, target(d)) for d in range(devices)])]
    pallas_call x2 -> x3, Pallas kernels: 18.8 us -> 23.1 us  [call(): pl.pallas_call(functools.partial(body, pieces=len(pieces), blocks=tuple((...]
    ppermute x7, starting transfers between devices: 7.93 us -> 11.1 us  [pass_on(): return lax.ppermute(array, axes, [(d, target(d)) for d in range(devices)])]
    unnamed x53 -> x55, local copies, waits for them, and re-layouts: 8.24 us -> 9.2 us
  transfers between devices with their start and end apart: 41 -> 41, of which waited for: 11 -> 9; matrix products, arithmetic and copies ran while one was open for 4% -> 4% of each run, Pallas kernels for 13% -> 14%
where the time goes in v6:
time: 267 us; the launch traced here: 266 us
  Pallas kernels  80.8 us (30%)
  starting transfers between devices  62.2 us (23%)
  waiting for transfers between devices  54.8 us (21%)
  blocking collectives  52.8 us (20%)
  local copies, waits for them, and re-layouts  12.9 us (5%)
    all_to_all x1, blocking collectives, local(): lax.all_to_all(expert_out.reshape(devices, capacity // 2, sub, LANES), ('...  52.8 us
    ppermute x32, starting transfers between devices, move(): return lax.ppermute(array, axes, [(d, target(d)) for d in range(devices)])  35.6 us
    all_to_all x1, waiting for transfers between devices, local(): lax.all_to_all(placed.reshape(devices, capacity // 2, sub, LANES), ('dp',...  32 us
    pallas_call x1, Pallas kernels, expert(): pl.pallas_call(functools.partial(expert_body, step=step, tile=tile, cols=...  29.1 us
    pallas_call x3, Pallas kernels, call(): pl.pallas_call(functools.partial(body, pieces=len(pieces), blocks=tuple((...  23.1 us
    ppermute x32, waiting for transfers between devices, move(): return lax.ppermute(array, axes, [(d, target(d)) for d in range(devices)])  13.8 us
    pallas_call x1, Pallas kernels, project(): pl.pallas_call(features_body, name='features', in_specs=[anywhere] * 4, o...  12.2 us
    all_to_all x1, starting transfers between devices, local(): lax.all_to_all(placed.reshape(devices, capacity // 2, sub, LANES), ('dp',...  11.9 us
  transfers between devices with their start and end apart: 41, of which 9 were waited for; matrix products, arithmetic and copies ran while one was open for 4% of the time, Pallas kernels for 14%

profile of v6, /device:TPU:1, one launch (start us, length us, event | category | flops | bytes accessed | tf_op | source)
XLA Modules:
  0.0 266.4 jit_solution(4018808899232659569)
XLA Ops:
  0.6 5.7 %dispatch.1 = (bf16[896,16,128]{2,1,0:T(8,128)(2,1)}, s32[6,128]{1,0:T(8,128)}) custom-call(s32[6,128]{1,0:T(8,128)} %bitcast.50, bf16[128,2048]{1,0:T(8,128)(2,1)} %tok_ref.1, f32[1,2048]{1,0:T(1,128)} %bitcast.49), custom_call_target="tpu_custom_call" | custom-call | tf_op jit(solution)/shard_map/dispatch/pallas_call | solution.py:54
  6.3 11.9 %all-to-all-start = ((bf16[128,7,16,128]{3,2,1,0:T(8,128)(2,1)}), bf16[128,7,16,128]{3,2,1,0:T(8,128)(2,1)}, u32[]{:S(2)}, u32[]{:S(2)}) async-start(bf16[128,7,16,128]{3,2,1,0:T(8,128)(2,1)} %bitcast.48), calls=%async_computation | async-start | bytes 7340032 | tf_op jit(solution)/shard_map/all_to_all | solution.py:570
  20.0 2.9 %copy.18 = bf16[2048,512]{0,1:T(8,128)(2,1)S(1)} copy(bf16[2048,512]{1,0:T(8,128)(2,1)} %param.21) | data formatting | bytes 4194304 | tf_op args[10]
  26.4 2.4 collective-permute-done.gate1
  28.8 4.1 %collective-permute-done.1.up1 = bf16[704,2048]{1,0:T(8,128)(2,1)} collective-permute-done((bf16[704,2048]{1,0:T(8,128)(2,1)}, bf16[704,2048]{1,0:T(8,128)(2,1)}, u32[]{:S(2)}, u32[]{:S(2)}) %collective-permute-start.1) | collective-permute-done | bytes 2883616 | tf_op jit(solution)/shard_map/ppermute | solution.py:556
  33.0 32.0 %all-to-all-done = bf16[128,7,16,128]{3,2,1,0:T(8,128)(2,1)} async-done(((bf16[128,7,16,128]{3,2,1,0:T(8,128)(2,1)}), bf16[128,7,16,128]{3,2,1,0:T(8,128)(2,1)}, u32[]{:S(2)}, u32[]{:S(2)}) %all-to-all-start) | async-done | bytes 3670048 | tf_op jit(solution)/shard_map/all_to_all | solution.py:570
  65.0 29.1 %expert.1 = bf16[896,16,128]{2,1,0:T(8,128)(2,1)} custom-call(bf16[896,16,128]{2,1,0:T(8,128)(2,1)} %bitcast.4.rows_hbm, bf16[704,2048]{1,0:T(8,128)(2,1)} %bitcast.6.gate0, bf16[704,2048]{1,0:T(8,128)(2,1)} %bitcast.8.up0, bf16[704,2048]{1,0:T(8,128)(2,1)} %bitcast.9.down0, bf16[704,2048]{1,0:T(8,128)(2,1)} %collective-permute-done.gate1, ...), custom_call_target="tpu_custom_call" | custom-call | tf_op jit(solution)/shard_map/expert/pallas_call | solution.py:172
  94.0 52.8 %all_to_all.15 = bf16[128,7,16,128]{3,2,1,0:T(8,128)(2,1)} all-to-all(bf16[128,7,16,128]{3,2,1,0:T(8,128)(2,1)} %bitcast.47), channel_id=1, replica_groups=mesh['dp'=8,'expert'=16] {'dp','expert'}, dimensions={0} | all-to-all | bytes 7340032 | tf_op jit(solution)/shard_map/all_to_all | solution.py:586
  146.9 5.6 %combine.1 = (bf16[128,2048]{1,0:T(8,128)(2,1)}, bf16[128,1024]{1,0:T(8,128)(2,1)}, bf16[128,1024]{1,0:T(8,128)(2,1)}) custom-call(s32[6,128]{1,0:T(8,128)} %get-tuple-element.29.pos_ref, f32[6,128]{1,0:T(8,128)} %bitcast.51, bf16[896,16,128]{2,1,0:T(8,128)(2,1)} %bitcast.46), custom_call_target="tpu_custom_call" | custom-call | tf_op jit(solution)/shard_map/combine/pallas_call | solution.py:92
  153.2 2.7 %collective-permute-start.4 = (bf16[128,1024]{1,0:T(8,128)(2,1)}, bf16[128,1024]{1,0:T(8,128)(2,1)S(1)}, u32[]{:S(2)}, u32[]{:S(2)}) collective-permute-start(bf16[128,1024]{1,0:T(8,128)(2,1)} %get-tuple-element.33.refs_0_), channel_id=1, source_target_pairs={{0,6},{1,7},{2,0},{3,1},{4,2},{5,3},{6,4},{7,5},{8,14},{9,15},{10,... | collective-permute-start | bytes 786440 | tf_op jit(solution)/shard_map/ppermute | solution.py:556
  164.0 2.5 collective-permute-done.22
  170.8 2.7 collective-permute-start.25
  183.6 3.2 %collective-permute-done.15.refs_13_ = bf16[64,1024]{1,0:T(8,128)(2,1)} collective-permute-done((bf16[64,1024]{1,0:T(8,128)(2,1)S(1)}, bf16[64,1024]{1,0:T(8,128)(2,1)}, u32[]{:S(2)}, u32[]{:S(2)}) %collective-permute-start.15) | collective-permute-done | bytes 131104 | tf_op jit(solution)/shard_map/ppermute | solution.py:556
  186.8 2.6 collective-permute-start.18
  193.4 3.3 %collective-permute-start.26 = (bf16[128,1024]{1,0:T(8,128)(2,1)S(1)}, bf16[128,1024]{1,0:T(8,128)(2,1)S(1)}, u32[]{:S(2)}, u32[]{:S(2)}) collective-permute-start(bf16[128,1024]{1,0:T(8,128)(2,1)S(1)} %slice.29), channel_id=1, source_target_pairs={{0,6},{1,7},{2,0},{3,1},{4,2},{5,3},{6,4},{7,5},{8,14},{9,15},{10,... | collective-permute-start | bytes 786440 | tf_op jit(solution)/shard_map/ppermute | solution.py:556
  197.3 9.2 %shard_map.146 = (bf16[8,768,128]{2,1,0:T(8,128)(2,1)}, bf16[2048,1024]{1,0:T(8,128)(2,1)}) custom-call(s32[28]{0:T(128)} %stack.153.at_ref, bf16[128,1024]{1,0:T(8,128)(2,1)} %get-tuple-element.33.refs_0_, bf16[128,1024]{1,0:T(8,128)(2,1)} %copy-done.13, bf16[128,1024]{1,0:T(8,128)(2,1)} %copy-done.14, bf16[64,1024]{1,0:T(8,128)(2,1)} %copy-done.22, ...), custom_call_target="tpu_custom_call" | custom-call | flops 3221225472 | bytes 10485760 | tf_op jit(solution)/shard_map/pallas_call | solution.py:421
  206.5 3.6 %all-to-all-start.2 = ((bf16[8,768,128]{2,1,0:T(8,128)(2,1)}), bf16[8,768,128]{2,1,0:T(8,128)(2,1)S(1)}, u32[]{:S(2)}, u32[]{:S(2)}) async-start(bf16[8,768,128]{2,1,0:T(8,128)(2,1)} %get-tuple-element.42), calls=%async_computation.2 | async-start | bytes 3145728 | tf_op jit(solution)/shard_map/all_to_all | solution.py:468
  212.1 7.8 %shard_map.147 = (f32[768,1024]{1,0:T(8,128)}, bf16[2048,1024]{1,0:T(8,128)(2,1)}) custom-call(s32[20]{0:T(128)} %stack.155.at_ref, bf16[256,1024]{1,0:T(8,128)(2,1)} %constant_dynamic-update-slice_fusion.refs_0_, bf16[256,1024]{1,0:T(8,128)(2,1)} %copy-done.12, bf16[256,1024]{1,0:T(8,128)(2,1)} %collective-permute-done.25.refs_2_, ...), custom_call_target="tpu_custom_call" | custom-call | flops 2415919104 | bytes 10485760 | tf_op jit(solution)/shard_map/pallas_call | solution.py:421
  220.8 6.1 %shard_map.148 = (bf16[768,128]{1,0:T(8,128)(2,1)}, bf16[768,128]{1,0:T(8,128)(2,1)}, bf16[768,128]{1,0:T(8,128)(2,1)}, bf16[768,128]{1,0:T(8,128)(2,1)}, bf16[7...) custom-call(s32[12]{0:T(128)} %stack.154.at_ref, ...), custom_call_target="tpu_custom_call", output_to_operand_aliasing={{8}: (7, {})} | custom-call | flops 805306368 | bytes 10485760 | tf_op jit(solution)/shard_map/pallas_call | solution.py:421
  226.8 4.1 %collective-permute-start.32 = (bf16[768,128]{1,0:T(8,128)(2,1)}, bf16[768,128]{1,0:T(8,128)(2,1)S(1)}, u32[]{:S(2)}, u32[]{:S(2)}) collective-permute-start(bf16[768,128]{1,0:T(8,128)(2,1)} %get-tuple-element.44), channel_id=1, source_target_pairs={{0,80},{1,81},{2,82},{3,83},{4,84},{5,85},{6,86},{7,87},{8,88},{9,... | collective-permute-start | bytes 589832 | tf_op jit(solution)/shard_map/ppermute | solution.py:562
  238.5 7.2 %collective-permute-done.33.refs_2_ = bf16[768,128]{1,0:T(8,128)(2,1)S(1)} collective-permute-done((bf16[768,128]{1,0:T(8,128)(2,1)}, bf16[768,128]{1,0:T(8,128)(2,1)S(1)}, u32[]{:S(2)}, u32[]{:S(2)}) %collective-permute-start.33) | collective-permute-done | bytes 196640 | tf_op jit(solution)/shard_map/ppermute | solution.py:562
  247.0 12.2 %features.1 = (bf16[2048,256]{1,0:T(8,128)(2,1)}, bf16[2048,512]{1,0:T(8,128)(2,1)}) custom-call(bf16[2048,1024]{1,0:T(8,128)(2,1)} %get-tuple-element.35.rows0, bf16[2048,1024]{1,0:T(8,128)(2,1)} %get-tuple-element.39.rows1, bf16[8,2,128,256]{3,2,1,0:T(8,128)(2,1)} %bitcast.53, bf16[8,2,128,512]{3,2,1,0:T(8,128)(2,1)} %bitcast.52), custom_call_target="tpu_custom_call" | custom-call | flops 6442450944 | bytes 14680064 | tf_op jit(solution)/shard_map/features/pallas_call | solution.py:486
  260.4 2.4 sum_first.1.first_ref
  263.8 2.7 sum_last.1
  (134 shorter events, 46.6 us)
Async XLA Ops:
  6.3 58.6 %all-to-all-start = ((bf16[128,7,16,128]{3,2,1,0:T(8,128)(2,1)}), bf16[128,7,16,128]{3,2,1,0:T(8,128)(2,1)}, u32[]{:S(2)}, u32[]{:S(2)}) async-start(bf16[128,7,16,128]{3,2,1,0:T(8,128)(2,1)} %bitcast.48), calls=%async_computation | async-start | bytes 7340032 | tf_op jit(solution)/shard_map/all_to_all | solution.py:570
  19.6 13.4 %collective-permute-start.1 = (bf16[704,2048]{1,0:T(8,128)(2,1)}, bf16[704,2048]{1,0:T(8,128)(2,1)}, u32[]{:S(2)}, u32[]{:S(2)}) collective-permute-start(bf16[704,2048]{1,0:T(8,128)(2,1)} %bitcast.8.up0), channel_id=1, source_target_pairs={{0,1},{1,0},{2,3},{3,2},{4,5},{5,4},{6,7},{7,6},{8,9},{9,8},{10,11... | collective-permute-start | bytes 8650760 | tf_op jit(solution)/shard_map/ppermute | solution.py:556
  155.9 10.5 %collective-permute-start.22 = (bf16[128,1024]{1,0:T(8,128)(2,1)}, bf16[128,1024]{1,0:T(8,128)(2,1)S(1)}, u32[]{:S(2)}, u32[]{:S(2)}) collective-permute-start(bf16[128,1024]{1,0:T(8,128)(2,1)} %get-tuple-element.36), channel_id=1, source_target_pairs={{0,8},{1,9},{2,10},{3,11},{4,12},{5,13},{6,14},{7,15},{8,0},{9,1},... | collective-permute-start | bytes 786440 | tf_op jit(solution)/shard_map/ppermute | solution.py:556
  158.2 12.6 %collective-permute-start.7 = (bf16[128,1024]{1,0:T(8,128)(2,1)}, bf16[128,1024]{1,0:T(8,128)(2,1)S(1)}, u32[]{:S(2)}, u32[]{:S(2)}) collective-permute-start(bf16[128,1024]{1,0:T(8,128)(2,1)} %get-tuple-element.33.refs_0_), channel_id=1, source_target_pairs={{0,1},{1,0},{2,3},{3,2},{4,5},{5,4},{6,7},{7,6},{8,9},{9,8},{10,11... | collective-permute-start | bytes 786440 | tf_op jit(solution)/shard_map/ppermute | solution.py:556
  160.8 14.9 %collective-permute-start.13 = (bf16[128,1024]{1,0:T(8,128)(2,1)S(1)}, bf16[128,1024]{1,0:T(8,128)(2,1)S(1)}, u32[]{:S(2)}, u32[]{:S(2)}) collective-permute-start(bf16[128,1024]{1,0:T(8,128)(2,1)S(1)} %collective-permute-done.12.refs_10_), channel_id=1, source_target_pairs={{0,2},{1,3},{2,4},{3,5},{4,6},{5,7},{6,0},{7,1},{8,10},{9,11},{10,... | collective-permute-start | bytes 786440 | tf_op jit(solution)/shard_map/ppermute | solution.py:556
  161.2 9.6 %collective-permute-start.5 = (bf16[64,1024]{1,0:T(8,128)(2,1)S(1)}, bf16[64,1024]{1,0:T(8,128)(2,1)S(1)}, u32[]{:S(2)}, u32[]{:S(2)}) collective-permute-start(bf16[64,1024]{1,0:T(8,128)(2,1)S(1)} %slice.24), channel_id=1, source_target_pairs={{0,2},{1,3},{2,4},{3,5},{4,6},{5,7},{6,0},{7,1},{8,10},{9,11},{10,... | collective-permute-start | bytes 393224 | tf_op jit(solution)/shard_map/ppermute | solution.py:556
  162.2 11.3 %collective-permute-start.6 = (bf16[64,1024]{1,0:T(8,128)(2,1)S(1)}, bf16[64,1024]{1,0:T(8,128)(2,1)S(1)}, u32[]{:S(2)}, u32[]{:S(2)}) collective-permute-start(bf16[64,1024]{1,0:T(8,128)(2,1)S(1)} %slice.25), channel_id=1, source_target_pairs={{0,6},{1,7},{2,0},{3,1},{4,2},{5,3},{6,4},{7,5},{8,14},{9,15},{10,... | collective-permute-start | bytes 393224 | tf_op jit(solution)/shard_map/ppermute | solution.py:556
  170.8 19.6 %collective-permute-start.23 = (bf16[256,1024]{1,0:T(8,128)(2,1)}, bf16[256,1024]{1,0:T(8,128)(2,1)S(1)}, u32[]{:S(2)}, u32[]{:S(2)}) collective-permute-start(bf16[256,1024]{1,0:T(8,128)(2,1)} %constant_dynamic-update-slice_fusion.refs_0_), channel_id=1, source_target_pairs={{0,2},{1,3},{2,4},{3,5},{4,6},{5,7},{6,0},{7,1},{8,10},{9,11},{10,... | collective-permute-start | bytes 1572872 | tf_op jit(solution)/shard_map/ppermute | solution.py:556
  170.8 19.6 %collective-permute-start.25 = (bf16[256,1024]{1,0:T(8,128)(2,1)}, bf16[256,1024]{1,0:T(8,128)(2,1)}, u32[]{:S(2)}, u32[]{:S(2)}) collective-permute-start(bf16[256,1024]{1,0:T(8,128)(2,1)} %constant_dynamic-update-slice_fusion.refs_0_), channel_id=1, source_target_pairs={{0,6},{1,7},{2,0},{3,1},{4,2},{5,3},{6,4},{7,5},{8,14},{9,15},{10,... | collective-permute-start | bytes 1572872 | tf_op jit(solution)/shard_map/ppermute | solution.py:556
  186.8 9.9 %collective-permute-start.18 = (bf16[128,1024]{1,0:T(8,128)(2,1)S(1)}, bf16[128,1024]{1,0:T(8,128)(2,1)}, u32[]{:S(2)}, u32[]{:S(2)}) collective-permute-start(bf16[128,1024]{1,0:T(8,128)(2,1)S(1)} %collective-permute-done.13.refs_11_), channel_id=1, source_target_pairs={{0,1},{1,0},{2,3},{3,2},{4,5},{5,4},{6,7},{7,6},{8,9},{9,8},{10,11... | collective-permute-start | bytes 786440 | tf_op jit(solution)/shard_map/ppermute | solution.py:556
  192.5 19.6 %collective-permute-start.29 = (bf16[256,1024]{1,0:T(8,128)(2,1)}, bf16[256,1024]{1,0:T(8,128)(2,1)}, u32[]{:S(2)}, u32[]{:S(2)}) collective-permute-start(bf16[256,1024]{1,0:T(8,128)(2,1)} %constant_dynamic-update-slice_fusion.refs_0_), channel_id=1, source_target_pairs={{0,1},{1,0},{2,3},{3,2},{4,5},{5,4},{6,7},{7,6},{8,9},{9,8},{10,11... | collective-permute-start | bytes 1572872 | tf_op jit(solution)/shard_map/ppermute | solution.py:556
  192.7 17.5 %collective-permute-start.24 = (bf16[128,1024]{1,0:T(8,128)(2,1)S(1)}, bf16[128,1024]{1,0:T(8,128)(2,1)S(1)}, u32[]{:S(2)}, u32[]{:S(2)}) collective-permute-start(bf16[128,1024]{1,0:T(8,128)(2,1)S(1)} %slice.28), channel_id=1, source_target_pairs={{0,2},{1,3},{2,4},{3,5},{4,6},{5,7},{6,0},{7,1},{8,10},{9,11},{10,... | collective-permute-start | bytes 786440 | tf_op jit(solution)/shard_map/ppermute | solution.py:556
  193.4 17.2 %collective-permute-start.26 = (bf16[128,1024]{1,0:T(8,128)(2,1)S(1)}, bf16[128,1024]{1,0:T(8,128)(2,1)S(1)}, u32[]{:S(2)}, u32[]{:S(2)}) collective-permute-start(bf16[128,1024]{1,0:T(8,128)(2,1)S(1)} %slice.29), channel_id=1, source_target_pairs={{0,6},{1,7},{2,0},{3,1},{4,2},{5,3},{6,4},{7,5},{8,14},{9,15},{10,... | collective-permute-start | bytes 786440 | tf_op jit(solution)/shard_map/ppermute | solution.py:556
  196.7 15.4 %collective-permute-start.30 = (bf16[256,1024]{1,0:T(8,128)(2,1)S(1)}, bf16[256,1024]{1,0:T(8,128)(2,1)}, u32[]{:S(2)}, u32[]{:S(2)}) collective-permute-start(bf16[256,1024]{1,0:T(8,128)(2,1)S(1)} %collective-permute-done.23.refs_1_), channel_id=1, source_target_pairs={{0,1},{1,0},{2,3},{3,2},{4,5},{5,4},{6,7},{7,6},{8,9},{9,8},{10,11... | collective-permute-start | bytes 1572872 | tf_op jit(solution)/shard_map/ppermute | solution.py:556
  197.1 15.0 %collective-permute-start.31 = (bf16[256,1024]{1,0:T(8,128)(2,1)}, bf16[256,1024]{1,0:T(8,128)(2,1)}, u32[]{:S(2)}, u32[]{:S(2)}) collective-permute-start(bf16[256,1024]{1,0:T(8,128)(2,1)} %collective-permute-done.25.refs_2_), channel_id=1, source_target_pairs={{0,1},{1,0},{2,3},{3,2},{4,5},{5,4},{6,7},{7,6},{8,9},{9,8},{10,11... | collective-permute-start | bytes 1572872 | tf_op jit(solution)/shard_map/ppermute | solution.py:556
  206.5 52.6 %all-to-all-start.2 = ((bf16[8,768,128]{2,1,0:T(8,128)(2,1)}), bf16[8,768,128]{2,1,0:T(8,128)(2,1)S(1)}, u32[]{:S(2)}, u32[]{:S(2)}) async-start(bf16[8,768,128]{2,1,0:T(8,128)(2,1)} %get-tuple-element.42), calls=%async_computation.2 | async-start | bytes 3145728 | tf_op jit(solution)/shard_map/all_to_all | solution.py:468
  210.2 9.8 %collective-permute-start.27 = (bf16[128,1024]{1,0:T(8,128)(2,1)S(1)}, bf16[128,1024]{1,0:T(8,128)(2,1)S(1)}, u32[]{:S(2)}, u32[]{:S(2)}) collective-permute-start(bf16[128,1024]{1,0:T(8,128)(2,1)S(1)} %collective-permute-done.24.refs_0_), channel_id=1, source_target_pairs={{0,1},{1,0},{2,3},{3,2},{4,5},{5,4},{6,7},{7,6},{8,9},{9,8},{10,11... | collective-permute-start | bytes 786440 | tf_op jit(solution)/shard_map/ppermute | solution.py:556
  226.8 9.8 %collective-permute-start.32 = (bf16[768,128]{1,0:T(8,128)(2,1)}, bf16[768,128]{1,0:T(8,128)(2,1)S(1)}, u32[]{:S(2)}, u32[]{:S(2)}) collective-permute-start(bf16[768,128]{1,0:T(8,128)(2,1)} %get-tuple-element.44), channel_id=1, source_target_pairs={{0,80},{1,81},{2,82},{3,83},{4,84},{5,85},{6,86},{7,87},{8,88},{9,... | collective-permute-start | bytes 589832 | tf_op jit(solution)/shard_map/ppermute | solution.py:562
  230.9 14.7 %collective-permute-start.33 = (bf16[768,128]{1,0:T(8,128)(2,1)}, bf16[768,128]{1,0:T(8,128)(2,1)S(1)}, u32[]{:S(2)}, u32[]{:S(2)}) collective-permute-start(bf16[768,128]{1,0:T(8,128)(2,1)} %get-tuple-element.45), channel_id=1, source_target_pairs={{0,64},{1,65},{2,66},{3,67},{4,68},{5,69},{6,70},{7,71},{8,72},{9,... | collective-permute-start | bytes 589832 | tf_op jit(solution)/shard_map/ppermute | solution.py:562
  231.2 31.6 %collective-permute-start.34 = (bf16[768,128]{1,0:T(8,128)(2,1)}, bf16[768,128]{1,0:T(8,128)(2,1)S(1)}, u32[]{:S(2)}, u32[]{:S(2)}) collective-permute-start(bf16[768,128]{1,0:T(8,128)(2,1)} %get-tuple-element.46), channel_id=1, source_target_pairs={{0,48},{1,49},{2,50},{3,51},{4,52},{5,53},{6,54},{7,55},{8,56},{9,... | collective-permute-start | bytes 589832 | tf_op jit(solution)/shard_map/ppermute | solution.py:562
  232.4 30.4 %collective-permute-start.35 = (bf16[768,128]{1,0:T(8,128)(2,1)}, bf16[768,128]{1,0:T(8,128)(2,1)S(1)}, u32[]{:S(2)}, u32[]{:S(2)}) collective-permute-start(bf16[768,128]{1,0:T(8,128)(2,1)} %get-tuple-element.47), channel_id=1, source_target_pairs={{0,112},{1,113},{2,114},{3,115},{4,116},{5,117},{6,118},{7,119},{8... | collective-permute-start | bytes 589832 | tf_op jit(solution)/shard_map/ppermute | solution.py:562
  234.8 28.0 %collective-permute-start.36 = (bf16[768,128]{1,0:T(8,128)(2,1)}, bf16[768,128]{1,0:T(8,128)(2,1)S(1)}, u32[]{:S(2)}, u32[]{:S(2)}) collective-permute-start(bf16[768,128]{1,0:T(8,128)(2,1)} %get-tuple-element.48), channel_id=1, source_target_pairs={{0,32},{1,33},{2,34},{3,35},{4,36},{5,37},{6,38},{7,39},{8,40},{9,... | collective-permute-start | bytes 589832 | tf_op jit(solution)/shard_map/ppermute | solution.py:562
  236.6 26.2 %collective-permute-start.37 = (bf16[768,128]{1,0:T(8,128)(2,1)}, bf16[768,128]{1,0:T(8,128)(2,1)S(1)}, u32[]{:S(2)}, u32[]{:S(2)}) collective-permute-start(bf16[768,128]{1,0:T(8,128)(2,1)} %get-tuple-element.49), channel_id=1, source_target_pairs={{0,96},{1,97},{2,98},{3,99},{4,100},{5,101},{6,102},{7,103},{8,104... | collective-permute-start | bytes 589832 | tf_op jit(solution)/shard_map/ppermute | solution.py:562
  245.7 17.2 %collective-permute-start.38 = (bf16[768,128]{1,0:T(8,128)(2,1)}, bf16[768,128]{1,0:T(8,128)(2,1)S(1)}, u32[]{:S(2)}, u32[]{:S(2)}) collective-permute-start(bf16[768,128]{1,0:T(8,128)(2,1)} %get-tuple-element.50), channel_id=1, source_target_pairs={{0,16},{1,17},{2,18},{3,19},{4,20},{5,21},{6,22},{7,23},{8,24},{9,... | collective-permute-start | bytes 589832 | tf_op jit(solution)/shard_map/ppermute | solution.py:562
  (43 other events, 452.7 us)

commit v7 on v5

--- a/solution.py
+++ b/solution.py
@@ -194,35 +194,45 @@
 VMEM_LIMIT = 60 * 1024 * 1024
 
 
-def terms_body(at_ref, *refs, pieces, blocks, scale, apart):
+def terms_body(at_ref, *refs, pieces, blocks, base, owners_at, scale, apart):
     parts = refs[:pieces]
-    cot_hbm, *out_hbm, all_rows, rows_ref, cot_ref, cut_ref, sem, side_sem, out_sem = refs[pieces:]
-    loads = []
-    for i, (piece, start, size) in enumerate(blocks):
-        to = pl.ds(pl.multiple_of(at_ref[i], size), size)
-        loads.append(pltpu.make_async_copy(parts[piece].at[pl.ds(start, size)], rows_ref.at[to], sem.at[i]))
-    cot_load = pltpu.make_async_copy(cot_hbm, cot_ref, side_sem.at[0])
+    cot_hbm, *out_hbm, all_rows, rows_ref, cot_ref, cut_ref, sem, keep_sem, cot_sem, out_sem = refs[pieces:]
+    owners = cut_ref.shape[0]
+    wide = 2 * LANES
+    tiles = owners // 2
+
+    def columns(d):
+        return pl.ds(d * wide if isinstance(d, int) else pl.multiple_of(d * wide, wide), wide)
+
+    def loads(d):
+        for i, (piece, start, size) in enumerate(blocks):
+            to = pl.ds(pl.multiple_of(at_ref[base + i], size), size)
+            ends = parts[piece].at[pl.ds(start, size), columns(d)], rows_ref.at[to, columns(d)]
+            yield pltpu.make_async_copy(*ends, sem.at[d, i])
+
+    def keep(d):
+        return pltpu.make_async_copy(rows_ref.at[:, columns(d)], all_rows.at[:, columns(d)], keep_sem.at[d])
+
+    cot_load = pltpu.make_async_copy(cot_hbm, cot_ref, cot_sem)
     cot_load.start()
-    for c in loads:
-        c.start()
-    for c in loads:
-        c.wait()
-    keep = pltpu.make_async_copy(rows_ref, all_rows, side_sem.at[1])
-    keep.start()
+    for d in range(tiles):
+        for c in loads(d):
+            c.start()
     cot_load.wait()
-    owners = cut_ref.shape[0]
 
     def step(d, carry):
-        at = pl.ds(pl.multiple_of(d * 2 * LANES, 2 * LANES), 2 * LANES)
-        terms = jnp.dot(cot_ref[...], rows_ref[:, at], preferred_element_type=jnp.float32) * scale
+        for c in loads(d):
+            c.wait()
+        keep(d).start()
+        terms = jnp.dot(cot_ref[...], rows_ref[:, columns(d)], preferred_element_type=jnp.float32) * scale
         cut_ref[2 * d] = terms[:, :LANES].astype(jnp.bfloat16)
         cut_ref[2 * d + 1] = terms[:, LANES:].astype(jnp.bfloat16)
         return carry
 
-    lax.fori_loop(0, owners // 2, step, 0)
+    lax.fori_loop(0, tiles, step, 0)
     if apart:
         outs = [
-            pltpu.make_async_copy(cut_ref.at[at_ref[len(blocks) + i]], out, out_sem.at[i]) for i, out in enumerate(out_hbm)
+            pltpu.make_async_copy(cut_ref.at[at_ref[owners_at + i]], out, out_sem.at[i]) for i, out in enumerate(out_hbm)
         ]
     else:
         outs = [pltpu.make_async_copy(cut_ref, out_hbm[0], out_sem.at[0])]
@@ -230,7 +240,8 @@
         c.start()
     for c in outs:
         c.wait()
-    keep.wait()
+    for d in range(tiles):
+        keep(d).wait()
 
 
 def features_body(rows0, rows1, one_hbm, two_hbm, feat_one, feat_two, rows_ref, one_ref, two_ref, out_one, out_two, sem, row_sem, out_sem):
@@ -295,40 +306,64 @@
     return total.T
 
 
-def sum_first_body(pieces_ref, out_ref):
-    out_ref[...] = total_of([pieces_ref[i] for i in range(pieces_ref.shape[0])])
-
-
-def sum_last_body(first_ref, *refs):
+def sums_body(first_ref, *refs):
     *pieces, one_ref, two_ref = refs
     split = one_ref.shape[1]
-    half = first_ref.shape[0]
-    one_ref[:half] = first_ref[:, :split]
-    two_ref[:half] = first_ref[:, split:]
-    total = total_of([piece[...] for piece in pieces])
-    one_ref[half:] = total[:, :split]
-    two_ref[half:] = total[:, split:]
-
-
-def project(parts, student_one, student_two, cots, move, pass_on, place):
+    halves = [[first_ref[i] for i in range(first_ref.shape[0])], [piece[...] for piece in pieces]]
+    for k, half in enumerate(halves):
+        total = total_of(half)
+        one_ref[k * LANES : (k + 1) * LANES] = total[:, :split]
+        two_ref[k * LANES : (k + 1) * LANES] = total[:, split:]
+
+
+STEPS = [(0, 0), (2, 1), (2, 0), (1, 1), (3, 1), (1, 0), (3, 0), (0, 1)]
+RING = 4
+
+
+def gathered_spots(place, rows):
+    z, y_lo, y_hi, x, core = place
+
+    def row_of(y, at, c):
+        return (y * RING + at % RING) * (2 * rows) + c * rows
+
+    def single(y, first):
+        half = rows // 2
+        out = []
+        for k, c in enumerate((core, 1 - core)):
+            at = first + 5 * k
+            out += [(at + i, 0, rows, row_of(y, x + d, c)) for i, d in enumerate((0, RING - 1, 1))]
+            out += [(at + 3 + i, 0, half, row_of(y, x + 2, c) + i * half) for i in range(2)]
+        return out
+
+    def double(first):
+        out = []
+        for k, c in enumerate((core, 1 - core)):
+            at = first + 5 * k
+            for side, y in enumerate((y_hi, 1 - y_hi)):
+                out += [(at + i, side * rows, rows, row_of(y, x + d, c)) for i, d in enumerate((0, RING - 1, 1))]
+                out.append((at + 3 + side, 0, rows, row_of(y, x + 2, c)))
+        return out
+
+    owners = [(z + dz) % 4 * 2 + (y_lo + dy) % 2 for dz, dy in STEPS]
+    return single(y_hi, 0) + single(1 - y_hi, 10), double(0), owners
+
+
+def spots_table(place, rows):
+    first, second, owners = gathered_spots(place, rows)
+    return jnp.stack([spot[3] for spot in first + second] + owners).astype(jnp.int32)
+
+
+def project(parts, student_one, student_two, cots, move, pass_on, place, table):
     rows, half_width = parts[0].shape
-    z, y_lo, y_hi, x, core = place
-    ring, owners = 4, 8
-    count = 4 * ring * rows
+    spots0, spots1, _ = gathered_spots(place, rows)
+    owners = len(STEPS)
+    count = 4 * RING * rows
     split = student_one.shape[1]
     cols = split + student_two.shape[1]
     bf16, f32 = jnp.bfloat16, jnp.float32
     dma = pltpu.SemaphoreType.DMA
     anywhere = pl.BlockSpec(memory_space=pl.ANY)
     inside = pl.BlockSpec(memory_space=pltpu.VMEM)
-
-    def row_of(y, at, c):
-        return (y * ring + at % ring) * (2 * rows) + c * rows
-
-    def spread(y, c):
-        half = rows // 2
-        near = [(0, rows, row_of(y, x + d, c)) for d in (0, ring - 1, 1)]
-        return near + [(0, half, row_of(y, x + 2, c) + k * half) for k in range(2)]
 
     def gather(block):
         half = block.shape[0] // 2
@@ -342,22 +377,7 @@
             swapped.append(move(piece, 0, 0, 1))
         return own + swapped
 
-    def single(y, first):
-        return [(first + i, *spot) for i, spot in enumerate(spread(y, core) + spread(y, 1 - core))]
-
-    def double(first):
-        out = []
-        for k, c in enumerate((core, 1 - core)):
-            at = first + 5 * k
-            for side, y in enumerate((y_hi, 1 - y_hi)):
-                out += [(at + i, side * rows, rows, row_of(y, x + d, c)) for i, d in enumerate((0, ring - 1, 1))]
-                out.append((at + 3 + side, 0, rows, row_of(y, x + 2, c)))
-        return out
-
-    steps = [(0, 0), (2, 1), (2, 0), (1, 1), (3, 1), (1, 0), (3, 0), (0, 1)]
-    owner_of = [(z + dz) % 4 * 2 + (y_lo + dy) % 2 for dz, dy in steps]
-
-    def terms(pieces, spots, apart):
+    def terms(pieces, spots, base, apart):
         cuts = (owners * [jax.ShapeDtypeStruct((cols, LANES), bf16)]) if apart else [
             jax.ShapeDtypeStruct((owners, cols, LANES), bf16)
         ]
@@ -367,6 +387,8 @@
                 terms_body,
                 pieces=len(pieces),
                 blocks=blocks,
+                base=base,
+                owners_at=table.shape[0] - owners,
                 scale=1.0 / math.sqrt(count * owners),
                 apart=apart,
             ),
@@ -380,8 +402,9 @@
                     pltpu.VMEM((count, half_width), bf16),
                     pltpu.VMEM((cols, count), bf16),
                     pltpu.VMEM((owners, cols, LANES), bf16),
-                    dma((len(blocks),)),
-                    dma((2,)),
+                    dma((owners // 2, len(blocks))),
+                    dma((owners // 2,)),
+                    dma,
                     dma((owners,)),
                 ],
             ),
@@ -390,14 +413,14 @@
             cost_estimate=pl.CostEstimate(
                 flops=2 * count * half_width * cols, transcendentals=0, bytes_accessed=12 << 20
             ),
-        )(jnp.stack([spot[3] for spot in spots] + owner_of).astype(jnp.int32), *pieces, cots)
+        )(table, *pieces, cots)
 
     other0 = move(parts[0], 2, 0, 0)
     other1 = move(parts[1], 2, 0, 0)
-    cut0, rows0 = terms(gather(parts[0]) + gather(other0), single(y_hi, 0) + single(1 - y_hi, 10), False)
+    cut0, rows0 = terms(gather(parts[0]) + gather(other0), spots0, 0, False)
     cut0 = lax.all_to_all(cut0, "dp", split_axis=0, concat_axis=0, tiled=True)
-    *cut1, rows1 = terms(gather(jnp.concatenate([parts[1], other1], axis=0)), double(0), True)
-    for i, (dz, dy) in enumerate(steps[1:], 1):
+    *cut1, rows1 = terms(gather(jnp.concatenate([parts[1], other1], axis=0)), spots1, len(spots0), True)
+    for i, (dz, dy) in enumerate(STEPS[1:], 1):
         cut1[i] = pass_on(cut1[i], dz, dy)
     shape = (owners, 2, LANES)
     feat_one, feat_two = pl.pallas_call(
@@ -422,23 +445,16 @@
         compiler_params=pltpu.CompilerParams(vmem_limit_bytes=VMEM_LIMIT),
         cost_estimate=pl.CostEstimate(flops=4 * count * half_width * cols, transcendentals=0, bytes_accessed=14 << 20),
     )(rows0, rows1, student_one.reshape(*shape, split), student_two.reshape(*shape, cols - split))
-    total0 = pl.pallas_call(
-        sum_first_body,
-        name="sum_first",
-        in_specs=[inside],
-        out_specs=inside,
-        out_shape=jax.ShapeDtypeStruct((LANES, cols), f32),
-    )(cut0)
     grad_one, grad_two = pl.pallas_call(
-        sum_last_body,
-        name="sum_last",
+        sums_body,
+        name="sums",
         in_specs=[inside] * (1 + owners),
         out_specs=(inside, inside),
         out_shape=(
             jax.ShapeDtypeStruct((2 * LANES, split), f32),
             jax.ShapeDtypeStruct((2 * LANES, cols - split), f32),
         ),
-    )(total0, *cut1)
+    )(cut0, *cut1)
     return feat_one, feat_two, grad_one, grad_two
 
 
@@ -481,7 +497,9 @@
     cots = jnp.concatenate([cot_one, cot_two], axis=1).T
     other_gate = move(jnp.swapaxes(gate_proj[0], 0, 1), 0, 0, 1)
     other_up = move(jnp.swapaxes(up_proj[0], 0, 1), 0, 0, 1)
-    other_down, cots = lax.optimization_barrier((move(down_proj[0], 0, 0, 1), cots))
+    place = (index // 32, index // 16 % 2, index // 8 % 2, index // 2 % 4, index % 2)
+    table = spots_table(place, tok_dev)
+    other_down, cots, table = lax.optimization_barrier((move(down_proj[0], 0, 0, 1), cots, table))
 
     placed, positions = dispatch(expert_ids.T, tokens, norm_gain.reshape(1, -1), experts, capacity)
     received = lax.all_to_all(
@@ -508,15 +526,7 @@
         tiled=True,
     )
     layer_out, *parts = combine(positions, gate_weights.T, returned.reshape(experts * capacity, sub, LANES))
-    feat_one, feat_two, grad_one, grad_two = project(
-        parts,
-        student_one,
-        student_two,
-        cots,
-        move,
-        pass_on,
-        (index // 32, index // 16 % 2, index // 8 % 2, index // 2 % 4, index % 2),
-    )
+    feat_one, feat_two, grad_one, grad_two = project(parts, student_one, student_two, cots, move, pass_on, place, table)
     return (layer_out, feat_one, feat_two, grad_one, grad_two)
 
 

time: 267 us -> 266 us (level)
    unnamed x53 -> x69, local copies, waits for them, and re-layouts: 8.24 us -> 8.3 us
  transfers between devices with their start and end apart: 41 -> 41, of which waited for: 11 -> 12; matrix products, arithmetic and copies ran while one was open for 4% -> 3% of each run, Pallas kernels for 13% -> 12%
where the time goes in v7:
time: 266 us; the launch traced here: 265 us
  Pallas kernels  76.2 us (29%)
  waiting for transfers between devices  62.6 us (24%)
  starting transfers between devices  60.9 us (23%)
  blocking collectives  52.8 us (20%)
  local copies, waits for them, and re-layouts  9.87 us (4%)
    all_to_all x1, blocking collectives, local(): lax.all_to_all(expert_out.reshape(devices, capacity // 2, sub, LANES), ('...  52.8 us
    ppermute x32, starting transfers between devices, move(): return lax.ppermute(array, axes, [(d, target(d)) for d in range(devices)])  37.6 us
    all_to_all x1, waiting for transfers between devices, local(): lax.all_to_all(placed.reshape(devices, capacity // 2, sub, LANES), ('dp',...  32 us
    pallas_call x1, Pallas kernels, expert(): pl.pallas_call(functools.partial(expert_body, step=step, tile=tile, cols=...  29 us
    pallas_call x2, Pallas kernels, terms(): pl.pallas_call(functools.partial(terms_body, pieces=len(pieces), blocks=b...  20.4 us
    ppermute x32, waiting for transfers between devices, move(): return lax.ppermute(array, axes, [(d, target(d)) for d in range(devices)])  15.9 us
    ppermute x7, waiting for transfers between devices, pass_on(): return lax.ppermute(array, axes, [(d, target(d)) for d in range(devices)])  14.7 us
    pallas_call x1, Pallas kernels, project(): pl.pallas_call(features_body, name='features', in_specs=[anywhere] * 4, o...  12.2 us
  transfers between devices with their start and end apart: 41, of which 12 were waited for; matrix products, arithmetic and copies ran while one was open for 3% of the time, Pallas kernels for 12%

profile of v7, /device:TPU:1, one launch (start us, length us, event | category | flops | bytes accessed | tf_op | source)
XLA Modules:
  0.0 265.4 jit_solution(3658358221837672191)
XLA Ops:
  0.6 5.7 %dispatch.1 = (bf16[896,16,128]{2,1,0:T(8,128)(2,1)}, s32[6,128]{1,0:T(8,128)}) custom-call(s32[6,128]{1,0:T(8,128)} %bitcast.50, bf16[128,2048]{1,0:T(8,128)(2,1)} %tok_ref.1, f32[1,2048]{1,0:T(1,128)} %bitcast.49), custom_call_target="tpu_custom_call" | custom-call | tf_op jit(solution)/shard_map/dispatch/pallas_call | solution.py:54
  6.3 11.9 %all-to-all-start = ((bf16[128,7,16,128]{3,2,1,0:T(8,128)(2,1)}), bf16[128,7,16,128]{3,2,1,0:T(8,128)(2,1)}, u32[]{:S(2)}, u32[]{:S(2)}) async-start(bf16[128,7,16,128]{3,2,1,0:T(8,128)(2,1)} %bitcast.48), calls=%async_computation | async-start | bytes 7340032 | tf_op jit(solution)/shard_map/all_to_all | solution.py:505
  20.6 3.1 %copy.17 = bf16[2048,512]{0,1:T(8,128)(2,1)S(1)} copy(bf16[2048,512]{1,0:T(8,128)(2,1)} %param.21) | data formatting | bytes 4194304 | tf_op args[10]
  26.3 2.5 collective-permute-done.gate1
  28.8 4.1 %collective-permute-done.1.up1 = bf16[704,2048]{1,0:T(8,128)(2,1)} collective-permute-done((bf16[704,2048]{1,0:T(8,128)(2,1)}, bf16[704,2048]{1,0:T(8,128)(2,1)}, u32[]{:S(2)}, u32[]{:S(2)}) %collective-permute-start.1) | collective-permute-done | bytes 2883616 | tf_op jit(solution)/shard_map/ppermute | solution.py:489
  33.0 32.0 %all-to-all-done = bf16[128,7,16,128]{3,2,1,0:T(8,128)(2,1)} async-done(((bf16[128,7,16,128]{3,2,1,0:T(8,128)(2,1)}), bf16[128,7,16,128]{3,2,1,0:T(8,128)(2,1)}, u32[]{:S(2)}, u32[]{:S(2)}) %all-to-all-start) | async-done | bytes 3670048 | tf_op jit(solution)/shard_map/all_to_all | solution.py:505
  65.0 29.0 %expert.1 = bf16[896,16,128]{2,1,0:T(8,128)(2,1)} custom-call(bf16[896,16,128]{2,1,0:T(8,128)(2,1)} %bitcast.4.rows_hbm, bf16[704,2048]{1,0:T(8,128)(2,1)} %bitcast.6.gate0, bf16[704,2048]{1,0:T(8,128)(2,1)} %bitcast.8.up0, bf16[704,2048]{1,0:T(8,128)(2,1)} %bitcast.9.down0, bf16[704,2048]{1,0:T(8,128)(2,1)} %collective-permute-done.gate1, ...), custom_call_target="tpu_custom_call" | custom-call | tf_op jit(solution)/shard_map/expert/pallas_call | solution.py:172
  94.0 52.8 %all_to_all.15 = bf16[128,7,16,128]{3,2,1,0:T(8,128)(2,1)} all-to-all(bf16[128,7,16,128]{3,2,1,0:T(8,128)(2,1)} %bitcast.47), channel_id=1, replica_groups=mesh['dp'=8,'expert'=16] {'dp','expert'}, dimensions={0} | all-to-all | bytes 7340032 | tf_op jit(solution)/shard_map/all_to_all | solution.py:521
  146.9 5.6 %combine.1 = (bf16[128,2048]{1,0:T(8,128)(2,1)}, bf16[128,1024]{1,0:T(8,128)(2,1)}, bf16[128,1024]{1,0:T(8,128)(2,1)}) custom-call(s32[6,128]{1,0:T(8,128)} %get-tuple-element.28.pos_ref, f32[6,128]{1,0:T(8,128)} %bitcast.51, bf16[896,16,128]{2,1,0:T(8,128)(2,1)} %bitcast.46), custom_call_target="tpu_custom_call" | custom-call | tf_op jit(solution)/shard_map/combine/pallas_call | solution.py:92
  156.9 2.4 collective-permute-start.7
  160.8 3.8 %collective-permute-start.17 = (bf16[128,1024]{1,0:T(8,128)(2,1)S(1)}, bf16[128,1024]{1,0:T(8,128)(2,1)S(1)}, u32[]{:S(2)}, u32[]{:S(2)}) collective-permute-start(bf16[128,1024]{1,0:T(8,128)(2,1)S(1)} %collective-permute-done.12.refs_10_), channel_id=1, source_target_pairs={{0,1},{1,0},{2,3},{3,2},{4,5},{5,4},{6,7},{7,6},{8,9},{9,8},{10,11... | collective-permute-start | bytes 786440 | tf_op jit(solution)/shard_map/ppermute | solution.py:489
  170.8 2.6 collective-permute-start.24
  177.7 4.2 %collective-permute-start.10 = (bf16[64,1024]{1,0:T(8,128)(2,1)S(1)}, bf16[64,1024]{1,0:T(8,128)(2,1)S(1)}, u32[]{:S(2)}, u32[]{:S(2)}) collective-permute-start(bf16[64,1024]{1,0:T(8,128)(2,1)S(1)} %collective-permute-done.5.refs_3_), channel_id=1, source_target_pairs={{0,1},{1,0},{2,3},{3,2},{4,5},{5,4},{6,7},{7,6},{8,9},{9,8},{10,11... | collective-permute-start | bytes 393224 | tf_op jit(solution)/shard_map/ppermute | solution.py:489
  184.1 4.3 %collective-permute-done.16.refs_14_ = bf16[64,1024]{1,0:T(8,128)(2,1)S(1)} collective-permute-done((bf16[64,1024]{1,0:T(8,128)(2,1)S(1)}, bf16[64,1024]{1,0:T(8,128)(2,1)S(1)}, u32[]{:S(2)}, u32[]{:S(2)}) %collective-permute-start.16) | collective-permute-done | bytes 131104 | tf_op jit(solution)/shard_map/ppermute | solution.py:489
  191.7 2.3 collective-permute-start.18
  199.2 10.3 %terms.2 = (bf16[8,768,128]{2,1,0:T(8,128)(2,1)}, bf16[2048,1024]{1,0:T(8,128)(2,1)}) custom-call(s32[44]{0:T(128)} %stack.131.at_ref, bf16[128,1024]{1,0:T(8,128)(2,1)} %get-tuple-element.33.refs_0_, bf16[128,1024]{1,0:T(8,128)(2,1)} %copy-done.12, bf16[128,1024]{1,0:T(8,128)(2,1)} %copy-done.11, bf16[64,1024]{1,0:T(8,128)(2,1)} %copy-done.26, ...), custom_call_target="tpu_custom_call" | custom-call | flops 3221225472 | bytes 12582912 | tf_op jit(solution)/shard_map/terms/pallas_call | solution.py:385
  209.5 3.6 %all-to-all-start.2 = ((bf16[8,768,128]{2,1,0:T(8,128)(2,1)}), bf16[8,768,128]{2,1,0:T(8,128)(2,1)S(1)}, u32[]{:S(2)}, u32[]{:S(2)}) async-start(bf16[8,768,128]{2,1,0:T(8,128)(2,1)} %get-tuple-element.40), calls=%async_computation.2 | async-start | bytes 3145728 | tf_op jit(solution)/shard_map/all_to_all | solution.py:421
  215.8 10.1 %terms.3 = (bf16[768,128]{1,0:T(8,128)(2,1)}, bf16[768,128]{1,0:T(8,128)(2,1)}, bf16[768,128]{1,0:T(8,128)(2,1)}, bf16[768,128]{1,0:T(8,128)(2,1)}, bf16[768,128...) custom-call(s32[44]{0:T(128)} %stack.131.at_ref, ...), custom_call_target="tpu_custom_call" | custom-call | flops 3221225472 | bytes 12582912 | tf_op jit(solution)/shard_map/terms/pallas_call | solution.py:385
  226.0 4.0 %collective-permute-start.32 = (bf16[768,128]{1,0:T(8,128)(2,1)}, bf16[768,128]{1,0:T(8,128)(2,1)S(1)}, u32[]{:S(2)}, u32[]{:S(2)}) collective-permute-start(bf16[768,128]{1,0:T(8,128)(2,1)} %get-tuple-element.42), channel_id=1, source_target_pairs={{0,80},{1,81},{2,82},{3,83},{4,84},{5,85},{6,86},{7,87},{8,88},{9,... | collective-permute-start | bytes 589832 | tf_op jit(solution)/shard_map/ppermute | solution.py:495
  231.4 2.4 collective-permute-start.35
  233.8 6.2 %collective-permute-done.32.refs_1_ = bf16[768,128]{1,0:T(8,128)(2,1)S(1)} collective-permute-done((bf16[768,128]{1,0:T(8,128)(2,1)}, bf16[768,128]{1,0:T(8,128)(2,1)S(1)}, u32[]{:S(2)}, u32[]{:S(2)}) %collective-permute-start.32) | collective-permute-done | bytes 196640 | tf_op jit(solution)/shard_map/ppermute | solution.py:495
  240.0 8.5 %collective-permute-done.33.refs_2_ = bf16[768,128]{1,0:T(8,128)(2,1)S(1)} collective-permute-done((bf16[768,128]{1,0:T(8,128)(2,1)}, bf16[768,128]{1,0:T(8,128)(2,1)S(1)}, u32[]{:S(2)}, u32[]{:S(2)}) %collective-permute-start.33) | collective-permute-done | bytes 196640 | tf_op jit(solution)/shard_map/ppermute | solution.py:495
  248.5 12.2 %features.1 = (bf16[2048,256]{1,0:T(8,128)(2,1)}, bf16[2048,512]{1,0:T(8,128)(2,1)}) custom-call(bf16[2048,1024]{1,0:T(8,128)(2,1)} %get-tuple-element.35.rows0, bf16[2048,1024]{1,0:T(8,128)(2,1)} %get-tuple-element.37.rows1, bf16[8,2,128,256]{3,2,1,0:T(8,128)(2,1)} %bitcast.53, bf16[8,2,128,512]{3,2,1,0:T(8,128)(2,1)} %bitcast.52), custom_call_target="tpu_custom_call" | custom-call | flops 6442450944 | bytes 14680064 | tf_op jit(solution)/shard_map/features/pallas_call | solution.py:426
  262.2 3.2 %sums.1 = (f32[256,256]{1,0:T(8,128)}, f32[256,512]{1,0:T(8,128)}) custom-call(bf16[8,768,128]{2,1,0:T(8,128)(2,1)} %copy-done, bf16[768,128]{1,0:T(8,128)(2,1)} %get-tuple-element.41.refs_0_, bf16[768,128]{1,0:T(8,128)(2,1)} %copy-done.2, bf16[768,128]{1,0:T(8,128)(2,1)} %copy-done.3, bf16[768,128]{1,0:T(8,128)(2,1)} %copy-done.4, ...), custom_call_target="tpu_custom_call" | custom-call | tf_op jit(solution)/shard_map/sums/pallas_call | solution.py:448
  (144 shorter events, 37.3 us)
Async XLA Ops:
  6.3 58.6 %all-to-all-start = ((bf16[128,7,16,128]{3,2,1,0:T(8,128)(2,1)}), bf16[128,7,16,128]{3,2,1,0:T(8,128)(2,1)}, u32[]{:S(2)}, u32[]{:S(2)}) async-start(bf16[128,7,16,128]{3,2,1,0:T(8,128)(2,1)} %bitcast.48), calls=%async_computation | async-start | bytes 7340032 | tf_op jit(solution)/shard_map/all_to_all | solution.py:505
  19.6 13.4 %collective-permute-start.1 = (bf16[704,2048]{1,0:T(8,128)(2,1)}, bf16[704,2048]{1,0:T(8,128)(2,1)}, u32[]{:S(2)}, u32[]{:S(2)}) collective-permute-start(bf16[704,2048]{1,0:T(8,128)(2,1)} %bitcast.8.up0), channel_id=1, source_target_pairs={{0,1},{1,0},{2,3},{3,2},{4,5},{5,4},{6,7},{7,6},{8,9},{9,8},{10,11... | collective-permute-start | bytes 8650760 | tf_op jit(solution)/shard_map/ppermute | solution.py:489
  153.2 11.4 %collective-permute-start.4 = (bf16[128,1024]{1,0:T(8,128)(2,1)}, bf16[128,1024]{1,0:T(8,128)(2,1)S(1)}, u32[]{:S(2)}, u32[]{:S(2)}) collective-permute-start(bf16[128,1024]{1,0:T(8,128)(2,1)} %get-tuple-element.33.refs_0_), channel_id=1, source_target_pairs={{0,6},{1,7},{2,0},{3,1},{4,2},{5,3},{6,4},{7,5},{8,14},{9,15},{10,... | collective-permute-start | bytes 786440 | tf_op jit(solution)/shard_map/ppermute | solution.py:489
  153.9 11.0 %collective-permute-start.3 = (bf16[128,1024]{1,0:T(8,128)(2,1)}, bf16[128,1024]{1,0:T(8,128)(2,1)S(1)}, u32[]{:S(2)}, u32[]{:S(2)}) collective-permute-start(bf16[128,1024]{1,0:T(8,128)(2,1)} %get-tuple-element.33.refs_0_), channel_id=1, source_target_pairs={{0,2},{1,3},{2,4},{3,5},{4,6},{5,7},{6,0},{7,1},{8,10},{9,11},{10,... | collective-permute-start | bytes 786440 | tf_op jit(solution)/shard_map/ppermute | solution.py:489
  154.7 11.8 %collective-permute-start.22 = (bf16[128,1024]{1,0:T(8,128)(2,1)}, bf16[128,1024]{1,0:T(8,128)(2,1)S(1)}, u32[]{:S(2)}, u32[]{:S(2)}) collective-permute-start(bf16[128,1024]{1,0:T(8,128)(2,1)} %get-tuple-element.36), channel_id=1, source_target_pairs={{0,8},{1,9},{2,10},{3,11},{4,12},{5,13},{6,14},{7,15},{8,0},{9,1},... | collective-permute-start | bytes 786440 | tf_op jit(solution)/shard_map/ppermute | solution.py:489
  156.9 13.1 %collective-permute-start.7 = (bf16[128,1024]{1,0:T(8,128)(2,1)}, bf16[128,1024]{1,0:T(8,128)(2,1)S(1)}, u32[]{:S(2)}, u32[]{:S(2)}) collective-permute-start(bf16[128,1024]{1,0:T(8,128)(2,1)} %get-tuple-element.33.refs_0_), channel_id=1, source_target_pairs={{0,1},{1,0},{2,3},{3,2},{4,5},{5,4},{6,7},{7,6},{8,9},{9,8},{10,11... | collective-permute-start | bytes 786440 | tf_op jit(solution)/shard_map/ppermute | solution.py:489
  160.8 12.6 %collective-permute-start.17 = (bf16[128,1024]{1,0:T(8,128)(2,1)S(1)}, bf16[128,1024]{1,0:T(8,128)(2,1)S(1)}, u32[]{:S(2)}, u32[]{:S(2)}) collective-permute-start(bf16[128,1024]{1,0:T(8,128)(2,1)S(1)} %collective-permute-done.12.refs_10_), channel_id=1, source_target_pairs={{0,1},{1,0},{2,3},{3,2},{4,5},{5,4},{6,7},{7,6},{8,9},{9,8},{10,11... | collective-permute-start | bytes 786440 | tf_op jit(solution)/shard_map/ppermute | solution.py:489
  170.8 23.2 %collective-permute-start.24 = (bf16[256,1024]{1,0:T(8,128)(2,1)}, bf16[256,1024]{1,0:T(8,128)(2,1)S(1)}, u32[]{:S(2)}, u32[]{:S(2)}) collective-permute-start(bf16[256,1024]{1,0:T(8,128)(2,1)} %constant_dynamic-update-slice_fusion.refs_0_), channel_id=1, source_target_pairs={{0,6},{1,7},{2,0},{3,1},{4,2},{5,3},{6,4},{7,5},{8,14},{9,15},{10,... | collective-permute-start | bytes 1572872 | tf_op jit(solution)/shard_map/ppermute | solution.py:489
  173.4 20.7 %collective-permute-start.23 = (bf16[256,1024]{1,0:T(8,128)(2,1)}, bf16[256,1024]{1,0:T(8,128)(2,1)S(1)}, u32[]{:S(2)}, u32[]{:S(2)}) collective-permute-start(bf16[256,1024]{1,0:T(8,128)(2,1)} %constant_dynamic-update-slice_fusion.refs_0_), channel_id=1, source_target_pairs={{0,2},{1,3},{2,4},{3,5},{4,6},{5,7},{6,0},{7,1},{8,10},{9,11},{10,... | collective-permute-start | bytes 1572872 | tf_op jit(solution)/shard_map/ppermute | solution.py:489
  182.1 9.6 %collective-permute-start.15 = (bf16[64,1024]{1,0:T(8,128)(2,1)S(1)}, bf16[64,1024]{1,0:T(8,128)(2,1)S(1)}, u32[]{:S(2)}, u32[]{:S(2)}) collective-permute-start(bf16[64,1024]{1,0:T(8,128)(2,1)S(1)} %slice.26), channel_id=1, source_target_pairs={{0,2},{1,3},{2,4},{3,5},{4,6},{5,7},{6,0},{7,1},{8,10},{9,11},{10,... | collective-permute-start | bytes 393224 | tf_op jit(solution)/shard_map/ppermute | solution.py:489
  183.6 11.0 %collective-permute-start.8 = (bf16[128,1024]{1,0:T(8,128)(2,1)S(1)}, bf16[128,1024]{1,0:T(8,128)(2,1)S(1)}, u32[]{:S(2)}, u32[]{:S(2)}) collective-permute-start(bf16[128,1024]{1,0:T(8,128)(2,1)S(1)} %collective-permute-done.3.refs_1_), channel_id=1, source_target_pairs={{0,1},{1,0},{2,3},{3,2},{4,5},{5,4},{6,7},{7,6},{8,9},{9,8},{10,11... | collective-permute-start | bytes 786440 | tf_op jit(solution)/shard_map/ppermute | solution.py:489
  194.6 19.1 %collective-permute-start.27 = (bf16[256,1024]{1,0:T(8,128)(2,1)}, bf16[256,1024]{1,0:T(8,128)(2,1)}, u32[]{:S(2)}, u32[]{:S(2)}) collective-permute-start(bf16[256,1024]{1,0:T(8,128)(2,1)} %constant_dynamic-update-slice_fusion.refs_0_), channel_id=1, source_target_pairs={{0,1},{1,0},{2,3},{3,2},{4,5},{5,4},{6,7},{7,6},{8,9},{9,8},{10,11... | collective-permute-start | bytes 1572872 | tf_op jit(solution)/shard_map/ppermute | solution.py:489
  195.4 17.8 %collective-permute-start.26 = (bf16[128,1024]{1,0:T(8,128)(2,1)S(1)}, bf16[128,1024]{1,0:T(8,128)(2,1)S(1)}, u32[]{:S(2)}, u32[]{:S(2)}) collective-permute-start(bf16[128,1024]{1,0:T(8,128)(2,1)S(1)} %slice.29), channel_id=1, source_target_pairs={{0,6},{1,7},{2,0},{3,1},{4,2},{5,3},{6,4},{7,5},{8,14},{9,15},{10,... | collective-permute-start | bytes 786440 | tf_op jit(solution)/shard_map/ppermute | solution.py:489
  195.4 17.9 %collective-permute-start.25 = (bf16[128,1024]{1,0:T(8,128)(2,1)S(1)}, bf16[128,1024]{1,0:T(8,128)(2,1)}, u32[]{:S(2)}, u32[]{:S(2)}) collective-permute-start(bf16[128,1024]{1,0:T(8,128)(2,1)S(1)} %slice.28), channel_id=1, source_target_pairs={{0,2},{1,3},{2,4},{3,5},{4,6},{5,7},{6,0},{7,1},{8,10},{9,11},{10,... | collective-permute-start | bytes 786440 | tf_op jit(solution)/shard_map/ppermute | solution.py:489
  196.8 17.9 %collective-permute-start.29 = (bf16[256,1024]{1,0:T(8,128)(2,1)S(1)}, bf16[256,1024]{1,0:T(8,128)(2,1)}, u32[]{:S(2)}, u32[]{:S(2)}) collective-permute-start(bf16[256,1024]{1,0:T(8,128)(2,1)S(1)} %collective-permute-done.24.refs_2_), channel_id=1, source_target_pairs={{0,1},{1,0},{2,3},{3,2},{4,5},{5,4},{6,7},{7,6},{8,9},{9,8},{10,11... | collective-permute-start | bytes 1572872 | tf_op jit(solution)/shard_map/ppermute | solution.py:489
  198.5 16.6 %collective-permute-start.28 = (bf16[256,1024]{1,0:T(8,128)(2,1)S(1)}, bf16[256,1024]{1,0:T(8,128)(2,1)}, u32[]{:S(2)}, u32[]{:S(2)}) collective-permute-start(bf16[256,1024]{1,0:T(8,128)(2,1)S(1)} %collective-permute-done.23.refs_1_), channel_id=1, source_target_pairs={{0,1},{1,0},{2,3},{3,2},{4,5},{5,4},{6,7},{7,6},{8,9},{9,8},{10,11... | collective-permute-start | bytes 1572872 | tf_op jit(solution)/shard_map/ppermute | solution.py:489
  209.5 51.3 %all-to-all-start.2 = ((bf16[8,768,128]{2,1,0:T(8,128)(2,1)}), bf16[8,768,128]{2,1,0:T(8,128)(2,1)S(1)}, u32[]{:S(2)}, u32[]{:S(2)}) async-start(bf16[8,768,128]{2,1,0:T(8,128)(2,1)} %get-tuple-element.40), calls=%async_computation.2 | async-start | bytes 3145728 | tf_op jit(solution)/shard_map/all_to_all | solution.py:421
  226.0 14.0 %collective-permute-start.32 = (bf16[768,128]{1,0:T(8,128)(2,1)}, bf16[768,128]{1,0:T(8,128)(2,1)S(1)}, u32[]{:S(2)}, u32[]{:S(2)}) collective-permute-start(bf16[768,128]{1,0:T(8,128)(2,1)} %get-tuple-element.42), channel_id=1, source_target_pairs={{0,80},{1,81},{2,82},{3,83},{4,84},{5,85},{6,86},{7,87},{8,88},{9,... | collective-permute-start | bytes 589832 | tf_op jit(solution)/shard_map/ppermute | solution.py:495
  230.0 18.5 %collective-permute-start.33 = (bf16[768,128]{1,0:T(8,128)(2,1)}, bf16[768,128]{1,0:T(8,128)(2,1)S(1)}, u32[]{:S(2)}, u32[]{:S(2)}) collective-permute-start(bf16[768,128]{1,0:T(8,128)(2,1)} %get-tuple-element.43), channel_id=1, source_target_pairs={{0,64},{1,65},{2,66},{3,67},{4,68},{5,69},{6,70},{7,71},{8,72},{9,... | collective-permute-start | bytes 589832 | tf_op jit(solution)/shard_map/ppermute | solution.py:495
  230.2 30.5 %collective-permute-start.34 = (bf16[768,128]{1,0:T(8,128)(2,1)}, bf16[768,128]{1,0:T(8,128)(2,1)S(1)}, u32[]{:S(2)}, u32[]{:S(2)}) collective-permute-start(bf16[768,128]{1,0:T(8,128)(2,1)} %get-tuple-element.44), channel_id=1, source_target_pairs={{0,48},{1,49},{2,50},{3,51},{4,52},{5,53},{6,54},{7,55},{8,56},{9,... | collective-permute-start | bytes 589832 | tf_op jit(solution)/shard_map/ppermute | solution.py:495
  231.4 29.3 %collective-permute-start.35 = (bf16[768,128]{1,0:T(8,128)(2,1)}, bf16[768,128]{1,0:T(8,128)(2,1)S(1)}, u32[]{:S(2)}, u32[]{:S(2)}) collective-permute-start(bf16[768,128]{1,0:T(8,128)(2,1)} %get-tuple-element.45), channel_id=1, source_target_pairs={{0,112},{1,113},{2,114},{3,115},{4,116},{5,117},{6,118},{7,119},{8... | collective-permute-start | bytes 589832 | tf_op jit(solution)/shard_map/ppermute | solution.py:495
  233.8 27.0 %collective-permute-start.36 = (bf16[768,128]{1,0:T(8,128)(2,1)}, bf16[768,128]{1,0:T(8,128)(2,1)S(1)}, u32[]{:S(2)}, u32[]{:S(2)}) collective-permute-start(bf16[768,128]{1,0:T(8,128)(2,1)} %get-tuple-element.46), channel_id=1, source_target_pairs={{0,32},{1,33},{2,34},{3,35},{4,36},{5,37},{6,38},{7,39},{8,40},{9,... | collective-permute-start | bytes 589832 | tf_op jit(solution)/shard_map/ppermute | solution.py:495
  240.0 20.8 %collective-permute-start.37 = (bf16[768,128]{1,0:T(8,128)(2,1)}, bf16[768,128]{1,0:T(8,128)(2,1)S(1)}, u32[]{:S(2)}, u32[]{:S(2)}) collective-permute-start(bf16[768,128]{1,0:T(8,128)(2,1)} %get-tuple-element.47), channel_id=1, source_target_pairs={{0,96},{1,97},{2,98},{3,99},{4,100},{5,101},{6,102},{7,103},{8,104... | collective-permute-start | bytes 589832 | tf_op jit(solution)/shard_map/ppermute | solution.py:495
  248.5 12.3 %collective-permute-start.38 = (bf16[768,128]{1,0:T(8,128)(2,1)}, bf16[768,128]{1,0:T(8,128)(2,1)S(1)}, u32[]{:S(2)}, u32[]{:S(2)}) collective-permute-start(bf16[768,128]{1,0:T(8,128)(2,1)} %get-tuple-element.48), channel_id=1, source_target_pairs={{0,16},{1,17},{2,18},{3,19},{4,20},{5,21},{6,22},{7,23},{8,24},{9,... | collective-permute-start | bytes 589832 | tf_op jit(solution)/shard_map/ppermute | solution.py:495
  (50 other events, 514.2 us)
